TPU v7x, 32 devices: a whole 2x2x4 slice. The times are simulated.
32 devices in a mesh: group: 2 (over y), blk: 4 (over z), gz: 2 (over x), view: 2 (over core).
Axes of the slice: x: 2, y: 2, z: 4, core: 2. Of those that a mesh axis runs over, the one named last changes fastest.
Arguments:
- estimate: float32 [32, 128, 128], P(('group', 'gz'), 'blk'), parts along dimension 0, may hold values from 0.5 to 2
- view_tiles: bfloat16 [192, 14, 14, 128], P(('group', 'blk', 'gz', 'view')), parts along dimension 0, may hold values from 0.25 to 4
- tile_pairs: int32 [192, 2], P('group'), parts along dimension 0, may hold values from 0 to 31, as said below
- kernel_table: bfloat16 [6, 16, 7, 7, 7], P('view', ('group', 'blk', 'gz')), parts along dimension 1, may hold values from 0.0014953613 to 0.0059814453
- kernel_ids: int32 [64, 6], P('group'), parts along dimension 0, may hold values from 0 to 7
Outputs:
- estimate_out: float32 [32, 128, 128], P(('group', 'gz'), 'blk'), parts along dimension 0
There are 2 independent parts, one for each index of `group`. A program takes and returns all parts, laid end to end along the dimension named above; each array names one. Nothing has to cross between parts.
Inputs may be any that keep to these rules, and one draw needn't show every extreme that they name: Tile t is stored on the device at position t // 6 in the order blk, gz, view. Its block b = tile_pairs[t, 0] lies in that device's sub-slab (b // 16 is its gz index) and its view tile_pairs[t, 1] in that device's half (view // 3 is its view index). No block has two tiles of one view; every block has at least one tile of each half of the views. The tiles of one device go to at most 3 tiles' worth of blocks with the same (b % 16) // 4, and some device reaches 3; the blocks of one sub-slab with the same (b % 16) // 4 have at most 12 tiles of one half of the views, and some reach it.
All inputs are finite; a program needn't handle non-finite values.
Results may differ from a plain program's by a relative error of at most 0.0003.
Values may be sent and summed in bfloat16 or wider, within the bound.
No kernel may reach another device: no remote copies, remote signals or barrier semaphores. Data moves between devices by JAX's collectives and lax.ppermute only.
A program may use at most 64 MiB of HBM per device.

v0:
```python
import jax
import jax.numpy as jnp
from jax import lax
from jax.sharding import PartitionSpec as P

ITERS = 2


def extended_2(array, sides, width):
    for axis, dim in sides:
        peers, length = (lax.axis_size(axis), array.shape[dim])
        up = [(i, (i + 1) % peers) for i in range(peers - 1)]
        down = [(j, i) for i, j in up]
        last = lax.slice_in_dim(array, length - width, length, axis=dim)
        leading = lax.slice_in_dim(array, 0, width, axis=dim)
        before = lax.ppermute(last, axis, up)
        after = lax.ppermute(leading, axis, down)
        array = jnp.concatenate([before, array, after], axis=dim)
    return array


def toeplitz_pair(kernel, cells_x):
    kernel_size = kernel.shape[0]
    kernel_reach = (kernel_size - 1) // 2
    row_index = jnp.arange(cells_x, dtype=jnp.int32)[:, None]
    column_index = jnp.arange(cells_x, dtype=jnp.int32)[None, :]
    tap_index = jnp.arange(kernel_size, dtype=jnp.int32)[:, None, None]
    forward_mask = ((row_index - column_index + kernel_reach)[None] == tap_index).astype(
        jnp.bfloat16
    )
    backward_mask = ((column_index - row_index + kernel_reach)[None] == tap_index).astype(
        jnp.bfloat16
    )
    forward = jnp.einsum(
        "abc,cji->abji", kernel, forward_mask, preferred_element_type=jnp.float32
    ).astype(jnp.bfloat16)
    backward = jnp.einsum(
        "abc,cji->abji", kernel, backward_mask, preferred_element_type=jnp.float32
    ).astype(jnp.bfloat16)
    return (
        forward.reshape(kernel_size, kernel_size * cells_x, cells_x),
        backward.reshape(kernel_size, kernel_size * cells_x, cells_x),
    )


def blurring(extended, forward, extent_z, extent_y):
    kernel_size = forward.shape[0]
    cells_x = extended.shape[2]
    shifted = jnp.stack(
        [extended[:, shift_y : shift_y + extent_y, :] for shift_y in range(kernel_size)], axis=2
    )
    shifted = shifted.reshape(extended.shape[0], extent_y, kernel_size * cells_x)
    accumulated = jnp.zeros((extent_z * extent_y, cells_x), jnp.float32)
    for plane_z in range(kernel_size):
        matrix_rows = shifted[plane_z : plane_z + extent_z].reshape(
            extent_z * extent_y, kernel_size * cells_x
        )
        accumulated = accumulated + jnp.dot(
            matrix_rows, forward[plane_z], preferred_element_type=jnp.float32
        )
    return accumulated.reshape(extent_z, extent_y, cells_x)


def spread(ratio, backward, extent_z, extent_y):
    kernel_size = backward.shape[0]
    kernel_reach = (kernel_size - 1) // 2
    cells_x = ratio.shape[2]
    shifted = jnp.stack(
        [
            ratio[:, 2 * kernel_reach - shift_y : 2 * kernel_reach - shift_y + extent_y, :]
            for shift_y in range(kernel_size)
        ],
        axis=2,
    )
    shifted = shifted.reshape(ratio.shape[0], extent_y, kernel_size * cells_x)
    accumulated = jnp.zeros((extent_z * extent_y, cells_x), jnp.float32)
    for plane_z in range(kernel_size):
        begin_z = 2 * kernel_reach - plane_z
        matrix_rows = shifted[begin_z : begin_z + extent_z].reshape(
            extent_z * extent_y, kernel_size * cells_x
        )
        accumulated = accumulated + jnp.dot(
            matrix_rows, backward[plane_z], preferred_element_type=jnp.float32
        )
    return accumulated.reshape(extent_z, extent_y, cells_x)


def tile_correction(one_tile, extended, kernel, first_z, first_y, volume_z, volume_y):
    extent_z, extent_y, cells_x = one_tile.shape
    kernel_reach = (kernel.shape[0] - 1) // 2
    forward, backward = toeplitz_pair(kernel, cells_x)
    blurred = blurring(extended, forward, extent_z, extent_y)
    cell_z = first_z + jnp.arange(extent_z, dtype=jnp.int32) - kernel_reach
    cell_y = first_y + jnp.arange(extent_y, dtype=jnp.int32) - kernel_reach
    inside = ((cell_z >= 0) & (cell_z < volume_z))[:, None, None] & (
        (cell_y >= 0) & (cell_y < volume_y)
    )[None, :, None]
    ratio = jnp.where(inside, one_tile.astype(jnp.float32) / blurred, 0.0).astype(jnp.bfloat16)
    return spread(ratio, backward, extent_z - 2 * kernel_reach, extent_y - 2 * kernel_reach)


def on_device(estimate, view_tiles, tile_pairs, kernel_table, kernel_ids):
    cells_z, local_y, cells_x = estimate.shape
    tile_count = view_tiles.shape[0]
    extent_y = view_tiles.shape[2]
    views_here = kernel_table.shape[0]
    kernel_reach = (kernel_table.shape[2] - 1) // 2
    block_cells = extent_y - 2 * kernel_reach
    blocks_here = local_y // block_cells
    block_devices = lax.axis_size("blk")
    slab_devices = lax.axis_size("gz")
    core_devices = lax.axis_size("view")
    block_rank = lax.axis_index("blk")
    slab_rank = lax.axis_index("gz")
    core_rank = lax.axis_index("view")
    volume_z = cells_z * slab_devices
    volume_y = local_y * block_devices
    blocks_row = blocks_here * block_devices
    slot_count = (views_here * blocks_here + block_devices - 1) // block_devices
    home_most = views_here * blocks_here
    device_total = block_devices * slab_devices * core_devices
    tile_total = tile_pairs.shape[0]
    kernels = lax.all_gather(kernel_table, ("blk", "gz"), axis=1, tiled=True)
    tile_block = tile_pairs[:, 0]
    tile_view = tile_pairs[:, 1]
    tile_ids = jnp.arange(tile_total, dtype=jnp.int32)
    block_row = tile_block % blocks_row
    home_group = block_row // blocks_here
    home_slab = tile_block // blocks_row
    in_block = block_row % blocks_here
    stored_group = tile_ids // tile_count // (slab_devices * core_devices)
    grouped = home_group.reshape(device_total, tile_count)
    earlier = jnp.arange(tile_count)[:, None] > jnp.arange(tile_count)[None, :]
    slot_rank = jnp.sum(
        ((grouped[:, :, None] == grouped[:, None, :]) & earlier[None]).astype(jnp.int32), axis=2
    ).reshape(-1)
    is_mine = (
        (home_slab == slab_rank)
        & (home_group == block_rank)
        & (tile_view // views_here == core_rank)
    )
    listed = jnp.argsort(jnp.where(is_mine, tile_ids, tile_ids + tile_total))[:home_most]
    live_count = jnp.sum(is_mine.astype(jnp.int32))
    list_source = stored_group[listed]
    list_rank = slot_rank[listed]
    list_block = tile_block[listed]
    list_view = tile_view[listed]
    list_local = in_block[listed]
    first_block = slab_rank * blocks_row + block_rank * blocks_here
    coverage = jnp.sum(
        (tile_block[None, :] == first_block + jnp.arange(blocks_here)[:, None]).astype(jnp.float32),
        axis=1,
    )
    count_field = jnp.repeat(coverage, block_cells)[None, :, None]
    own_ids = (
        block_rank * slab_devices * core_devices + slab_rank * core_devices + core_rank
    ) * tile_count + jnp.arange(tile_count, dtype=jnp.int32)

    def correction_for(one_tile, extended, block_id, view_id):
        kernel = kernels[view_id - core_rank * views_here, kernel_ids[block_id, view_id]]
        first_z = block_id // blocks_row * cells_z
        first_y = block_id % blocks_row * block_cells
        return tile_correction(one_tile, extended, kernel, first_z, first_y, volume_z, volume_y)

    outgoing = jnp.zeros((block_devices, slot_count) + view_tiles.shape[1:], view_tiles.dtype)
    outgoing = outgoing.at[home_group[own_ids], slot_rank[own_ids]].set(view_tiles)
    arrived = lax.all_to_all(outgoing, "blk", split_axis=0, concat_axis=0, tiled=True)
    arrived = arrived.reshape((block_devices * slot_count,) + view_tiles.shape[1:])
    current = estimate
    for iteration in range(ITERS):
        padded = extended_2(current.astype(jnp.bfloat16), (("blk", 1), ("gz", 0)), 2 * kernel_reach)

        def visit_tile(position, summed):
            block_local = list_local[position]
            one_tile = lax.dynamic_index_in_dim(
                arrived, list_source[position] * slot_count + list_rank[position], 0, keepdims=False
            )
            extended = lax.dynamic_slice_in_dim(
                padded, block_local * block_cells, block_cells + 4 * kernel_reach, 1
            )
            correction = correction_for(
                one_tile, extended, list_block[position], list_view[position]
            )
            offset = block_local * block_cells
            window = lax.dynamic_slice_in_dim(summed, offset, block_cells, 1)
            return lax.dynamic_update_slice_in_dim(summed, window + correction, offset, 1)

        summed = lax.fori_loop(0, live_count, visit_tile, jnp.zeros(estimate.shape, jnp.float32))
        combined = lax.psum(summed, "view")
        current = current * combined / count_field
    return current


def solution(mesh):
    in_specs = (
        P(("group", "gz"), "blk", None),
        P(("group", "blk", "gz", "view"), None, None, None),
        P("group", None),
        P("view", ("group", "blk", "gz"), None, None, None),
        P("group", None),
    )
    out_specs = P(("group", "gz"), "blk", None)
    return jax.shard_map(
        on_device, mesh=mesh, in_specs=in_specs, out_specs=out_specs, check_vma=False
    )
```

profile of v0, /device:TPU:11, one launch (start us, length us, event | category | flops | bytes accessed | tf_op | source)
XLA Modules:
  0.0 750.7 jit_solution(275208694247272833)
XLA Ops:
  6.5 0.8 slice_bitcast_fusion.42
  7.3 0.8 add_select_fusion.2
  9.9 1.0 broadcast_in_dim.74
  10.9 2.4 scatter_fusion
  13.2 4.8 all-to-all-start
  18.0 3.1 collective-permute-start
  21.1 2.2 collective-permute-start.1
  23.3 0.7 and_select_fusion.2
  24.0 2.5 sort.17
  27.2 0.7 gather_fusion
  27.9 0.7 gather_fusion.1
  28.6 0.7 gather_fusion.6
  29.2 3.1 collective-permute-done
  32.4 2.0 collective-permute-done.1
  34.5 1.3 collective-permute-start.2
  35.8 4.0 collective-permute-start.3
  40.5 20.6 %all_gather.3 = bf16[3,8,7,7,7]{4,3,2,1,0:T(8,128)(2,1)} all-gather(bf16[3,1,7,7,7]{4,3,2,1,0:T(8,128)(2,1)S(1)} %copy-done.4), channel_id=1, replica_groups=mesh['group'=2,'blk'=4,'gz'=2,'view'=2] {'blk','gz'}, dimensions={1}, use_global_device_ids=true | all-gather | bytes 18522 | tf_op jit(solution)/shard_map/all_gather | solution.py:123
  61.2 103.9 %while.26 = (s32[]{:T(128)}, f32[8,32,128]{2,1,0:T(8,128)S(1)}, s32[]{:T(128)}, s32[12]{0:T(128)S(1)}, s32[12]{0:T(128)S(1)}, /*index=5*/s32[12]{0:T(128)S(1)}, ...) while((s32[]{:T(128)}, f32[8,32,128]{2,1,0:T(8,128)S(1)}, ...), condition=%wide.region_5.6_spmd, body=%wide.region_4.5_spmd.sunk | while | flops 442152288 | bytes 46343604 | solution.py:188
  69.0 1.3 dynamic_slice.188
  72.7 1.3 convolution_convert_fusion.9
  82.8 0.9 fusion.225
  83.9 1.3 convolution_convert_fusion.8
  94.8 1.3 dynamic_slice.188
  98.5 1.3 convolution_convert_fusion.9
  108.6 0.9 fusion.225
  109.7 1.3 convolution_convert_fusion.8
  120.6 1.3 dynamic_slice.188
  124.3 1.3 convolution_convert_fusion.9
  134.4 0.9 fusion.225
  135.5 1.3 convolution_convert_fusion.8
  146.4 1.3 dynamic_slice.188
  150.1 1.3 convolution_convert_fusion.9
  160.2 0.9 fusion.225
  161.3 1.3 convolution_convert_fusion.8
  166.2 233.5 %all-reduce.3.cloned.1.call-done = f32[8,32,128]{2,1,0:T(8,128)} async-done(((f32[8,32,128]{2,1,0:T(8,128)}), f32[8,32,128]{2,1,0:T(8,128)}) %all-reduce.3.cloned.1.call-update) | async-done | bytes 131088 | tf_op jit(solution)/shard_map/psum | solution.py:189
  399.7 1.0 fusion.56
  400.7 3.1 collective-permute-start.4
  403.8 2.2 collective-permute-start.5
  406.0 2.3 collective-permute-done.5
  408.4 1.3 collective-permute-start.6
  409.7 4.0 collective-permute-start.7
  413.7 1.4 collective-permute-done.7
  415.1 102.3 %while.27 = (s32[]{:T(128)}, f32[8,32,128]{2,1,0:T(8,128)S(1)}, s32[]{:T(128)}, s32[12]{0:T(128)S(1)}, s32[12]{0:T(128)S(1)}, /*index=5*/s32[12]{0:T(128)S(1)}, ...) while((s32[]{:T(128)}, f32[8,32,128]{2,1,0:T(8,128)S(1)}, ...), condition=%wide.region_9.10_spmd, body=%wide.region_8.9_spmd.sunk | while | flops 442152288 | bytes 46343604 | solution.py:188
  416.0 0.7 dynamic_slice.195
  422.9 1.4 dynamic_slice.198
  426.9 1.3 convolution_convert_fusion.11
  436.5 0.9 fusion.264
  437.6 1.3 convolution_convert_fusion.10
  441.4 0.7 dynamic_slice.195
  448.3 1.4 dynamic_slice.198
  452.3 1.3 convolution_convert_fusion.11
  461.8 0.9 fusion.264
  463.0 1.3 convolution_convert_fusion.10
  466.7 0.7 dynamic_slice.195
  473.6 1.4 dynamic_slice.198
  477.6 1.3 convolution_convert_fusion.11
  487.2 0.9 fusion.264
  488.3 1.3 convolution_convert_fusion.10
  499.0 1.4 dynamic_slice.198
  503.0 1.3 convolution_convert_fusion.11
  512.6 0.9 fusion.264
  513.7 1.3 convolution_convert_fusion.10
  518.2 224.0 %all-reduce.5.cloned.1.call-done = f32[8,32,128]{2,1,0:T(8,128)} async-done(((f32[8,32,128]{2,1,0:T(8,128)}), f32[8,32,128]{2,1,0:T(8,128)}) %all-reduce.5.cloned.1.call-update) | async-done | bytes 131088 | tf_op jit(solution)/shard_map/psum | solution.py:189
  742.1 1.7 multiply_divide_fusion
  (657 shorter events, 81.8 us)
Async XLA Ops:
  6.5 4.3 copy-start.3
  9.2 8.8 %copy-start.2 = (f32[8,32,128]{2,1,0:T(8,128)S(1)}, f32[8,32,128]{2,1,0:T(8,128)}, u32[]{:S(2)}) copy-start(f32[8,32,128]{2,1,0:T(8,128)} %param.9) | copy-start | bytes 393220
  13.2 47.9 %all-to-all-start = ((bf16[4,3,14,14,128]{4,3,2,1,0:T(8,128)(2,1)}), bf16[4,3,14,14,128]{4,3,2,1,0:T(8,128)(2,1)}, u32[]{:S(2)}, u32[]{:S(2)}) async-start(bf16[4,3,14,14,128]{4,3,2,1,0:T(8,128)(2,1)} %scatter_fusion), calls=%async_computation | async-start | bytes 1376256 | tf_op jit(solution)/shard_map/all_to_all | solution.py:167
  18.0 22.5 %copy-start.4 = (bf16[3,1,7,7,7]{4,3,2,1,0:T(8,128)(2,1)S(1)}, bf16[3,1,7,7,7]{4,3,2,1,0:T(8,128)(2,1)}, u32[]{:S(2)}) copy-start(bf16[3,1,7,7,7]{4,3,2,1,0:T(8,128)(2,1)} %param.12) | copy-start | bytes 6178
  18.0 381.7 %all-reduce.3.cloned.1.call-start = ((), (), s32[]{:S(2)}) async-start(), calls=%async_computation.1 | async-start | bytes 262144 | tf_op jit(solution)/shard_map/psum | solution.py:189
  18.0 14.3 %collective-permute-start = (bf16[8,6,128]{2,1,0:T(8,128)(2,1)S(1)}, bf16[8,6,128]{2,1,0:T(8,128)(2,1)S(1)}, u32[]{:S(2)}, u32[]{:S(2)}) collective-permute-start(bf16[8,6,128]{2,1,0:T(8,128)(2,1)S(1)} %get-tuple-element.543), channel_id=1, source_target_pairs={{0,4},{4,8},{8,12},{1,5},{5,9},{9,13},{2,6},{6,10},{10,14},{3,7},{... | collective-permute-start | bytes 36872 | tf_op jit(solution)/shard_map/ppermute | solution.py:16
  21.1 13.3 %collective-permute-start.1 = (bf16[8,6,128]{2,1,0:T(8,128)(2,1)S(1)}, bf16[8,6,128]{2,1,0:T(8,128)(2,1)S(1)}, u32[]{:S(2)}, u32[]{:S(2)}) collective-permute-start(bf16[8,6,128]{2,1,0:T(8,128)(2,1)S(1)} %get-tuple-element.544), channel_id=1, source_target_pairs={{4,0},{8,4},{12,8},{5,1},{9,5},{13,9},{6,2},{10,6},{14,10},{7,3},{... | collective-permute-start | bytes 36872 | tf_op jit(solution)/shard_map/ppermute | solution.py:17
  34.5 26.6 %collective-permute-start.2 = (bf16[6,44,128]{2,1,0:T(8,128)(2,1)S(1)}, bf16[6,44,128]{2,1,0:T(8,128)(2,1)S(1)}, u32[]{:S(2)}, u32[]{:S(2)}) collective-permute-start(bf16[6,44,128]{2,1,0:T(8,128)(2,1)S(1)} %get-tuple-element.539), channel_id=1, source_target_pairs={{0,2},{1,3},{4,6},{5,7},{8,10},{9,11},{12,14},{13,15},{16,18},{17,... | collective-permute-start | bytes 202760 | tf_op jit(solution)/shard_map/ppermute | solution.py:16
  35.8 25.3 %collective-permute-start.3 = (bf16[6,44,128]{2,1,0:T(8,128)(2,1)S(1)}, bf16[6,44,128]{2,1,0:T(8,128)(2,1)S(1)}, u32[]{:S(2)}, u32[]{:S(2)}) collective-permute-start(bf16[6,44,128]{2,1,0:T(8,128)(2,1)S(1)} %get-tuple-element.540), channel_id=1, source_target_pairs={{2,0},{3,1},{6,4},{7,5},{10,8},{11,9},{14,12},{15,13},{18,16},{19,... | collective-permute-start | bytes 202760 | tf_op jit(solution)/shard_map/ppermute | solution.py:17
  165.1 0.7 copy-start.1
  165.8 576.4 %all-reduce.5.cloned.1.call-start = ((), (), s32[]{:S(2)}) async-start(), calls=%async_computation.2 | async-start | bytes 262144 | tf_op jit(solution)/shard_map/psum | solution.py:189
  400.7 5.3 collective-permute-start.4
  403.8 4.5 collective-permute-start.5
  408.4 5.3 collective-permute-start.6
  409.7 5.4 collective-permute-start.7
  517.5 0.7 copy-start
Sparse Core Ops, SparseCore 0:
  165.9 233.7 all-reduce.2
  518.3 223.8 all-reduce.4
where the time goes:
time: 761 us; the launch traced here: 751 us
  waiting for transfers between devices  466 us (61%)
  loops' own time  88.1 us (12%)
  local copies, waits for them, and re-layouts  74.3 us (10%)
  matrix products  46.2 us (6%)
  starting transfers between devices  25.9 us (3%)
  blocking collectives  20.6 us (3%)
  other arithmetic  15.5 us (2%)
  between operations  13.7 us (2%)
    psum x2, waiting for transfers between devices, on_device(): combined = lax.psum(summed, 'view')  458 us
    another operation x2, loops' own time, on_device(): lax.fori_loop(0, live_count, visit_tile, jnp.zeros(estimate.shape, jnp.fl...  88.1 us
    all_gather x1, blocking collectives, on_device(): kernels = lax.all_gather(kernel_table, ('blk', 'gz'), axis=1, tiled=True)  20.6 us
  transfers between devices with their start and end apart: 11, of which 6 were waited for; matrix products, arithmetic and copies ran while one was open for 1% of the time, Pallas kernels for 0%

commit v1 on v0

v1 whole, which is shorter than its diff:
```python
import functools

import jax
import jax.numpy as jnp
from jax import lax
from jax.experimental import pallas as pl
from jax.experimental.pallas import tpu as pltpu
from jax.sharding import PartitionSpec as P

ITERS = 2
F32, BF16 = jnp.float32, jnp.bfloat16
VM = pl.BlockSpec(memory_space=pltpu.VMEM)
SM = pl.BlockSpec(memory_space=pltpu.SMEM)


def up8(n):
    return (n + 7) // 8 * 8


class Plan:
    def __init__(self, estimate, view_tiles, tile_pairs, kernel_table, kernel_ids):
        self.cz, self.ly, self.nx = estimate.shape
        self.tiles, self.ez, self.ey, _ = view_tiles.shape
        self.views_here, self.sets_here, self.taps = kernel_table.shape[:3]
        self.reach = (self.taps - 1) // 2
        self.by = self.ey - 2 * self.reach
        self.blocks = self.ly // self.by
        self.n_blk = lax.axis_size("blk")
        self.n_gz = lax.axis_size("gz")
        self.n_view = lax.axis_size("view")
        self.views = self.views_here * self.n_view
        self.row_blocks = self.blocks * self.n_blk
        self.total = tile_pairs.shape[0]
        self.slots = -(-self.views_here * self.blocks // self.n_blk)
        self.slots = min(self.slots, self.tiles)
        self.fast = self.n_blk == 4 and self.n_gz == 2 and self.sets_here == 1
        self.n_sets = self.n_blk * self.n_gz * self.sets_here
        self.halo = 2 * self.reach
        assert self.by == 8 and self.cz == 8 and self.nx == 128 and self.taps == 7
        assert self.n_blk % 2 == 0 and self.blocks % 2 == 0 and self.ez <= 16
        self.zz = self.cz + 2 * self.halo
        self.rows = self.ly + 16
        self.windows = self.blocks // 2


def ranks():
    return lax.axis_index("blk"), lax.axis_index("gz"), lax.axis_index("view")


def lane_shift(plane, e, reach, lane):
    d = e - reach
    if d == 0:
        return plane
    n = plane.shape[-1]
    rolled = pltpu.roll(plane, (-d) % n, 1)
    ok = (lane < n - d) if d > 0 else (lane >= -d)
    return jnp.where(ok, rolled, 0.0)


def pack_kernel(p, pairs_ref, tiles_ref, *outs):
    b, g, v = ranks()
    first = ((b * p.n_gz + g) * p.n_view + v) * p.tiles
    homes = [(pairs_ref[2 * (first + j)] % p.row_blocks) // p.blocks for j in range(p.tiles)]
    for j in range(p.tiles):
        rank = sum([(homes[i] == homes[j]).astype(jnp.int32) for i in range(j)], jnp.int32(0))
        k = lax.rem(homes[j] - b + p.n_blk, p.n_blk)
        for kk in range(p.n_blk):

            @pl.when(k == kk)
            def _():
                outs[kk][rank] = tiles_ref[j]


def pack(p, pairs, tiles):
    return pl.pallas_call(
        functools.partial(pack_kernel, p),
        out_shape=[jax.ShapeDtypeStruct((p.slots,) + tiles.shape[1:], tiles.dtype)] * p.n_blk,
        in_specs=[SM, VM],
        out_specs=[VM] * p.n_blk,
        name="pack",
    )(pairs, tiles)


def sends_of(p, b, g, x, own_ref, sa_ref, sb_ref):
    even = b % 2 == 0
    for z in range(p.cz):
        xb = x[z].astype(BF16)
        own_ref[z] = xb
        lo, hi = xb[:8], xb[p.ly - 8 :]
        lo, hi = x[z][:8], x[z][p.ly - 8 :]
        sa_ref[z] = jnp.where(even, hi, lo).astype(BF16)
        sb_ref[z] = jnp.where(even, lo, hi).astype(BF16)


def first_kernel(p, est_ref, own_ref, sa_ref, sb_ref):
    b, g, v = ranks()
    sends_of(p, b, g, [est_ref[z] for z in range(p.cz)], own_ref, sa_ref, sb_ref)


def update_kernel(p, count_ref, est_ref, mine_ref, other_ref, new_ref, own_ref=None, sa_ref=None, sb_ref=None):
    b, g, v = ranks()
    x = []
    for z in range(p.cz):
        rows = []
        for k in range(p.blocks):
            at = slice(k * 8, k * 8 + 8)
            total = mine_ref[z, at, :] + other_ref[z, at, :]
            rows.append(est_ref[z, at, :] * total / count_ref[k])
        x.append(jnp.concatenate(rows, axis=0))
        new_ref[z] = x[z]
    if own_ref is not None:
        sends_of(p, b, g, x, own_ref, sa_ref, sb_ref)


def sends_shape(p):
    return [
        jax.ShapeDtypeStruct((p.cz, p.ly, p.nx), BF16),
        jax.ShapeDtypeStruct((p.cz, 8, p.nx), BF16),
        jax.ShapeDtypeStruct((p.cz, 8, p.nx), BF16),
    ]


def first_sends(p, est):
    return pl.pallas_call(
        functools.partial(first_kernel, p), out_shape=sends_shape(p), in_specs=[VM],
        out_specs=[VM] * 3, name="first",
    )(est)


def update(p, count, est, mine, other, last):
    shapes = [jax.ShapeDtypeStruct(est.shape, F32)] + ([] if last else sends_shape(p))
    return pl.pallas_call(
        functools.partial(update_kernel, p), out_shape=shapes, in_specs=[SM, VM, VM, VM],
        out_specs=[VM] * len(shapes), name="update",
    )(count, est, mine, other)


def edges_kernel(p, own_ref, ra_ref, rb_ref, lo_ref, hi_ref=None):
    b, g, v = ranks()
    even = b % 2 == 0
    has_lo, has_hi = b > 0, b < p.n_blk - 1

    def planes(out_ref, start):
        for i in range(p.halo):
            ra, rb = ra_ref[start + i].astype(F32), rb_ref[start + i].astype(F32)
            left = jnp.where(has_lo, jnp.where(even, rb, ra), 0.0)
            right = jnp.where(has_hi, jnp.where(even, ra, rb), 0.0)
            out_ref[i, :8] = left.astype(BF16)
            out_ref[i, 8 : 8 + p.ly] = own_ref[start + i]
            out_ref[i, 8 + p.ly :] = right.astype(BF16)

    if hi_ref is None:
        planes(lo_ref, jnp.where(g == 0, p.cz - p.halo, 0))
    else:
        planes(lo_ref, p.cz - p.halo)
        planes(hi_ref, 0)


def halos(p, own, sa, sb, kern=None):
    n = p.n_blk
    pair = [(i, i ^ 1) for i in range(n)]
    odd = [(i, (i + 1) % n if i % 2 else (i - 1) % n) for i in range(n)]
    nz = p.cz * 8
    if kern is not None and p.fast:
        kr = kern.shape[0]
        got = lax.ppermute(jnp.concatenate([sa.reshape(nz, p.nx), kern]), "blk", pair)
        ra, kern = got[:nz].reshape(sa.shape), jnp.concatenate([kern, got[nz:]])
        got = lax.ppermute(jnp.concatenate([sb.reshape(nz, p.nx), kern]), "blk", odd)
        rb, kern = got[:nz].reshape(sb.shape), jnp.concatenate([kern, got[nz:]])
    else:
        ra, rb = lax.ppermute(sa, "blk", pair), lax.ppermute(sb, "blk", odd)
    two = p.n_gz == 2
    edge = jax.ShapeDtypeStruct((p.halo, p.rows, p.nx), BF16)
    out = pl.pallas_call(
        functools.partial(edges_kernel, p), out_shape=[edge] if two else [edge, edge],
        in_specs=[VM] * 3, out_specs=[VM] * (1 if two else 2), name="edges",
    )(own, ra, rb)
    if two:
        swap = [(0, 1), (1, 0)]
        if kern is not None and p.fast:
            ne = p.halo * p.rows
            got = lax.ppermute(jnp.concatenate([out[0].reshape(ne, p.nx), kern]), "gz", swap)
            below = above = got[:ne].reshape(edge.shape)
            kern = jnp.concatenate([kern, got[ne:]])
        else:
            below = above = lax.ppermute(out[0], "gz", swap)
    else:
        ups = [(i, i + 1) for i in range(p.n_gz - 1)]
        below = lax.ppermute(out[0], "gz", ups)
        above = lax.ppermute(out[1], "gz", [(j, i) for i, j in ups])
    return (own, ra, rb, below, above), kern


def tiles_kernel(p, pairs_ref, ids_ref, own_ref, ra_ref, rb_ref, below_ref, above_ref, kern_ref, *rest):
    arrived = rest[: p.n_blk]
    out_ref, xs_ref, kf_ref, kb_ref, tile_ref, r_ref, r2_ref = rest[p.n_blk :]
    b, g, v = ranks()
    even = b % 2 == 0
    taps, reach, nx = p.taps, p.reach, p.nx
    lane8 = lax.broadcasted_iota(jnp.int32, (8, nx), 1)

    row = lax.broadcasted_iota(jnp.int32, (128, 256), 0)
    col = lax.broadcasted_iota(jnp.int32, (128, 256), 1)
    sel_f = ((row // taps == col % 32) & (row % taps == col // 32) & (row < taps * taps)).astype(BF16)
    row = lax.broadcasted_iota(jnp.int32, (128, 128), 0)
    col = lax.broadcasted_iota(jnp.int32, (128, 128), 1)
    sel_b = (
        (taps - 1 - row // taps == col % 16) & (taps - 1 - row % taps == col // 16) & (row < taps * taps)
    ).astype(BF16)
    kf_ref[...] = jnp.dot(kern_ref[...], sel_f, preferred_element_type=F32)
    kb_ref[...] = jnp.dot(kern_ref[...], sel_b, preferred_element_type=F32)

    depth = taps * 32
    xs_ref[:, depth:, :] = jnp.zeros((p.windows, xs_ref.shape[1] - depth, xs_ref.shape[2]), BF16)
    r2_ref[taps * 16 :, :] = jnp.zeros((r2_ref.shape[0] - taps * 16, r2_ref.shape[1]), BF16)
    r_ref[...] = jnp.zeros(r_ref.shape, F32)
    out_ref[...] = jnp.zeros(out_ref.shape, F32)
    has_left, has_right = b > 0, b < p.n_blk - 1
    has_below, has_above = g > 0, g < p.n_gz - 1
    lane = lax.broadcasted_iota(jnp.int32, (p.rows, nx), 1)
    for z in range(p.zz):
        if z < p.halo:
            plane = jnp.where(has_below, below_ref[z].astype(F32), 0.0)
        elif z >= p.halo + p.cz:
            plane = jnp.where(has_above, above_ref[z - p.halo - p.cz].astype(F32), 0.0)
        else:
            i = z - p.halo
            ra, rb = ra_ref[i].astype(F32), rb_ref[i].astype(F32)
            left = jnp.where(has_left, jnp.where(even, rb, ra), 0.0)
            right = jnp.where(has_right, jnp.where(even, ra, rb), 0.0)
            plane = jnp.concatenate([left, own_ref[i].astype(F32), right], axis=0)
        for e in range(taps):
            moved = lane_shift(plane, e, reach, lane).astype(BF16)
            for w in range(p.windows):
                xs_ref[w, e * 32 : e * 32 + 32, z * nx : (z + 1) * nx] = moved[16 * w : 16 * w + 32]

    z_low = jnp.where(has_below, 0, reach)
    z_high = jnp.where(has_above, p.ez, p.ez - reach)
    u_row = lax.broadcasted_iota(jnp.int32, (p.ey, nx), 0)
    lane16 = lax.broadcasted_iota(jnp.int32, (16, nx), 1)

    def visit(t, k, rank):
        block, view = pairs_ref[2 * t], pairs_ref[2 * t + 1]
        bl = lax.rem(lax.rem(block, p.row_blocks), p.blocks)
        kid = ids_ref[block * p.views + view]
        if p.fast:
            x = (kid // p.n_gz) ^ b
            at = jnp.where(lax.rem(kid, p.n_gz) == g, 0, p.n_blk) + (x ^ (x >> 1))
            at = at * p.views_here + (view - v * p.views_here)
        else:
            at = (view - v * p.views_here) * p.n_sets + kid
        w, odd = bl // 2, lax.rem(bl, 2)
        for kk in range(p.n_blk):

            @pl.when(k == kk)
            def _():
                tile_ref[...] = arrived[kk][rank]

        base = kf_ref[pl.ds(pl.multiple_of(at * 8, 8), 8), :]
        base = jnp.where(odd == 1, pltpu.roll(base, 10, 1), pltpu.roll(base, 2, 1))
        wf = [
            pltpu.roll(jnp.broadcast_to(base[a : a + 1], (16, 256)), 0, 1, stride=1, stride_axis=0)
            for a in range(taps)
        ]
        wf = jnp.concatenate(wf, axis=0).astype(BF16)
        base = kb_ref[pl.ds(pl.multiple_of(at * 8, 8), 8), :]
        wb = [
            pltpu.roll(jnp.broadcast_to(base[a : a + 1], (8, 128)), 0, 1, stride=1, stride_axis=0)
            for a in range(taps)
        ]
        wb = jnp.concatenate(wb, axis=0).astype(BF16)

        y_first = lax.rem(block, p.row_blocks) * p.by - reach
        y_ok = (u_row + y_first >= 0) & (u_row + y_first < p.row_blocks * p.by)
        acc = {}
        for pair in range(p.zz // 2):
            got = jnp.dot(wf, xs_ref[w, :, pair * 2 * nx : (pair + 1) * 2 * nx], preferred_element_type=F32)
            for half in range(2):
                z = pair * 2 + half
                for a in range(taps):
                    s = z - a
                    if 0 <= s < p.ez:
                        part = got[16 * a : 16 * a + 16, half * nx : (half + 1) * nx]
                        acc[s] = part if s not in acc else acc[s] + part
                s = z - taps + 1
                if 0 <= s < p.ez:
                    z_ok = (s >= z_low) & (s < z_high)
                    ratio = tile_ref[s].astype(F32) / acc[s][: p.ey]
                    r_ref[s, : p.ey, :] = jnp.where(y_ok & z_ok, ratio, 0.0)
                    full = r_ref[s]
                    for e in range(taps):
                        r2_ref[e * 16 : e * 16 + 16, s * nx : (s + 1) * nx] = lane_shift(
                            full, e, reach, lane16
                        ).astype(BF16)
        term = {}
        for pair in range(p.ez // 2):
            got = jnp.dot(wb, r2_ref[:, pair * 2 * nx : (pair + 1) * 2 * nx], preferred_element_type=F32)
            for half in range(2):
                s = pair * 2 + half
                for a in range(taps):
                    z = s + a - 2 * reach
                    if 0 <= z < p.cz:
                        part = got[8 * a : 8 * a + 8, half * nx : (half + 1) * nx]
                        term[z] = part if z not in term else term[z] + part
        for z in range(p.cz):
            at_y = pl.ds(pl.multiple_of(bl * 8, 8), 8)
            out_ref[z, at_y, :] = out_ref[z, at_y, :] + term[z]

    def from_source(k, carry):
        src = lax.rem(b - k + p.n_blk, p.n_blk)
        first = ((src * p.n_gz + g) * p.n_view + v) * p.tiles

        def one(j, rank):
            home = lax.rem(pairs_ref[2 * (first + j)], p.row_blocks) // p.blocks
            mine = home == b

            @pl.when(mine)
            def _():
                visit(first + j, k, rank)

            return rank + mine.astype(jnp.int32)

        lax.fori_loop(0, p.tiles, one, jnp.int32(0))
        return carry

    lax.fori_loop(0, p.n_blk, from_source, 0)


def corrections(p, pairs, ids, pieces, kern, arrived):
    return pl.pallas_call(
        functools.partial(tiles_kernel, p),
        out_shape=jax.ShapeDtypeStruct((p.cz, p.ly, p.nx), F32),
        in_specs=[SM, SM] + [VM] * (6 + p.n_blk),
        out_specs=VM,
        scratch_shapes=[
            pltpu.VMEM((p.windows, 256, p.zz * p.nx), BF16),
            pltpu.VMEM((kern.shape[0], 256), F32),
            pltpu.VMEM((kern.shape[0], 128), F32),
            pltpu.VMEM((p.ez, p.ey, p.nx), BF16),
            pltpu.VMEM((p.ez, 16, p.nx), F32),
            pltpu.VMEM((128, p.ez * p.nx), BF16),
        ],
        name="tiles",
    )(pairs, ids, *pieces, kern, *arrived)


def on_device(estimate, view_tiles, tile_pairs, kernel_table, kernel_ids):
    p = Plan(estimate, view_tiles, tile_pairs, kernel_table, kernel_ids)
    b, g, v = ranks()
    pairs = tile_pairs.reshape(-1)
    ids = kernel_ids.reshape(-1)
    first_block = g * p.row_blocks + b * p.blocks
    own_blocks = first_block + jnp.arange(p.blocks, dtype=jnp.int32)
    count = jnp.sum((tile_pairs[None, :, 0] == own_blocks[:, None]).astype(F32), axis=1)

    kern = kernel_table.reshape(p.views_here * p.sets_here, p.taps, p.taps * p.taps)
    kern = jnp.pad(kern, ((0, 0), (0, 1), (0, 128 - p.taps * p.taps)))
    if not p.fast:
        kern = kern.reshape(p.views_here, p.sets_here * 8, 128)
        kern = lax.all_gather(kern, ("blk", "gz"), axis=1, tiled=True)
    kern = kern.reshape(-1, 128)

    pieces, gathered = halos(p, *first_sends(p, estimate), kern)
    kern = gathered if p.fast else kern
    packed = pack(p, pairs, view_tiles)
    arrived = [packed[0]] + [
        lax.ppermute(packed[k], "blk", [(i, (i + k) % p.n_blk) for i in range(p.n_blk)])
        for k in range(1, p.n_blk)
    ]
    current = estimate
    for iteration in range(ITERS):
        mine = corrections(p, pairs, ids, pieces, kern, arrived)
        other = lax.ppermute(mine, "view", [(0, 1), (1, 0)])
        last = iteration == ITERS - 1
        out = update(p, count, current, mine, other, last)
        current = out[0]
        if not last:
            pieces, _ = halos(p, *out[1:])
    return current


def solution(mesh):
    in_specs = (
        P(("group", "gz"), "blk", None),
        P(("group", "blk", "gz", "view"), None, None, None),
        P("group", None),
        P("view", ("group", "blk", "gz"), None, None, None),
        P("group", None),
    )
    out_specs = P(("group", "gz"), "blk", None)
    return jax.shard_map(
        on_device, mesh=mesh, in_specs=in_specs, out_specs=out_specs, check_vma=False
    )
```

time: 761 us -> 81.8 us (0.11); the launches traced: 751 us -> 80.3 us
  waiting for transfers between devices: 466 us -> 23.3 us
  loops' own time: 88.1 us -> 0 us
  local copies, waits for them, and re-layouts: 74.3 us -> 8.29 us
  matrix products: 46.2 us -> 0 us
  Pallas kernels: 0 us -> 22.6 us
  blocking collectives: 20.6 us -> 0 us
  between operations: 13.7 us -> 0.08 us
  other arithmetic: 15.5 us -> 2.94 us
    psum x2 -> x0, waiting for transfers between devices: 458 us -> none  [on_device(): combined = lax.psum(summed, 'view')]
    another operation x2 -> x0, loops' own time: 88.1 us -> none  [on_device(): lax.fori_loop(0, live_count, visit_tile, jnp.zeros(estimate.shape, jnp.fl...]
    dot_general x128 -> x0, matrix products: 46.2 us -> none  [the longest x56 14.7 us: blurring(): jnp.dot(matrix_rows, forward[plane_z], preferred_element_type=jnp.float32)]
    dynamic_slice x48 -> x0, local copies, waits for them, and re-layouts: 35 us -> none  [the longest x8 10.6 us: correction_for(): kernel_ids[block_id, view_id]]
    pallas_call x0 -> x8, Pallas kernels: none -> 22.6 us  [the longest x2 12.5 us: corrections(): pl.pallas_call(functools.partial(tiles_kernel, p), out_shape=jax.ShapeDty...]
    all_gather x1 -> x0, blocking collectives: 20.6 us -> none  [on_device(): kernels = lax.all_gather(kernel_table, ('blk', 'gz'), axis=1, tiled=True)]
    slice x196 -> x4, local copies, waits for them, and re-layouts: 17.6 us -> 0.63 us  [the longest x1 0.62 us: halos(): below = above = got[:ne].reshape(edge.shape)]
    ppermute x8 -> x11, waiting for transfers between devices: 8.87 us -> 23.3 us  [the longest x1 13.7 us: halos(): lax.ppermute(jnp.concatenate([sb.reshape(nz, p.nx), kern]), 'blk', odd)]
  transfers between devices with their start and end apart: 11 -> 11, of which waited for: 6 -> 6; matrix products, arithmetic and copies ran while one was open for 1% -> 7% of each run, Pallas kernels for 0% -> 4%
where the time goes in v1:
time: 81.8 us; the launch traced here: 80.3 us
  waiting for transfers between devices  23.3 us (28%)
  starting transfers between devices  23.1 us (28%)
  Pallas kernels  22.6 us (28%)
  local copies, waits for them, and re-layouts  8.29 us (10%)
  other arithmetic  2.94 us (4%)
    ppermute x2, starting transfers between devices, on_device(): other = lax.ppermute(mine, 'view', [(0, 1), (1, 0)])  17.6 us
    ppermute x1, waiting for transfers between devices, halos(): lax.ppermute(jnp.concatenate([sb.reshape(nz, p.nx), kern]), 'blk', odd)  13.7 us
    pallas_call x2, Pallas kernels, corrections(): pl.pallas_call(functools.partial(tiles_kernel, p), out_shape=jax.ShapeDty...  12.5 us
    unnamed x24, local copies, waits for them, and re-layouts  4.19 us
    ppermute x3, starting transfers between devices, on_device(): lax.ppermute(packed[k], 'blk', [(i, (i + k) % p.n_blk) for i in range(p.n...  3.77 us
    pallas_call x2, Pallas kernels, update(): pl.pallas_call(functools.partial(update_kernel, p), out_shape=shapes, in_...  3.49 us
    ppermute x1, waiting for transfers between devices, halos(): below = above = lax.ppermute(out[0], 'gz', swap)  3.22 us
    pallas_call x2, Pallas kernels, halos(): pl.pallas_call(functools.partial(edges_kernel, p), out_shape=[edge] if tw...  3 us
  transfers between devices with their start and end apart: 11, of which 6 were waited for; matrix products, arithmetic and copies ran while one was open for 7% of the time, Pallas kernels for 4%

profile of v1, /device:TPU:11, one launch (start us, length us, event | category | flops | bytes accessed | tf_op | source)
XLA Modules:
  0.0 80.3 jit_solution(15753203612966245347)
XLA Ops:
  0.0 0.9 %reshape.38 = bf16[3,7,49]{2,1,0:T(8,128)(2,1)S(1)} reshape(bf16[3,1,7,7,7]{4,3,2,1,0:T(8,128)(2,1)} %param.8) | data formatting | bytes 4116 | tf_op jit(solution)/shard_map/reshape | solution.py:356
  0.9 1.5 %first.1 = (bf16[8,32,128]{2,1,0:T(8,128)(2,1)}, bf16[8,8,128]{2,1,0:T(8,128)(2,1)}, bf16[8,8,128]{2,1,0:T(8,128)(2,1)}) custom-call(f32[8,32,128]{2,1,0:T(8,128)} %est_ref.3), custom_call_target="tpu_custom_call" | custom-call | tf_op jit(solution)/shard_map/first/pallas_call | solution.py:124
  2.4 0.0 copy-start.10
  2.4 0.7 pad_maximum_fusion.3
  3.2 0.2 collective-permute-start
  3.3 0.0 copy-done.10
  3.4 0.1 copy.8
  3.5 0.7 reshape.35.pairs_ref
  4.2 2.1 %pack.1 = (bf16[3,14,14,128]{3,2,1,0:T(8,128)(2,1)}, bf16[3,14,14,128]{3,2,1,0:T(8,128)(2,1)}, bf16[3,14,14,128]{3,2,1,0:T(8,128)(2,1)}, bf16[3,14,14,128]{3,2,1,0:T(8,128)(2,1)}) custom-call(s32[192]{0:T(256)} %reshape.35.pairs_ref, bf16[6,14,14,128]{3,2,1,0:T(8,128)(2,1)} %tiles_ref.1), custom_call_target="tpu_custom_call" | custom-call | tf_op jit(solution)/shard_map/pack/pallas_call | solution.py:75
  6.2 0.0 copy-start.8
  6.2 2.4 %collective-permute-start.3 = (bf16[3,14,14,128]{3,2,1,0:T(8,128)(2,1)}, bf16[3,14,14,128]{3,2,1,0:T(8,128)(2,1)S(1)}, u32[]{:S(2)}, u32[]{:S(2)}) collective-permute-start(bf16[3,14,14,128]{3,2,1,0:T(8,128)(2,1)} %get-tuple-element.20), channel_id=1, source_target_pairs={{0,4},{4,8},{8,12},{12,0},{1,5},{5,9},{9,13},{13,1},{2,6},{6,10},{... | collective-permute-start | bytes 451592 | tf_op jit(solution)/shard_map/ppermute | solution.py:367
  8.7 1.0 %collective-permute-start.4 = (bf16[3,14,14,128]{3,2,1,0:T(8,128)(2,1)}, bf16[3,14,14,128]{3,2,1,0:T(8,128)(2,1)S(1)}, u32[]{:S(2)}, u32[]{:S(2)}) collective-permute-start(bf16[3,14,14,128]{3,2,1,0:T(8,128)(2,1)} %get-tuple-element.21), channel_id=1, source_target_pairs={{0,8},{4,12},{8,0},{12,4},{1,9},{5,13},{9,1},{13,5},{2,10},{6,14},... | collective-permute-start | bytes 451592 | tf_op jit(solution)/shard_map/ppermute | solution.py:367
  9.6 0.4 collective-permute-start.5
  10.0 0.0 collective-permute-done
  10.0 0.0 copy-done.8
  10.0 1.1 %collective-permute-start.1 = (bf16[112,128]{1,0:T(8,128)(2,1)S(1)}, bf16[112,128]{1,0:T(8,128)(2,1)S(1)}, u32[]{:S(2)}, u32[]{:S(2)}) collective-permute-start(bf16[112,128]{1,0:T(8,128)(2,1)S(1)} %pad_maximum_fusion.2), channel_id=1, source_target_pairs={{0,12},{4,8},{8,4},{12,0},{1,13},{5,9},{9,5},{13,1},{2,14},{6,10},... | collective-permute-start | bytes 86024 | tf_op jit(solution)/shard_map/ppermute | solution.py:168
  11.2 0.6 slice_bitcast_fusion.1.ra_ref
  11.8 13.7 %collective-permute-done.1 = bf16[112,128]{1,0:T(8,128)(2,1)S(1)} collective-permute-done((bf16[112,128]{1,0:T(8,128)(2,1)S(1)}, bf16[112,128]{1,0:T(8,128)(2,1)S(1)}, u32[]{:S(2)}, u32[]{:S(2)}) %collective-permute-start.1) | collective-permute-done | bytes 28704 | tf_op jit(solution)/shard_map/ppermute | solution.py:168
  25.5 0.6 slice_bitcast_fusion.rb_ref
  26.1 1.5 %edges.2 = bf16[6,48,128]{2,1,0:T(8,128)(2,1)} custom-call(bf16[8,32,128]{2,1,0:T(8,128)(2,1)} %get-tuple-element.16.own_ref, bf16[8,8,128]{2,1,0:T(8,128)(2,1)} %slice_bitcast_fusion.1.ra_ref, bf16[8,8,128]{2,1,0:T(8,128)(2,1)} %slice_bitcast_fusion.rb_ref), custom_call_target="tpu_custom_call" | custom-call | tf_op jit(solution)/shard_map/edges/pallas_call | solution.py:174
  27.6 0.9 %pad_maximum_fusion = bf16[384,128]{1,0:T(8,128)(2,1)S(1)} fusion(bf16[48,128]{1,0:T(8,128)(2,1)S(1)} %slice.31, bf16[24,128]{1,0:T(8,128)(2,1)S(1)} %slice.29, bf16[24,128]{1,0:T(8,128)(2,1)S(1)} %pad_bitcast_fusion, bf16[288,128]{1,0:T(8,128)(2,1)} %bitcast.14), kind=kLoop, calls=%fused_computation | loop fusion | flops 393216 | bytes 196608 | tf_op jit(solution)/shard_map/concatenate | solution.py:182
  28.5 0.1 collective-permute-start.2
  28.7 0.0 copy-start.9
  28.7 0.7 copy-done.9
  29.4 0.1 copy.9
  29.4 0.7 reshape.36.ids_ref
  30.1 1.9 %collective-permute-done.2 = bf16[384,128]{1,0:T(8,128)(2,1)S(1)} collective-permute-done((bf16[384,128]{1,0:T(8,128)(2,1)S(1)}, bf16[384,128]{1,0:T(8,128)(2,1)S(1)}, u32[]{:S(2)}, u32[]{:S(2)}) %collective-permute-start.2) | collective-permute-done | bytes 98336 | tf_op jit(solution)/shard_map/ppermute | solution.py:182
  32.0 0.6 slice.32
  32.6 0.6 pad_maximum_fusion.1.kern_ref
  33.2 0.0 collective-permute-done.3.rest_1_
  33.2 0.0 copy-start
  33.2 0.0 collective-permute-done.4.rest_2_
  33.2 0.0 copy-start.1
  33.2 0.0 collective-permute-done.5.rest_3_
  33.3 0.0 copy-start.2
  33.3 0.6 copy-done
  33.9 0.1 copy-done.1
  34.0 0.1 copy-done.2
  34.0 6.3 %tiles.2.mine_ref = f32[8,32,128]{2,1,0:T(8,128)} custom-call(s32[192]{0:T(256)} %reshape.35.pairs_ref, s32[192]{0:T(256)} %reshape.36.ids_ref, bf16[8,32,128]{2,1,0:T(8,128)(2,1)} %get-tuple-element.16.own_ref, bf16[8,8,128]{2,1,0:T(8,128)(2,1)} %slice_bitcast_fusion.1.ra_ref, bf16[8,8,128]{2,1,0:T(8,128)(2,1)} %slice_bitcast_fusion.rb_ref, ...), custom_call_target="tpu_custom_call" | custom-call | tf_op jit(solution)/shard_map/tiles/pallas_call | solution.py:330
  40.3 8.7 %collective-permute-start.6 = (f32[8,32,128]{2,1,0:T(8,128)}, f32[8,32,128]{2,1,0:T(8,128)S(1)}, u32[]{:S(2)}, u32[]{:S(2)}) collective-permute-start(f32[8,32,128]{2,1,0:T(8,128)} %tiles.2.mine_ref), channel_id=1, source_target_pairs={{0,1},{1,0},{2,3},{3,2},{4,5},{5,4},{6,7},{7,6},{8,9},{9,8},{10,11... | collective-permute-start | bytes 393224 | tf_op jit(solution)/shard_map/ppermute | solution.py:373
  48.9 0.7 convert_reduce_fusion.count_ref
  49.6 0.5 collective-permute-done.6.other_ref
  50.1 0.0 copy-start.5
  50.1 0.7 copy-done.5
  50.8 1.8 %update.2 = (f32[8,32,128]{2,1,0:T(8,128)}, bf16[8,32,128]{2,1,0:T(8,128)(2,1)}, bf16[8,8,128]{2,1,0:T(8,128)(2,1)}, bf16[8,8,128]{2,1,0:T(8,128)(2,1)}) custom-call(f32[4]{0:T(128)} %convert_reduce_fusion.count_ref, f32[8,32,128]{2,1,0:T(8,128)} %est_ref.3, f32[8,32,128]{2,1,0:T(8,128)} %tiles.2.mine_ref, f32[8,32,128]{2,1,0:T(8,128)} %copy-done.5), custom_call_target="tpu_custom_call" | custom-call | tf_op jit(solution)/shard_map/update/pallas_call | solution.py:132
  52.6 0.0 collective-permute-start.7
  52.6 0.0 collective-permute-start.8
  52.6 2.8 %collective-permute-done.7.ra_ref = bf16[8,8,128]{2,1,0:T(8,128)(2,1)S(1)} collective-permute-done((bf16[8,8,128]{2,1,0:T(8,128)(2,1)}, bf16[8,8,128]{2,1,0:T(8,128)(2,1)S(1)}, u32[]{:S(2)}, u32[]{:S(2)}) %collective-permute-start.7) | collective-permute-done | bytes 16416 | tf_op jit(solution)/shard_map/ppermute | solution.py:171
  55.4 0.0 copy-start.6
  55.4 0.0 collective-permute-done.8.rb_ref
  55.4 0.0 copy-start.7
  55.4 0.6 copy-done.6
  56.0 0.0 copy-done.7
  56.0 1.5 %edges.3 = bf16[6,48,128]{2,1,0:T(8,128)(2,1)} custom-call(bf16[8,32,128]{2,1,0:T(8,128)(2,1)} %get-tuple-element.24.own_ref, bf16[8,8,128]{2,1,0:T(8,128)(2,1)} %copy-done.6, bf16[8,8,128]{2,1,0:T(8,128)(2,1)} %copy-done.7), custom_call_target="tpu_custom_call" | custom-call | tf_op jit(solution)/shard_map/edges/pallas_call | solution.py:174
  57.5 0.2 collective-permute-start.9
  57.7 3.2 %collective-permute-done.9.below_ref.above_ref = bf16[6,48,128]{2,1,0:T(8,128)(2,1)S(1)} collective-permute-done((bf16[6,48,128]{2,1,0:T(8,128)(2,1)}, bf16[6,48,128]{2,1,0:T(8,128)(2,1)S(1)}, u32[]{:S(2)}, u32[]{:S(2)}) %collective-permute-start.9) | collective-permute-done | bytes 73760 | tf_op jit(solution)/shard_map/ppermute | solution.py:186
  60.9 0.0 copy-start.3
  60.9 0.6 copy-done.3
  61.6 6.3 %tiles.3.mine_ref = f32[8,32,128]{2,1,0:T(8,128)} custom-call(s32[192]{0:T(256)} %reshape.35.pairs_ref, s32[192]{0:T(256)} %reshape.36.ids_ref, bf16[8,32,128]{2,1,0:T(8,128)(2,1)} %get-tuple-element.24.own_ref, bf16[8,8,128]{2,1,0:T(8,128)(2,1)} %copy-done.6, bf16[8,8,128]{2,1,0:T(8,128)(2,1)} %copy-done.7, bf16[6,48,128]{2,1,0:T(8,128)(2,1)} %copy-done.3, ...), custom_call_target="tpu_custom_call" | custom-call | tf_op jit(solution)/shard_map/tiles/pallas_call | solution.py:330
  67.8 8.9 %collective-permute-start.10 = (f32[8,32,128]{2,1,0:T(8,128)}, f32[8,32,128]{2,1,0:T(8,128)S(1)}, u32[]{:S(2)}, u32[]{:S(2)}) collective-permute-start(f32[8,32,128]{2,1,0:T(8,128)} %tiles.3.mine_ref), channel_id=1, source_target_pairs={{0,1},{1,0},{2,3},{3,2},{4,5},{5,4},{6,7},{7,6},{8,9},{9,8},{10,11... | collective-permute-start | bytes 393224 | tf_op jit(solution)/shard_map/ppermute | solution.py:373
  76.8 1.2 %collective-permute-done.10.other_ref = f32[8,32,128]{2,1,0:T(8,128)S(1)} collective-permute-done((f32[8,32,128]{2,1,0:T(8,128)}, f32[8,32,128]{2,1,0:T(8,128)S(1)}, u32[]{:S(2)}, u32[]{:S(2)}) %collective-permute-start.10) | collective-permute-done | bytes 131104 | tf_op jit(solution)/shard_map/ppermute | solution.py:373
  78.0 0.0 copy-start.4
  78.0 0.6 copy-done.4
  78.6 1.7 %update.3 = f32[8,32,128]{2,1,0:T(8,128)} custom-call(f32[4]{0:T(128)} %convert_reduce_fusion.count_ref, f32[8,32,128]{2,1,0:T(8,128)} %get-tuple-element.23.est_ref, f32[8,32,128]{2,1,0:T(8,128)} %tiles.3.mine_ref, f32[8,32,128]{2,1,0:T(8,128)} %copy-done.4), custom_call_target="tpu_custom_call" | custom-call | tf_op jit(solution)/shard_map/update/pallas_call | solution.py:132
  (7 shorter events, 0.0 us)
Async XLA Ops:
  2.4 0.9 %copy-start.10 = (s32[96,2]{0,1:T(2,128)S(1)}, s32[96,2]{0,1:T(2,128)}, u32[]{:S(2)}) copy-start(s32[96,2]{0,1:T(2,128)} %param.7) | copy-start | bytes 2308
  3.2 6.8 %collective-permute-start = (bf16[88,128]{1,0:T(8,128)(2,1)S(1)}, bf16[88,128]{1,0:T(8,128)(2,1)S(1)}, u32[]{:S(2)}, u32[]{:S(2)}) collective-permute-start(bf16[88,128]{1,0:T(8,128)(2,1)S(1)} %pad_maximum_fusion.3), channel_id=1, source_target_pairs={{0,4},{4,0},{8,12},{12,8},{1,5},{5,1},{9,13},{13,9},{2,6},{6,2},{1... | collective-permute-start | bytes 67592 | tf_op jit(solution)/shard_map/ppermute | solution.py:166
  6.2 3.8 %copy-start.8 = (bf16[8,8,128]{2,1,0:T(8,128)(2,1)S(1)}, bf16[8,8,128]{2,1,0:T(8,128)(2,1)}, u32[]{:S(2)}) copy-start(bf16[8,8,128]{2,1,0:T(8,128)(2,1)} %get-tuple-element.18) | copy-start | bytes 49156
  6.2 27.0 %collective-permute-start.3 = (bf16[3,14,14,128]{3,2,1,0:T(8,128)(2,1)}, bf16[3,14,14,128]{3,2,1,0:T(8,128)(2,1)S(1)}, u32[]{:S(2)}, u32[]{:S(2)}) collective-permute-start(bf16[3,14,14,128]{3,2,1,0:T(8,128)(2,1)} %get-tuple-element.20), channel_id=1, source_target_pairs={{0,4},{4,8},{8,12},{12,0},{1,5},{5,9},{9,13},{13,1},{2,6},{6,10},{... | collective-permute-start | bytes 451592 | tf_op jit(solution)/shard_map/ppermute | solution.py:367
  8.7 24.6 %collective-permute-start.4 = (bf16[3,14,14,128]{3,2,1,0:T(8,128)(2,1)}, bf16[3,14,14,128]{3,2,1,0:T(8,128)(2,1)S(1)}, u32[]{:S(2)}, u32[]{:S(2)}) collective-permute-start(bf16[3,14,14,128]{3,2,1,0:T(8,128)(2,1)} %get-tuple-element.21), channel_id=1, source_target_pairs={{0,8},{4,12},{8,0},{12,4},{1,9},{5,13},{9,1},{13,5},{2,10},{6,14},... | collective-permute-start | bytes 451592 | tf_op jit(solution)/shard_map/ppermute | solution.py:367
  9.6 23.6 %collective-permute-start.5 = (bf16[3,14,14,128]{3,2,1,0:T(8,128)(2,1)}, bf16[3,14,14,128]{3,2,1,0:T(8,128)(2,1)S(1)}, u32[]{:S(2)}, u32[]{:S(2)}) collective-permute-start(bf16[3,14,14,128]{3,2,1,0:T(8,128)(2,1)} %get-tuple-element.22), channel_id=1, source_target_pairs={{0,12},{4,0},{8,4},{12,8},{1,13},{5,1},{9,5},{13,9},{2,14},{6,2},{... | collective-permute-start | bytes 451592 | tf_op jit(solution)/shard_map/ppermute | solution.py:367
  10.0 15.5 %collective-permute-start.1 = (bf16[112,128]{1,0:T(8,128)(2,1)S(1)}, bf16[112,128]{1,0:T(8,128)(2,1)S(1)}, u32[]{:S(2)}, u32[]{:S(2)}) collective-permute-start(bf16[112,128]{1,0:T(8,128)(2,1)S(1)} %pad_maximum_fusion.2), channel_id=1, source_target_pairs={{0,12},{4,8},{8,4},{12,0},{1,13},{5,9},{9,5},{13,1},{2,14},{6,10},... | collective-permute-start | bytes 86024 | tf_op jit(solution)/shard_map/ppermute | solution.py:168
  28.5 3.5 %collective-permute-start.2 = (bf16[384,128]{1,0:T(8,128)(2,1)S(1)}, bf16[384,128]{1,0:T(8,128)(2,1)S(1)}, u32[]{:S(2)}, u32[]{:S(2)}) collective-permute-start(bf16[384,128]{1,0:T(8,128)(2,1)S(1)} %pad_maximum_fusion), channel_id=1, source_target_pairs={{0,2},{2,0},{1,3},{3,1},{4,6},{6,4},{5,7},{7,5},{8,10},{10,8},{9,1... | collective-permute-start | bytes 294920 | tf_op jit(solution)/shard_map/ppermute | solution.py:182
  28.7 0.7 copy-start.9
  33.2 0.7 copy-start
  33.2 0.7 copy-start.1
  33.3 0.8 copy-start.2
  40.3 9.8 %collective-permute-start.6 = (f32[8,32,128]{2,1,0:T(8,128)}, f32[8,32,128]{2,1,0:T(8,128)S(1)}, u32[]{:S(2)}, u32[]{:S(2)}) collective-permute-start(f32[8,32,128]{2,1,0:T(8,128)} %tiles.2.mine_ref), channel_id=1, source_target_pairs={{0,1},{1,0},{2,3},{3,2},{4,5},{5,4},{6,7},{7,6},{8,9},{9,8},{10,11... | collective-permute-start | bytes 393224 | tf_op jit(solution)/shard_map/ppermute | solution.py:373
  50.1 0.7 copy-start.5
  52.6 2.8 %collective-permute-start.7 = (bf16[8,8,128]{2,1,0:T(8,128)(2,1)}, bf16[8,8,128]{2,1,0:T(8,128)(2,1)S(1)}, u32[]{:S(2)}, u32[]{:S(2)}) collective-permute-start(bf16[8,8,128]{2,1,0:T(8,128)(2,1)} %get-tuple-element.25), channel_id=1, source_target_pairs={{0,4},{4,0},{8,12},{12,8},{1,5},{5,1},{9,13},{13,9},{2,6},{6,2},{1... | collective-permute-start | bytes 49160 | tf_op jit(solution)/shard_map/ppermute | solution.py:171
  52.6 2.8 %collective-permute-start.8 = (bf16[8,8,128]{2,1,0:T(8,128)(2,1)}, bf16[8,8,128]{2,1,0:T(8,128)(2,1)S(1)}, u32[]{:S(2)}, u32[]{:S(2)}) collective-permute-start(bf16[8,8,128]{2,1,0:T(8,128)(2,1)} %get-tuple-element.26), channel_id=1, source_target_pairs={{0,12},{4,8},{8,4},{12,0},{1,13},{5,9},{9,5},{13,1},{2,14},{6,10},... | collective-permute-start | bytes 49160 | tf_op jit(solution)/shard_map/ppermute | solution.py:171
  55.4 0.6 copy-start.6
  55.4 0.6 copy-start.7
  57.5 3.4 %collective-permute-start.9 = (bf16[6,48,128]{2,1,0:T(8,128)(2,1)}, bf16[6,48,128]{2,1,0:T(8,128)(2,1)S(1)}, u32[]{:S(2)}, u32[]{:S(2)}) collective-permute-start(bf16[6,48,128]{2,1,0:T(8,128)(2,1)} %edges.3), channel_id=1, source_target_pairs={{0,2},{2,0},{1,3},{3,1},{4,6},{6,4},{5,7},{7,5},{8,10},{10,8},{9,1... | collective-permute-start | bytes 221192 | tf_op jit(solution)/shard_map/ppermute | solution.py:186
  60.9 0.6 copy-start.3
  67.8 10.1 %collective-permute-start.10 = (f32[8,32,128]{2,1,0:T(8,128)}, f32[8,32,128]{2,1,0:T(8,128)S(1)}, u32[]{:S(2)}, u32[]{:S(2)}) collective-permute-start(f32[8,32,128]{2,1,0:T(8,128)} %tiles.3.mine_ref), channel_id=1, source_target_pairs={{0,1},{1,0},{2,3},{3,2},{4,5},{5,4},{6,7},{7,6},{8,9},{9,8},{10,11... | collective-permute-start | bytes 393224 | tf_op jit(solution)/shard_map/ppermute | solution.py:373
  78.0 0.6 copy-start.4

commit v2 on v1

v2 whole, which is shorter than its diff:
```python
import functools

import jax
import jax.numpy as jnp
from jax import lax
from jax.experimental import pallas as pl
from jax.experimental.pallas import tpu as pltpu
from jax.sharding import PartitionSpec as P


ITERS = 2
F32, BF16 = jnp.float32, jnp.bfloat16
VM = pl.BlockSpec(memory_space=pltpu.VMEM)
SM = pl.BlockSpec(memory_space=pltpu.SMEM)


def send_order(n_blk):
    return sorted(range(1, n_blk), key=lambda k: (k < n_blk // 2, k))


class Plan:
    def __init__(self, estimate, view_tiles, kernel_table):
        self.cz, self.ly, self.nx = estimate.shape
        self.tiles, self.ez, self.ey, _ = view_tiles.shape
        self.views_here, self.sets_here, self.taps = kernel_table.shape[:3]
        self.reach = (self.taps - 1) // 2
        self.by = self.ey - 2 * self.reach
        self.blocks = self.ly // self.by
        self.n_blk = lax.axis_size("blk")
        self.n_gz = lax.axis_size("gz")
        self.n_view = lax.axis_size("view")
        self.views = self.views_here * self.n_view
        self.row_blocks = self.blocks * self.n_blk
        self.slots = -(-self.views_here * self.blocks // self.n_blk)
        self.slots = min(self.slots, self.tiles)
        self.fast = self.n_blk == 4 and self.n_gz == 2 and self.sets_here == 1
        self.n_sets = self.n_blk * self.n_gz * self.sets_here
        self.halo = 2 * self.reach
        assert self.by == 8 and self.cz == 8 and self.nx == 128 and self.taps == 7
        assert self.n_blk & (self.n_blk - 1) == 0 and self.n_blk > 1 and self.ez <= 16
        self.zz = self.cz + 2 * self.halo
        self.rows = self.ly + 16
        self.yw = 24
        self.depth = (self.taps * self.yw + 15) // 16 * 16
        self.send_order = send_order(self.n_blk)


def ranks():
    return lax.axis_index("blk"), lax.axis_index("gz"), lax.axis_index("view")


def lane_shift(plane, e, reach, lane):
    d = e - reach
    if d == 0:
        return plane
    n = plane.shape[-1]
    rolled = pltpu.roll(plane, (-d) % n, 1)
    ok = (lane < n - d) if d > 0 else (lane >= -d)
    return jnp.where(ok, rolled, 0.0)


def pack_kernel(p, pairs_ref, tiles_ref, *outs):
    b, g, v = ranks()
    first = ((b * p.n_gz + g) * p.n_view + v) * p.tiles
    homes = [(pairs_ref[2 * (first + j)] % p.row_blocks) // p.blocks for j in range(p.tiles)]
    for j in range(p.tiles):
        rank = sum([(homes[i] == homes[j]).astype(jnp.int32) for i in range(j)], jnp.int32(0))
        k = homes[j] ^ b
        for kk in range(p.n_blk):

            @pl.when(k == kk)
            def _():
                for s in range(p.ez):
                    outs[kk][rank, s * p.ey : (s + 1) * p.ey, :] = tiles_ref[j, s]


def pack(p, pairs, tiles):
    return pl.pallas_call(
        functools.partial(pack_kernel, p),
        out_shape=[jax.ShapeDtypeStruct((p.slots, p.ez * p.ey, p.nx), tiles.dtype)] * p.n_blk,
        in_specs=[SM, VM],
        out_specs=[VM] * p.n_blk,
        name="pack", compiler_params=pltpu.CompilerParams(vmem_limit_bytes=4 << 20),
    )(pairs, tiles)


def sends_of(p, b, x, own_ref, sa_ref, sb_ref):
    even = b % 2 == 0
    for z in range(p.cz):
        xb = x[z].astype(BF16)
        own_ref[z] = xb
        lo, hi = xb[:8], xb[p.ly - 8 :]
        lo, hi = x[z][:8], x[z][p.ly - 8 :]
        sa_ref[z] = jnp.where(even, hi, lo).astype(BF16)
        sb_ref[z] = jnp.where(even, lo, hi).astype(BF16)


def first_kernel(p, est_ref, own_ref, sa_ref, sb_ref):
    b, _, _ = ranks()
    sends_of(p, b, [est_ref[z] for z in range(p.cz)], own_ref, sa_ref, sb_ref)


def update_kernel(p, count_ref, est_ref, mine_ref, other_ref, new_ref, own_ref=None, sa_ref=None, sb_ref=None):
    b, _, _ = ranks()
    x = []
    for z in range(p.cz):
        rows = []
        for k in range(p.blocks):
            at = slice(k * 8, k * 8 + 8)
            total = mine_ref[z, at, :] + other_ref[z, at, :]
            rows.append(est_ref[z, at, :] * total / count_ref[k])
        x.append(jnp.concatenate(rows, axis=0))
        new_ref[z] = x[z]
    if own_ref is not None:
        sends_of(p, b, x, own_ref, sa_ref, sb_ref)


def sends_shape(p):
    return [
        jax.ShapeDtypeStruct((p.cz, p.ly, p.nx), BF16),
        jax.ShapeDtypeStruct((p.cz, 8, p.nx), BF16),
        jax.ShapeDtypeStruct((p.cz, 8, p.nx), BF16),
    ]


def first_sends(p, est):
    return pl.pallas_call(
        functools.partial(first_kernel, p), out_shape=sends_shape(p), in_specs=[VM],
        out_specs=[VM] * 3, name="first", compiler_params=pltpu.CompilerParams(vmem_limit_bytes=4 << 20),
    )(est)


def update(p, count, est, mine, other, last):
    shapes = [jax.ShapeDtypeStruct(est.shape, F32)] + ([] if last else sends_shape(p))
    return pl.pallas_call(
        functools.partial(update_kernel, p), out_shape=shapes, in_specs=[SM, VM, VM, VM],
        out_specs=[VM] * len(shapes), name="update", compiler_params=pltpu.CompilerParams(vmem_limit_bytes=4 << 20),
    )(count, est, mine, other)


def edges_kernel(p, own_ref, ra_ref, rb_ref, lo_ref, hi_ref=None):
    b, g, _ = ranks()
    even = b % 2 == 0
    has_lo, has_hi = b > 0, b < p.n_blk - 1

    def planes(out_ref, start):
        for i in range(p.halo):
            ra, rb = ra_ref[start + i].astype(F32), rb_ref[start + i].astype(F32)
            left = jnp.where(has_lo, jnp.where(even, rb, ra), 0.0)
            right = jnp.where(has_hi, jnp.where(even, ra, rb), 0.0)
            out_ref[i, :8] = left.astype(BF16)
            out_ref[i, 8 : 8 + p.ly] = own_ref[start + i]
            out_ref[i, 8 + p.ly :] = right.astype(BF16)

    if hi_ref is None:
        planes(lo_ref, jnp.where(g == 0, p.cz - p.halo, 0))
    else:
        planes(lo_ref, p.cz - p.halo)
        planes(hi_ref, 0)


def pairs_of(n):
    pair = [(i, i ^ 1) for i in range(n)]
    odd = [(i, (i + 1) % n if i % 2 else (i - 1) % n) for i in range(n)]
    return pair, odd


def halos(p, own, sa, sb, kern=None):
    pair, odd = pairs_of(p.n_blk)
    nz = p.cz * 8
    carry = kern is not None and p.fast
    if carry:
        got = lax.ppermute(jnp.concatenate([sa.reshape(nz, p.nx), kern]), "blk", pair)
        ra, kern = got[:nz].reshape(sa.shape), jnp.concatenate([kern, got[nz:]])
        got = lax.ppermute(jnp.concatenate([sb.reshape(nz, p.nx), kern]), "blk", odd)
        rb, kern = got[:nz].reshape(sb.shape), jnp.concatenate([kern, got[nz:]])
    else:
        ra, rb = lax.ppermute(sa, "blk", pair), lax.ppermute(sb, "blk", odd)
    two = p.n_gz == 2
    edge = jax.ShapeDtypeStruct((p.halo, p.rows, p.nx), BF16)
    out = pl.pallas_call(
        functools.partial(edges_kernel, p), out_shape=[edge] if two else [edge, edge],
        in_specs=[VM] * 3, out_specs=[VM] * (1 if two else 2), name="edges",
        compiler_params=pltpu.CompilerParams(vmem_limit_bytes=4 << 20),
    )(own, ra, rb)
    if two:
        swap = [(0, 1), (1, 0)]
        if carry:
            ne = p.halo * p.rows
            got = lax.ppermute(jnp.concatenate([out[0].reshape(ne, p.nx), kern]), "gz", swap)
            below = above = got[:ne].reshape(edge.shape)
            kern = jnp.concatenate([kern, got[ne:]])
        else:
            below = above = lax.ppermute(out[0], "gz", swap)
    else:
        ups = [(i, i + 1) for i in range(p.n_gz - 1)]
        below = lax.ppermute(out[0], "gz", ups)
        above = lax.ppermute(out[1], "gz", [(j, i) for i, j in ups])
    return (own, ra, rb, below, above), kern


def blur_kernel(p, ids_ref, own_ref, ra_ref, rb_ref, below_ref, above_ref, kern_ref, *rest):
    first = len(rest) == 4
    out_ref, kb_ref, xs_ref, kf_ref = rest if first else (rest[0], None, *rest[1:])
    taps, nx, yw = p.taps, p.nx, p.yw
    row = lax.broadcasted_iota(jnp.int32, (128, 256), 0)
    col = lax.broadcasted_iota(jnp.int32, (128, 256), 1)
    select = ((row // taps == col % yw) & (row % taps == col // yw) & (row < taps * taps)).astype(BF16)
    kf_ref[...] = jnp.dot(kern_ref[...], select, preferred_element_type=F32)
    if first:
        row = lax.broadcasted_iota(jnp.int32, (128, 128), 0)
        col = lax.broadcasted_iota(jnp.int32, (128, 128), 1)
        select = (
            (taps - 1 - row // taps == col % 16) & (taps - 1 - row % taps == col // 16) & (row < taps * taps)
        ).astype(BF16)
        kb_ref[...] = jnp.dot(kern_ref[...], select, preferred_element_type=F32)

    b, g, _ = ranks()
    even = b % 2 == 0
    has_left, has_right = b > 0, b < p.n_blk - 1
    has_below, has_above = g > 0, g < p.n_gz - 1
    lane = lax.broadcasted_iota(jnp.int32, (p.rows, nx), 1)
    for z in range(p.zz):
        i = z - p.halo
        if i < 0:
            plane = jnp.where(has_below, below_ref[z].astype(F32), 0.0)
        elif i >= p.cz:
            plane = jnp.where(has_above, above_ref[i - p.cz].astype(F32), 0.0)
        else:
            ra, rb = ra_ref[i].astype(F32), rb_ref[i].astype(F32)
            left = jnp.where(has_left, jnp.where(even, rb, ra), 0.0)
            right = jnp.where(has_right, jnp.where(even, ra, rb), 0.0)
            plane = jnp.concatenate([left, own_ref[i].astype(F32), right], axis=0)
        moved = [lane_shift(plane, e, p.reach, lane) for e in range(taps)] + [jnp.zeros_like(plane)]
        for bl in range(p.blocks):
            for e in range(0, taps, 2):
                at = slice(8 * bl, 8 * bl + yw)
                high = moved[e + 1][at] if e + 1 < taps else jnp.zeros((p.depth - e * yw - yw, nx), F32)
                both = jnp.concatenate([moved[e][at], high], axis=0).astype(BF16)
                xs_ref[bl, e * yw : e * yw + both.shape[0], z * nx : (z + 1) * nx] = both

    def block(bl, carry):
        wf = [[] for _ in range(taps)]
        for view in range(p.views_here):
            base = pltpu.roll(kf_ref[kernel_rows(p, ids_ref, bl, view), :], 2, 1)
            for a in range(taps):
                wide = jnp.broadcast_to(base[a : a + 1], (16, 256))
                wf[a].append(pltpu.roll(wide, 0, 1, stride=1, stride_axis=0))
        wf = jnp.concatenate([x for y in wf for x in y], axis=0).astype(BF16)[:, : p.depth]
        m = 16 * p.views_here
        acc = {}
        for pair in range(p.zz // 2):
            z0 = pair * 2
            lo, hi = max(0, z0 - p.ez + 1), min(taps - 1, z0 + 1)
            got = jnp.dot(
                wf[m * lo : m * (hi + 1)], xs_ref[bl, :, z0 * nx : (z0 + 2) * nx], preferred_element_type=F32
            )
            for half in range(2):
                z = z0 + half
                for a in range(lo, hi + 1):
                    s = z - a
                    if 0 <= s < p.ez:
                        part = got[m * (a - lo) : m * (a - lo + 1), half * nx : (half + 1) * nx]
                        acc[s] = part if s not in acc else acc[s] + part
                s = z - taps + 1
                if 0 <= s < p.ez:
                    done = acc.pop(s)
                    for view in range(p.views_here):
                        out_ref[bl * p.views_here + view, s] = done[16 * view : 16 * view + 16]
        return carry

    lax.fori_loop(0, p.blocks, block, 0)


def kernel_rows(p, ids_ref, bl, view):
    b, g, v = ranks()
    number = g * p.row_blocks + b * p.blocks + bl
    kid = ids_ref[number * p.views + v * p.views_here + view]
    if p.fast:
        x = (kid // p.n_gz) ^ b
        at = jnp.where(lax.rem(kid, p.n_gz) == g, 0, p.n_blk) + (x ^ (x >> 1))
        at = at * p.views_here + view
    else:
        at = view * p.n_sets + kid
    return pl.ds(pl.multiple_of(at * 8, 8), 8)


def blur(p, ids, pieces, kern, first):
    blurred = jax.ShapeDtypeStruct((p.blocks * p.views_here, p.ez, 16, p.nx), F32)
    table = jax.ShapeDtypeStruct((kern.shape[0], 128), F32)
    ins = [ids, *pieces, kern]
    return pl.pallas_call(
        functools.partial(blur_kernel, p),
        out_shape=[blurred, table] if first else [blurred],
        in_specs=[SM] + [VM] * (len(ins) - 1),
        out_specs=[VM] * (2 if first else 1),
        scratch_shapes=[
            pltpu.VMEM((p.blocks, p.depth, p.zz * p.nx), BF16),
            pltpu.VMEM((kern.shape[0], 256), F32),
        ],
        name="blur", compiler_params=pltpu.CompilerParams(vmem_limit_bytes=10 << 20),
    )(*ins)


def spread_kernel(p, pairs_ref, ids_ref, blur_ref, kb_ref, tiles_ref, out_ref, slot_ref, r_ref, r2_ref):
    b, g, v = ranks()
    taps, reach, nx, views = p.taps, p.reach, p.nx, p.views_here
    r_ref[...] = jnp.zeros(r_ref.shape, F32)
    for view in range(views):
        r2_ref[view * 128 + taps * 16 : (view + 1) * 128, :] = jnp.zeros((128 - taps * 16, r2_ref.shape[1]), BF16)
    has_below, has_above = g > 0, g < p.n_gz - 1
    z_low = jnp.where(has_below, 0, reach)
    z_high = jnp.where(has_above, p.ez, p.ez - reach)
    u_row = lax.broadcasted_iota(jnp.int32, (p.ey, nx), 0)
    lane16 = lax.broadcasted_iota(jnp.int32, (16, nx), 1)

    for i in range(p.blocks * views):
        slot_ref[i] = -1

    def from_source(k, carry):
        first = (((b ^ k) * p.n_gz + g) * p.n_view + v) * p.tiles
        rank = jnp.int32(0)
        for j in range(p.tiles):
            place = lax.rem(pairs_ref[2 * (first + j)], p.row_blocks)
            mine = place // p.blocks == b
            at = lax.rem(place, p.blocks) * views + pairs_ref[2 * (first + j) + 1] - v * views
            at = jnp.where(mine, at, p.blocks * views)
            slot_ref[at] = k * p.slots + rank
            rank = rank + mine.astype(jnp.int32)
        return carry

    lax.fori_loop(0, p.n_blk, from_source, 0)

    def block(bl, carry):
        wb = []
        for view in range(views):
            base = kb_ref[kernel_rows(p, ids_ref, bl, view), :]
            rows = [
                pltpu.roll(jnp.broadcast_to(base[a : a + 1], (8, 128)), 0, 1, stride=1, stride_axis=0)
                for a in range(taps)
            ]
            wb.append(jnp.concatenate(rows + [jnp.zeros((8, 128), F32)], axis=0))
        wb = jnp.concatenate(wb, axis=1).astype(BF16)
        y_first = (b * p.blocks + bl) * p.by - reach
        y_ok = (u_row + y_first >= 0) & (u_row + y_first < p.row_blocks * p.by)
        slots = [slot_ref[bl * views + view] for view in range(views)]
        term = {}
        for pair in range(p.ez // 2):
            s0 = pair * 2
            for s in (s0, s0 + 1):
                z_ok = (s >= z_low) & (s < z_high)
                for view in range(views):
                    tile = tiles_ref[jnp.maximum(slots[view], 0), s * p.ey : (s + 1) * p.ey, :].astype(F32)
                    ratio = tile / blur_ref[bl * views + view, s, : p.ey, :]
                    keep = y_ok & (z_ok & (slots[view] >= 0))
                    r_ref[view, s, : p.ey, :] = jnp.where(keep, ratio, 0.0)
                    full = r_ref[view, s]
                    for e in range(taps):
                        at = view * 128 + e * 16
                        r2_ref[at : at + 16, s * nx : (s + 1) * nx] = lane_shift(full, e, reach, lane16).astype(BF16)
            lo, hi = max(0, 2 * reach - s0 - 1) // 2 * 2, min(taps - 1, 2 * reach + p.cz - 1 - s0) // 2 * 2 + 1
            got = jnp.dot(
                wb[8 * lo : 8 * hi + 8], r2_ref[:, s0 * nx : (s0 + 2) * nx], preferred_element_type=F32
            )
            for half in range(2):
                s = s0 + half
                for a in range(lo, min(hi, taps - 1) + 1):
                    z = s + a - 2 * reach
                    if 0 <= z < p.cz:
                        at_a = 8 * (a - lo)
                        part = got[at_a : at_a + 8, half * nx : (half + 1) * nx]
                        term[z] = part if z not in term else term[z] + part
        for z in range(p.cz):
            out_ref[z, pl.ds(pl.multiple_of(bl * 8, 8), 8), :] = term[z]
        return carry

    lax.fori_loop(0, p.blocks, block, 0)


def spread(p, pairs, ids, blurred, table, arrived):
    ins = [pairs, ids, blurred, table, arrived]
    return pl.pallas_call(
        functools.partial(spread_kernel, p),
        out_shape=jax.ShapeDtypeStruct((p.cz, p.ly, p.nx), F32),
        in_specs=[SM, SM] + [VM] * (len(ins) - 2),
        out_specs=VM,
        scratch_shapes=[
            pltpu.SMEM((p.blocks * p.views_here + 1,), jnp.int32),
            pltpu.VMEM((p.views_here, p.ez, 16, p.nx), F32),
            pltpu.VMEM((p.views_here * 128, p.ez * p.nx), BF16),
        ],
        name="spread", compiler_params=pltpu.CompilerParams(vmem_limit_bytes=6 << 20),
    )(*ins)


def on_device(estimate, view_tiles, tile_pairs, kernel_table, kernel_ids):
    p = Plan(estimate, view_tiles, kernel_table)
    b, g, _ = ranks()
    pairs = tile_pairs.reshape(-1)
    ids = kernel_ids.reshape(-1)
    first_block = g * p.row_blocks + b * p.blocks
    own_blocks = first_block + jnp.arange(p.blocks, dtype=jnp.int32)
    count = jnp.sum((tile_pairs[None, :, 0] == own_blocks[:, None]).astype(F32), axis=1)

    kern = kernel_table.reshape(p.views_here * p.sets_here, p.taps, p.taps * p.taps)
    kern = jnp.pad(kern, ((0, 0), (0, 1), (0, 128 - p.taps * p.taps)))
    if not p.fast:
        kern = kern.reshape(p.views_here, p.sets_here * 8, 128)
        kern = lax.all_gather(kern, ("blk", "gz"), axis=1, tiled=True)
    kern = kern.reshape(-1, 128)

    pieces, gathered = halos(p, *first_sends(p, estimate), kern)
    kern = gathered if p.fast else kern
    packed = pack(p, pairs, view_tiles)
    arrived = [packed[0]] + [None] * (p.n_blk - 1)
    for k in p.send_order:
        arrived[k] = lax.ppermute(packed[k], "blk", [(i, i ^ k) for i in range(p.n_blk)])
    blurred, table = blur(p, ids, pieces, kern, True)
    arrived = jnp.concatenate(arrived)
    current = estimate
    for iteration in range(ITERS):
        last = iteration == ITERS - 1
        mine = spread(p, pairs, ids, blurred, table, arrived)
        other = lax.ppermute(mine, "view", [(0, 1), (1, 0)])
        out = update(p, count, current, mine, other, last)
        current = out[0]
        if not last:
            pieces, _ = halos(p, *out[1:])
            blurred = blur(p, ids, pieces, kern, False)[0]
    return current


def solution(mesh):
    in_specs = (
        P(("group", "gz"), "blk", None),
        P(("group", "blk", "gz", "view"), None, None, None),
        P("group", None),
        P("view", ("group", "blk", "gz"), None, None, None),
        P("group", None),
    )
    out_specs = P(("group", "gz"), "blk", None)
    return jax.shard_map(
        on_device, mesh=mesh, in_specs=in_specs, out_specs=out_specs, check_vma=False
    )
```

time: 81.8 us -> 59.8 us (0.73)
  the two profiles are of different devices: /device:TPU:11 before, /device:TPU:0 now
where the time goes in v2:
time: 59.8 us; the launch traced here: 59.6 us
  starting transfers between devices  20.3 us (34%)
  waiting for transfers between devices  17.6 us (29%)
  Pallas kernels  16.6 us (28%)
  local copies, waits for them, and re-layouts  4.67 us (8%)
    pallas_call x2, Pallas kernels, blur(): pl.pallas_call(functools.partial(blur_kernel, p), out_shape=[blurred, tab...  7.39 us
    ppermute x1, waiting for transfers between devices, halos(): lax.ppermute(jnp.concatenate([sb.reshape(nz, p.nx), kern]), 'blk', odd)  7.14 us
    ppermute x2, starting transfers between devices, halos(): ra, rb = (lax.ppermute(sa, 'blk', pair), lax.ppermute(sb, 'blk', odd))  7.01 us
    pallas_call x2, Pallas kernels, spread(): pl.pallas_call(functools.partial(spread_kernel, p), out_shape=jax.ShapeDt...  6.53 us
    ppermute x3, starting transfers between devices, on_device(): lax.ppermute(packed[k], 'blk', [(i, i ^ k) for i in range(p.n_blk)])  4.45 us
    ppermute x1, starting transfers between devices, halos(): lax.ppermute(jnp.concatenate([sa.reshape(nz, p.nx), kern]), 'blk', pair)  3.12 us
    ppermute x1, waiting for transfers between devices, halos(): lax.ppermute(jnp.concatenate([out[0].reshape(ne, p.nx), kern]), 'gz', swap)  2.89 us
    ppermute x1, waiting for transfers between devices, halos(): below = above = lax.ppermute(out[0], 'gz', swap)  2.87 us
  transfers between devices with their start and end apart: 11, of which 6 were waited for; matrix products, arithmetic and copies ran while one was open for 3% of the time, Pallas kernels for 8%

profile of v2, /device:TPU:0, one launch (start us, length us, event | category | flops | bytes accessed | tf_op | source)
XLA Modules:
  0.0 59.6 jit_solution(4932503002462564961)
XLA Ops:
  0.0 0.0 copy-start.3
  0.0 0.9 %reshape.38 = bf16[3,7,49]{2,1,0:T(8,128)(2,1)S(1)} reshape(bf16[3,1,7,7,7]{4,3,2,1,0:T(8,128)(2,1)} %param.8) | data formatting | bytes 4116 | tf_op jit(solution)/shard_map/reshape | solution.py:405
  0.9 0.0 copy-start
  0.9 0.9 %copy-done = f32[8,32,128]{2,1,0:T(8,128)S(1)} copy-done((f32[8,32,128]{2,1,0:T(8,128)S(1)}, f32[8,32,128]{2,1,0:T(8,128)}, u32[]{:S(2)}) %copy-start) | copy-done | bytes 131096
  1.9 3.1 %collective-permute-start = (bf16[88,128]{1,0:T(8,128)(2,1)S(1)}, bf16[88,128]{1,0:T(8,128)(2,1)S(1)}, u32[]{:S(2)}, u32[]{:S(2)}) collective-permute-start(bf16[88,128]{1,0:T(8,128)(2,1)S(1)} %pad_maximum_fusion.3), channel_id=1, source_target_pairs={{0,4},{4,0},{8,12},{12,8},{1,5},{5,1},{9,13},{13,9},{2,6},{6,2},{1... | collective-permute-start | bytes 67592 | tf_op jit(solution)/shard_map/ppermute | solution.py:173
  5.0 0.8 %copy.8 = s32[96,2]{1,0:T(8,128)S(1)} copy(s32[96,2]{0,1:T(2,128)} %param.7) | data formatting | bytes 1536 | tf_op args[2]
  5.8 0.1 reshape.35.pairs_ref
  5.9 0.0 copy-start.2
  5.9 1.0 %copy-done.2 = bf16[6,14,14,128]{3,2,1,0:T(8,128)(2,1)S(1)} copy-done((bf16[6,14,14,128]{3,2,1,0:T(8,128)(2,1)S(1)}, bf16[6,14,14,128]{3,2,1,0:T(8,128)(2,1)}, u32[]{:S(2)}) %copy-start.2) | copy-done | bytes 301080
  6.9 0.8 %pack.1 = (bf16[3,196,128]{2,1,0:T(8,128)(2,1)S(1)}, bf16[3,196,128]{2,1,0:T(8,128)(2,1)S(1)}, bf16[3,196,128]{2,1,0:T(8,128)(2,1)S(1)}, bf16[3,196,128]{2,1,0:T(8,128)(2,1)S(1)}) custom-call(s32[192]{0:T(256)S(1)} %reshape.35.pairs_ref, bf16[6,14,14,128]{3,2,1,0:T(8,128)(2,1)S(1)} %copy-done.2), custom_call_target="tpu_custom_call" | custom-call | tf_op jit(solution)/shard_map/pack/pallas_call | solution.py:78
  7.7 0.1 collective-permute-start.3
  7.8 3.0 %collective-permute-start.4 = (bf16[3,196,128]{2,1,0:T(8,128)(2,1)S(1)}, bf16[3,196,128]{2,1,0:T(8,128)(2,1)S(1)}, u32[]{:S(2)}, u32[]{:S(2)}) collective-permute-start(bf16[3,196,128]{2,1,0:T(8,128)(2,1)S(1)} %get-tuple-element.25), channel_id=1, source_target_pairs={{0,8},{4,12},{8,0},{12,4},{1,9},{5,13},{9,1},{13,5},{2,10},{6,14},... | collective-permute-start | bytes 451592 | tf_op jit(solution)/shard_map/ppermute | solution.py:417
  10.8 1.3 %collective-permute-start.5 = (bf16[3,196,128]{2,1,0:T(8,128)(2,1)S(1)}, bf16[3,196,128]{2,1,0:T(8,128)(2,1)S(1)}, u32[]{:S(2)}, u32[]{:S(2)}) collective-permute-start(bf16[3,196,128]{2,1,0:T(8,128)(2,1)S(1)} %get-tuple-element.26), channel_id=1, source_target_pairs={{0,12},{4,8},{8,4},{12,0},{1,13},{5,9},{9,5},{13,1},{2,14},{6,10},... | collective-permute-start | bytes 451592 | tf_op jit(solution)/shard_map/ppermute | solution.py:417
  12.2 0.7 %slice_bitcast_fusion.2 = s32[96]{0:T(128)S(1)} fusion(s32[96,2]{0,1:T(2,128)} %param.7), kind=kLoop, calls=%fused_computation.13 | loop fusion | bytes 768 | tf_op jit(solution)/shard_map/eq | solution.py:403
  12.8 0.0 collective-permute-done
  12.8 2.5 %collective-permute-start.1 = (bf16[112,128]{1,0:T(8,128)(2,1)S(1)}, bf16[112,128]{1,0:T(8,128)(2,1)S(1)}, u32[]{:S(2)}, u32[]{:S(2)}) collective-permute-start(bf16[112,128]{1,0:T(8,128)(2,1)S(1)} %pad_maximum_fusion.2), channel_id=1, source_target_pairs={{0,12},{4,8},{8,4},{12,0},{1,13},{5,9},{9,5},{13,1},{2,14},{6,10},... | collective-permute-start | bytes 86024 | tf_op jit(solution)/shard_map/ppermute | solution.py:175
  15.4 7.1 %collective-permute-done.1 = bf16[112,128]{1,0:T(8,128)(2,1)S(1)} collective-permute-done((bf16[112,128]{1,0:T(8,128)(2,1)S(1)}, bf16[112,128]{1,0:T(8,128)(2,1)S(1)}, u32[]{:S(2)}, u32[]{:S(2)}) %collective-permute-start.1) | collective-permute-done | bytes 28704 | tf_op jit(solution)/shard_map/ppermute | solution.py:175
  22.6 1.6 %collective-permute-start.2 = (bf16[384,128]{1,0:T(8,128)(2,1)S(1)}, bf16[384,128]{1,0:T(8,128)(2,1)S(1)}, u32[]{:S(2)}, u32[]{:S(2)}) collective-permute-start(bf16[384,128]{1,0:T(8,128)(2,1)S(1)} %pad_maximum_fusion), channel_id=1, source_target_pairs={{0,2},{2,0},{1,3},{3,1},{4,6},{6,4},{5,7},{7,5},{8,10},{10,8},{9,1... | collective-permute-start | bytes 294920 | tf_op jit(solution)/shard_map/ppermute | solution.py:190
  24.2 0.0 copy-done.3
  24.2 0.1 copy.9
  24.3 0.1 reshape.36.ids_ref
  24.4 2.9 %collective-permute-done.2 = bf16[384,128]{1,0:T(8,128)(2,1)S(1)} collective-permute-done((bf16[384,128]{1,0:T(8,128)(2,1)S(1)}, bf16[384,128]{1,0:T(8,128)(2,1)S(1)}, u32[]{:S(2)}, u32[]{:S(2)}) %collective-permute-start.2) | collective-permute-done | bytes 98336 | tf_op jit(solution)/shard_map/ppermute | solution.py:190
  27.3 3.7 %blur.2 = (f32[12,14,16,128]{3,2,1,0:T(8,128)S(1)}, f32[192,128]{1,0:T(8,128)S(1)}) custom-call(s32[192]{0:T(256)S(1)} %reshape.36.ids_ref, bf16[8,32,128]{2,1,0:T(8,128)(2,1)S(1)} %get-tuple-element.18.own_ref, bf16[8,8,128]{2,1,0:T(8,128)(2,1)S(1)} %slice_bitcast_fusion.1.ra_ref, bf16[8,8,128]{2,1,0:T(8,128)(2,1)S(1)} %slice_bitcast_fusion.rb_ref, ...), custom_call_target="tpu_custom_call" | custom-call | tf_op jit(solution)/shard_map/blur/pallas_call | solution.py:292
  31.0 0.0 collective-permute-done.3
  31.0 0.0 copy-start.1
  31.1 0.0 collective-permute-done.4
  31.1 0.0 collective-permute-done.5
  31.1 3.3 %spread.2.mine_ref = f32[8,32,128]{2,1,0:T(8,128)S(1)} custom-call(s32[192]{0:T(256)S(1)} %reshape.35.pairs_ref, s32[192]{0:T(256)S(1)} %reshape.36.ids_ref, f32[12,14,16,128]{3,2,1,0:T(8,128)S(1)} %get-tuple-element.21.blur_ref, f32[192,128]{1,0:T(8,128)S(1)} %get-tuple-element.22.kb_ref, bf16[12,196,128]{2,1,0:T(8,128)(2,1)S(1)} %constant_dynamic-update-slice_fusion.tiles_ref), custom_call_target="tpu_custom_call" | custom-call | tf_op jit(solution)/shard_map/spread/pallas_call | solution.py:382
  34.4 0.1 collective-permute-start.6
  34.5 0.2 convert_reduce_fusion.count_ref
  34.7 1.1 %collective-permute-done.6.other_ref = f32[8,32,128]{2,1,0:T(8,128)S(1)} collective-permute-done((f32[8,32,128]{2,1,0:T(8,128)S(1)}, f32[8,32,128]{2,1,0:T(8,128)S(1)}, u32[]{:S(2)}, u32[]{:S(2)}) %collective-permute-start.6) | collective-permute-done | bytes 131104 | tf_op jit(solution)/shard_map/ppermute | solution.py:424
  35.8 0.0 copy-done.1
  35.8 0.6 update.2
  36.4 3.6 %collective-permute-start.7 = (bf16[8,8,128]{2,1,0:T(8,128)(2,1)S(1)}, bf16[8,8,128]{2,1,0:T(8,128)(2,1)S(1)}, u32[]{:S(2)}, u32[]{:S(2)}) collective-permute-start(bf16[8,8,128]{2,1,0:T(8,128)(2,1)S(1)} %get-tuple-element.29), channel_id=1, source_target_pairs={{0,4},{4,0},{8,12},{12,8},{1,5},{5,1},{9,13},{13,9},{2,6},{6,2},{1... | collective-permute-start | bytes 49160 | tf_op jit(solution)/shard_map/ppermute | solution.py:178
  40.0 3.4 %collective-permute-start.8 = (bf16[8,8,128]{2,1,0:T(8,128)(2,1)S(1)}, bf16[8,8,128]{2,1,0:T(8,128)(2,1)S(1)}, u32[]{:S(2)}, u32[]{:S(2)}) collective-permute-start(bf16[8,8,128]{2,1,0:T(8,128)(2,1)S(1)} %get-tuple-element.30), channel_id=1, source_target_pairs={{0,12},{4,8},{8,4},{12,0},{1,13},{5,9},{9,5},{13,1},{2,14},{6,10},... | collective-permute-start | bytes 49160 | tf_op jit(solution)/shard_map/ppermute | solution.py:178
  43.4 0.0 collective-permute-done.7.ra_ref
  43.4 2.2 %collective-permute-done.8.rb_ref = bf16[8,8,128]{2,1,0:T(8,128)(2,1)S(1)} collective-permute-done((bf16[8,8,128]{2,1,0:T(8,128)(2,1)S(1)}, bf16[8,8,128]{2,1,0:T(8,128)(2,1)S(1)}, u32[]{:S(2)}, u32[]{:S(2)}) %collective-permute-start.8) | collective-permute-done | bytes 16416 | tf_op jit(solution)/shard_map/ppermute | solution.py:178
  45.6 1.5 %collective-permute-start.9 = (bf16[6,48,128]{2,1,0:T(8,128)(2,1)S(1)}, bf16[6,48,128]{2,1,0:T(8,128)(2,1)S(1)}, u32[]{:S(2)}, u32[]{:S(2)}) collective-permute-start(bf16[6,48,128]{2,1,0:T(8,128)(2,1)S(1)} %edges.3), channel_id=1, source_target_pairs={{0,2},{2,0},{1,3},{3,1},{4,6},{6,4},{5,7},{7,5},{8,10},{10,8},{9,1... | collective-permute-start | bytes 221192 | tf_op jit(solution)/shard_map/ppermute | solution.py:194
  47.1 2.9 %collective-permute-done.9.below_ref.above_ref = bf16[6,48,128]{2,1,0:T(8,128)(2,1)S(1)} collective-permute-done((bf16[6,48,128]{2,1,0:T(8,128)(2,1)S(1)}, bf16[6,48,128]{2,1,0:T(8,128)(2,1)S(1)}, u32[]{:S(2)}, u32[]{:S(2)}) %collective-permute-start.9) | collective-permute-done | bytes 73760 | tf_op jit(solution)/shard_map/ppermute | solution.py:194
  50.0 3.7 %blur.3.blur_ref = f32[12,14,16,128]{3,2,1,0:T(8,128)S(1)} custom-call(s32[192]{0:T(256)S(1)} %reshape.36.ids_ref, bf16[8,32,128]{2,1,0:T(8,128)(2,1)S(1)} %get-tuple-element.28.own_ref, bf16[8,8,128]{2,1,0:T(8,128)(2,1)S(1)} %collective-permute-done.7.ra_ref, bf16[8,8,128]{2,1,0:T(8,128)(2,1)S(1)} %collective-permute-done.8.rb_ref, ...), custom_call_target="tpu_custom_call" | custom-call | tf_op jit(solution)/shard_map/blur/pallas_call | solution.py:292
  53.7 3.3 %spread.3.mine_ref = f32[8,32,128]{2,1,0:T(8,128)S(1)} custom-call(s32[192]{0:T(256)S(1)} %reshape.35.pairs_ref, s32[192]{0:T(256)S(1)} %reshape.36.ids_ref, f32[12,14,16,128]{3,2,1,0:T(8,128)S(1)} %blur.3.blur_ref, f32[192,128]{1,0:T(8,128)S(1)} %get-tuple-element.22.kb_ref, bf16[12,196,128]{2,1,0:T(8,128)(2,1)S(1)} %constant_dynamic-update-slice_fusion.tiles_ref), custom_call_target="tpu_custom_call" | custom-call | tf_op jit(solution)/shard_map/spread/pallas_call | solution.py:382
  56.9 0.1 collective-permute-start.10
  57.0 1.3 %collective-permute-done.10.other_ref = f32[8,32,128]{2,1,0:T(8,128)S(1)} collective-permute-done((f32[8,32,128]{2,1,0:T(8,128)S(1)}, f32[8,32,128]{2,1,0:T(8,128)S(1)}, u32[]{:S(2)}, u32[]{:S(2)}) %collective-permute-start.10) | collective-permute-done | bytes 131104 | tf_op jit(solution)/shard_map/ppermute | solution.py:424
  58.3 1.2 %update.3 = f32[8,32,128]{2,1,0:T(8,128)} custom-call(f32[4]{0:T(128)S(1)} %convert_reduce_fusion.count_ref, f32[8,32,128]{2,1,0:T(8,128)S(1)} %get-tuple-element.27.est_ref, f32[8,32,128]{2,1,0:T(8,128)S(1)} %spread.3.mine_ref, f32[8,32,128]{2,1,0:T(8,128)S(1)} %collective-permute-done.10.other_ref), custom_call_target="tpu_custom_call" | custom-call | tf_op jit(solution)/shard_map/update/pallas_call | solution.py:135
  (19 shorter events, 0.2 us)
Async XLA Ops:
  0.0 24.2 %copy-start.3 = (s32[32,6]{0,1:T(8,128)S(1)}, s32[32,6]{0,1:T(8,128)}, u32[]{:S(2)}) copy-start(s32[32,6]{0,1:T(8,128)} %param.9) | copy-start | bytes 2308
  0.9 0.9 %copy-start = (f32[8,32,128]{2,1,0:T(8,128)S(1)}, f32[8,32,128]{2,1,0:T(8,128)}, u32[]{:S(2)}) copy-start(f32[8,32,128]{2,1,0:T(8,128)} %est_ref.3) | copy-start | bytes 393220
  1.9 11.0 %collective-permute-start = (bf16[88,128]{1,0:T(8,128)(2,1)S(1)}, bf16[88,128]{1,0:T(8,128)(2,1)S(1)}, u32[]{:S(2)}, u32[]{:S(2)}) collective-permute-start(bf16[88,128]{1,0:T(8,128)(2,1)S(1)} %pad_maximum_fusion.3), channel_id=1, source_target_pairs={{0,4},{4,0},{8,12},{12,8},{1,5},{5,1},{9,13},{13,9},{2,6},{6,2},{1... | collective-permute-start | bytes 67592 | tf_op jit(solution)/shard_map/ppermute | solution.py:173
  5.9 1.0 %copy-start.2 = (bf16[6,14,14,128]{3,2,1,0:T(8,128)(2,1)S(1)}, bf16[6,14,14,128]{3,2,1,0:T(8,128)(2,1)}, u32[]{:S(2)}) copy-start(bf16[6,14,14,128]{3,2,1,0:T(8,128)(2,1)} %tiles_ref.1) | copy-start | bytes 903172
  7.7 23.3 %collective-permute-start.3 = (bf16[3,196,128]{2,1,0:T(8,128)(2,1)S(1)}, bf16[3,196,128]{2,1,0:T(8,128)(2,1)S(1)}, u32[]{:S(2)}, u32[]{:S(2)}) collective-permute-start(bf16[3,196,128]{2,1,0:T(8,128)(2,1)S(1)} %get-tuple-element.24), channel_id=1, source_target_pairs={{0,4},{4,0},{8,12},{12,8},{1,5},{5,1},{9,13},{13,9},{2,6},{6,2},{1... | collective-permute-start | bytes 451592 | tf_op jit(solution)/shard_map/ppermute | solution.py:417
  7.8 23.3 %collective-permute-start.4 = (bf16[3,196,128]{2,1,0:T(8,128)(2,1)S(1)}, bf16[3,196,128]{2,1,0:T(8,128)(2,1)S(1)}, u32[]{:S(2)}, u32[]{:S(2)}) collective-permute-start(bf16[3,196,128]{2,1,0:T(8,128)(2,1)S(1)} %get-tuple-element.25), channel_id=1, source_target_pairs={{0,8},{4,12},{8,0},{12,4},{1,9},{5,13},{9,1},{13,5},{2,10},{6,14},... | collective-permute-start | bytes 451592 | tf_op jit(solution)/shard_map/ppermute | solution.py:417
  10.8 20.3 %collective-permute-start.5 = (bf16[3,196,128]{2,1,0:T(8,128)(2,1)S(1)}, bf16[3,196,128]{2,1,0:T(8,128)(2,1)S(1)}, u32[]{:S(2)}, u32[]{:S(2)}) collective-permute-start(bf16[3,196,128]{2,1,0:T(8,128)(2,1)S(1)} %get-tuple-element.26), channel_id=1, source_target_pairs={{0,12},{4,8},{8,4},{12,0},{1,13},{5,9},{9,5},{13,1},{2,14},{6,10},... | collective-permute-start | bytes 451592 | tf_op jit(solution)/shard_map/ppermute | solution.py:417
  12.8 9.7 %collective-permute-start.1 = (bf16[112,128]{1,0:T(8,128)(2,1)S(1)}, bf16[112,128]{1,0:T(8,128)(2,1)S(1)}, u32[]{:S(2)}, u32[]{:S(2)}) collective-permute-start(bf16[112,128]{1,0:T(8,128)(2,1)S(1)} %pad_maximum_fusion.2), channel_id=1, source_target_pairs={{0,12},{4,8},{8,4},{12,0},{1,13},{5,9},{9,5},{13,1},{2,14},{6,10},... | collective-permute-start | bytes 86024 | tf_op jit(solution)/shard_map/ppermute | solution.py:175
  22.6 4.7 %collective-permute-start.2 = (bf16[384,128]{1,0:T(8,128)(2,1)S(1)}, bf16[384,128]{1,0:T(8,128)(2,1)S(1)}, u32[]{:S(2)}, u32[]{:S(2)}) collective-permute-start(bf16[384,128]{1,0:T(8,128)(2,1)S(1)} %pad_maximum_fusion), channel_id=1, source_target_pairs={{0,2},{2,0},{1,3},{3,1},{4,6},{6,4},{5,7},{7,5},{8,10},{10,8},{9,1... | collective-permute-start | bytes 294920 | tf_op jit(solution)/shard_map/ppermute | solution.py:190
  31.0 4.8 %copy-start.1 = (f32[8,32,128]{2,1,0:T(8,128)S(1)}, f32[8,32,128]{2,1,0:T(8,128)}, u32[]{:S(2)}) copy-start(f32[8,32,128]{2,1,0:T(8,128)} %est_ref.3) | copy-start | bytes 393220
  34.4 1.4 %collective-permute-start.6 = (f32[8,32,128]{2,1,0:T(8,128)S(1)}, f32[8,32,128]{2,1,0:T(8,128)S(1)}, u32[]{:S(2)}, u32[]{:S(2)}) collective-permute-start(f32[8,32,128]{2,1,0:T(8,128)S(1)} %spread.2.mine_ref), channel_id=1, source_target_pairs={{0,1},{1,0},{2,3},{3,2},{4,5},{5,4},{6,7},{7,6},{8,9},{9,8},{10,11... | collective-permute-start | bytes 393224 | tf_op jit(solution)/shard_map/ppermute | solution.py:424
  36.4 7.0 %collective-permute-start.7 = (bf16[8,8,128]{2,1,0:T(8,128)(2,1)S(1)}, bf16[8,8,128]{2,1,0:T(8,128)(2,1)S(1)}, u32[]{:S(2)}, u32[]{:S(2)}) collective-permute-start(bf16[8,8,128]{2,1,0:T(8,128)(2,1)S(1)} %get-tuple-element.29), channel_id=1, source_target_pairs={{0,4},{4,0},{8,12},{12,8},{1,5},{5,1},{9,13},{13,9},{2,6},{6,2},{1... | collective-permute-start | bytes 49160 | tf_op jit(solution)/shard_map/ppermute | solution.py:178
  40.0 5.5 %collective-permute-start.8 = (bf16[8,8,128]{2,1,0:T(8,128)(2,1)S(1)}, bf16[8,8,128]{2,1,0:T(8,128)(2,1)S(1)}, u32[]{:S(2)}, u32[]{:S(2)}) collective-permute-start(bf16[8,8,128]{2,1,0:T(8,128)(2,1)S(1)} %get-tuple-element.30), channel_id=1, source_target_pairs={{0,12},{4,8},{8,4},{12,0},{1,13},{5,9},{9,5},{13,1},{2,14},{6,10},... | collective-permute-start | bytes 49160 | tf_op jit(solution)/shard_map/ppermute | solution.py:178
  45.6 4.4 %collective-permute-start.9 = (bf16[6,48,128]{2,1,0:T(8,128)(2,1)S(1)}, bf16[6,48,128]{2,1,0:T(8,128)(2,1)S(1)}, u32[]{:S(2)}, u32[]{:S(2)}) collective-permute-start(bf16[6,48,128]{2,1,0:T(8,128)(2,1)S(1)} %edges.3), channel_id=1, source_target_pairs={{0,2},{2,0},{1,3},{3,1},{4,6},{6,4},{5,7},{7,5},{8,10},{10,8},{9,1... | collective-permute-start | bytes 221192 | tf_op jit(solution)/shard_map/ppermute | solution.py:194
  56.9 1.4 %collective-permute-start.10 = (f32[8,32,128]{2,1,0:T(8,128)S(1)}, f32[8,32,128]{2,1,0:T(8,128)S(1)}, u32[]{:S(2)}, u32[]{:S(2)}) collective-permute-start(f32[8,32,128]{2,1,0:T(8,128)S(1)} %spread.3.mine_ref), channel_id=1, source_target_pairs={{0,1},{1,0},{2,3},{3,2},{4,5},{5,4},{6,7},{7,6},{8,9},{9,8},{10,11... | collective-permute-start | bytes 393224 | tf_op jit(solution)/shard_map/ppermute | solution.py:424

commit v3 on v2

--- a/solution.py
+++ b/solution.py
@@ -29,7 +29,6 @@
         self.n_blk = lax.axis_size("blk")
         self.n_gz = lax.axis_size("gz")
         self.n_view = lax.axis_size("view")
-        self.views = self.views_here * self.n_view
         self.row_blocks = self.blocks * self.n_blk
         self.slots = -(-self.views_here * self.blocks // self.n_blk)
         self.slots = min(self.slots, self.tiles)
@@ -56,32 +55,7 @@
     n = plane.shape[-1]
     rolled = pltpu.roll(plane, (-d) % n, 1)
     ok = (lane < n - d) if d > 0 else (lane >= -d)
-    return jnp.where(ok, rolled, 0.0)
-
-
-def pack_kernel(p, pairs_ref, tiles_ref, *outs):
-    b, g, v = ranks()
-    first = ((b * p.n_gz + g) * p.n_view + v) * p.tiles
-    homes = [(pairs_ref[2 * (first + j)] % p.row_blocks) // p.blocks for j in range(p.tiles)]
-    for j in range(p.tiles):
-        rank = sum([(homes[i] == homes[j]).astype(jnp.int32) for i in range(j)], jnp.int32(0))
-        k = homes[j] ^ b
-        for kk in range(p.n_blk):
-
-            @pl.when(k == kk)
-            def _():
-                for s in range(p.ez):
-                    outs[kk][rank, s * p.ey : (s + 1) * p.ey, :] = tiles_ref[j, s]
-
-
-def pack(p, pairs, tiles):
-    return pl.pallas_call(
-        functools.partial(pack_kernel, p),
-        out_shape=[jax.ShapeDtypeStruct((p.slots, p.ez * p.ey, p.nx), tiles.dtype)] * p.n_blk,
-        in_specs=[SM, VM],
-        out_specs=[VM] * p.n_blk,
-        name="pack", compiler_params=pltpu.CompilerParams(vmem_limit_bytes=4 << 20),
-    )(pairs, tiles)
+    return jnp.where(ok, rolled, jnp.zeros_like(rolled))
 
 
 def sends_of(p, b, x, own_ref, sa_ref, sb_ref):
@@ -95,9 +69,71 @@
         sb_ref[z] = jnp.where(even, lo, hi).astype(BF16)
 
 
-def first_kernel(p, est_ref, own_ref, sa_ref, sb_ref):
-    b, _, _ = ranks()
+def first_kernel(p, pairs_hbm, est_hbm, tiles_hbm, table_hbm, *refs):
+    own_ref, sa_ref, sb_ref, kern_ref, count_ref, *packed = refs[: 5 + p.n_blk]
+    pairs_ref, blocks_ref, est_ref, tiles_ref, table_ref, sems = refs[5 + p.n_blk :]
+    moves = [(est_hbm, est_ref), (table_hbm, table_ref), (pairs_hbm, pairs_ref), (pairs_hbm, blocks_ref), (tiles_hbm, tiles_ref)]
+    copies = [pltpu.make_async_copy(i, j, sems.at[n]) for n, (i, j) in enumerate(moves)]
+    for copy in copies:
+        copy.start()
+    b, g, v = ranks()
+    copies[0].wait()
     sends_of(p, b, [est_ref[z] for z in range(p.cz)], own_ref, sa_ref, sb_ref)
+    copies[1].wait()
+    kern_ref[...] = jnp.zeros(kern_ref.shape, BF16)
+    if p.sets_here == 1:
+        for i in range(p.views_here):
+            cube = table_ref[i, 0].astype(F32)
+            rows = jnp.concatenate([cube[:, c, :] for c in range(p.taps)], axis=1)
+            rows = jnp.concatenate([rows, jnp.zeros((p.taps, 128 - p.taps * p.taps), F32)], axis=1)
+            rows = jnp.concatenate([rows, jnp.zeros((8 - p.taps, 128), F32)], axis=0)
+            kern_ref[8 * i : 8 * i + 8, :] = rows.astype(BF16)
+
+    copies[2].wait()
+    copies[3].wait()
+    for k in range(p.blocks):
+        same = blocks_ref[0:1, :] == g * p.row_blocks + b * p.blocks + k
+        count = jnp.sum(jnp.where(same, 1.0, 0.0), axis=1, keepdims=True)
+        count_ref[8 * k : 8 * k + 8, :] = jnp.broadcast_to(count, (8, p.nx))
+    copies[4].wait()
+    first = ((b * p.n_gz + g) * p.n_view + v) * p.tiles
+    homes = [lax.rem(pairs_ref[0, first + j], p.row_blocks) // p.blocks for j in range(p.tiles)]
+    for j in range(p.tiles):
+        rank = sum([(homes[i] == homes[j]).astype(jnp.int32) for i in range(j)], jnp.int32(0))
+        for k in range(p.n_blk):
+
+            @pl.when(homes[j] ^ b == k)
+            def _():
+                for s in range(p.ez):
+                    packed[k][rank, s * p.ey : (s + 1) * p.ey, :] = tiles_ref[j, s]
+
+
+def slots_kernel(p, pairs_ref, after_ref, slot_ref):
+    b, g, v = ranks()
+    for i in range(p.blocks * p.views_here):
+        slot_ref[i] = -1
+
+    def from_source(k, carry):
+        first = (((b ^ k) * p.n_gz + g) * p.n_view + v) * p.tiles
+        rank = jnp.int32(0)
+        for j in range(p.tiles):
+            place = lax.rem(pairs_ref[0, first + j], p.row_blocks)
+            mine = place // p.blocks == b
+            at = lax.rem(place, p.blocks) * p.views_here + pairs_ref[1, first + j] - v * p.views_here
+            slot_ref[jnp.where(mine, at, p.blocks * p.views_here)] = k * p.slots + rank
+            rank = rank + mine.astype(jnp.int32)
+        return carry
+
+    lax.fori_loop(0, p.n_blk, from_source, 0)
+
+
+def slots_of(p, pairs, after):
+    return pl.pallas_call(
+        functools.partial(slots_kernel, p),
+        out_shape=jax.ShapeDtypeStruct((p.blocks * p.views_here + 1,), jnp.int32),
+        in_specs=[SM, pl.BlockSpec(memory_space=pl.ANY)], out_specs=SM, name="slots",
+        compiler_params=pltpu.CompilerParams(vmem_limit_bytes=1 << 20),
+    )(pairs, after)
 
 
 def update_kernel(p, count_ref, est_ref, mine_ref, other_ref, new_ref, own_ref=None, sa_ref=None, sb_ref=None):
@@ -108,7 +144,7 @@
         for k in range(p.blocks):
             at = slice(k * 8, k * 8 + 8)
             total = mine_ref[z, at, :] + other_ref[z, at, :]
-            rows.append(est_ref[z, at, :] * total / count_ref[k])
+            rows.append(est_ref[z, at, :] * total / count_ref[at, :])
         x.append(jnp.concatenate(rows, axis=0))
         new_ref[z] = x[z]
     if own_ref is not None:
@@ -123,17 +159,28 @@
     ]
 
 
-def first_sends(p, est):
+def first_sends(p, pairs, est, tiles, table):
+    shapes = sends_shape(p) + [
+        jax.ShapeDtypeStruct((8 * p.views_here, 128), BF16),
+        jax.ShapeDtypeStruct((8 * p.blocks, p.nx), F32),
+    ]
+    shapes += [jax.ShapeDtypeStruct((p.slots, p.ez * p.ey, p.nx), tiles.dtype)] * p.n_blk
     return pl.pallas_call(
-        functools.partial(first_kernel, p), out_shape=sends_shape(p), in_specs=[VM],
-        out_specs=[VM] * 3, name="first", compiler_params=pltpu.CompilerParams(vmem_limit_bytes=4 << 20),
-    )(est)
+        functools.partial(first_kernel, p), out_shape=shapes,
+        in_specs=[pl.BlockSpec(memory_space=pltpu.HBM)] * 4,
+        out_specs=[VM] * len(shapes), name="first",
+        scratch_shapes=[
+            pltpu.SMEM(pairs.shape, pairs.dtype), pltpu.VMEM(pairs.shape, pairs.dtype), pltpu.VMEM(est.shape, est.dtype),
+            pltpu.VMEM(tiles.shape, tiles.dtype), pltpu.VMEM(table.shape, table.dtype), pltpu.SemaphoreType.DMA((5,)),
+        ],
+        compiler_params=pltpu.CompilerParams(vmem_limit_bytes=4 << 20),
+    )(*[pltpu.with_memory_space_constraint(x, pltpu.HBM) for x in (pairs, est, tiles, table)])
 
 
 def update(p, count, est, mine, other, last):
     shapes = [jax.ShapeDtypeStruct(est.shape, F32)] + ([] if last else sends_shape(p))
     return pl.pallas_call(
-        functools.partial(update_kernel, p), out_shape=shapes, in_specs=[SM, VM, VM, VM],
+        functools.partial(update_kernel, p), out_shape=shapes, in_specs=[VM] * 4,
         out_specs=[VM] * len(shapes), name="update", compiler_params=pltpu.CompilerParams(vmem_limit_bytes=4 << 20),
     )(count, est, mine, other)
 
@@ -170,10 +217,11 @@
     nz = p.cz * 8
     carry = kern is not None and p.fast
     if carry:
-        got = lax.ppermute(jnp.concatenate([sa.reshape(nz, p.nx), kern]), "blk", pair)
-        ra, kern = got[:nz].reshape(sa.shape), jnp.concatenate([kern, got[nz:]])
-        got = lax.ppermute(jnp.concatenate([sb.reshape(nz, p.nx), kern]), "blk", odd)
-        rb, kern = got[:nz].reshape(sb.shape), jnp.concatenate([kern, got[nz:]])
+        a = lax.ppermute(jnp.concatenate([sa.reshape(nz, p.nx), kern]), "blk", pair)
+        b = lax.ppermute(jnp.concatenate([sb.reshape(nz, p.nx), kern]), "blk", odd)
+        c = lax.ppermute(kern, "blk", [(i, i ^ 2) for i in range(p.n_blk)])
+        ra, rb = a[:nz].reshape(sa.shape), b[:nz].reshape(sb.shape)
+        kern = jnp.concatenate([kern, a[nz:], b[nz:], c])
     else:
         ra, rb = lax.ppermute(sa, "blk", pair), lax.ppermute(sb, "blk", odd)
     two = p.n_gz == 2
@@ -210,10 +258,10 @@
     if first:
         row = lax.broadcasted_iota(jnp.int32, (128, 128), 0)
         col = lax.broadcasted_iota(jnp.int32, (128, 128), 1)
-        select = (
-            (taps - 1 - row // taps == col % 16) & (taps - 1 - row % taps == col // 16) & (row < taps * taps)
-        ).astype(BF16)
-        kb_ref[...] = jnp.dot(kern_ref[...], select, preferred_element_type=F32)
+        for e in range(taps):
+            select = (row // taps == taps - 1 - col % 16) & (row % taps == taps - 1 - e)
+            select = (select & (row < taps * taps)).astype(BF16)
+            kb_ref[e] = jnp.dot(kern_ref[...], select, preferred_element_type=F32)
 
     b, g, _ = ranks()
     even = b % 2 == 0
@@ -237,7 +285,7 @@
                 at = slice(8 * bl, 8 * bl + yw)
                 high = moved[e + 1][at] if e + 1 < taps else jnp.zeros((p.depth - e * yw - yw, nx), F32)
                 both = jnp.concatenate([moved[e][at], high], axis=0).astype(BF16)
-                xs_ref[bl, e * yw : e * yw + both.shape[0], z * nx : (z + 1) * nx] = both
+                xs_ref[bl, z, e * yw : e * yw + both.shape[0], :] = both
 
     def block(bl, carry):
         wf = [[] for _ in range(taps)]
@@ -252,9 +300,8 @@
         for pair in range(p.zz // 2):
             z0 = pair * 2
             lo, hi = max(0, z0 - p.ez + 1), min(taps - 1, z0 + 1)
-            got = jnp.dot(
-                wf[m * lo : m * (hi + 1)], xs_ref[bl, :, z0 * nx : (z0 + 2) * nx], preferred_element_type=F32
-            )
+            planes = jnp.concatenate([xs_ref[bl, z0], xs_ref[bl, z0 + 1]], axis=1)
+            got = jnp.dot(wf[m * lo : m * (hi + 1)], planes, preferred_element_type=F32)
             for half in range(2):
                 z = z0 + half
                 for a in range(lo, hi + 1):
@@ -269,13 +316,14 @@
                         out_ref[bl * p.views_here + view, s] = done[16 * view : 16 * view + 16]
         return carry
 
-    lax.fori_loop(0, p.blocks, block, 0)
+    for bl in range(p.blocks):
+        block(bl, 0)
 
 
 def kernel_rows(p, ids_ref, bl, view):
     b, g, v = ranks()
     number = g * p.row_blocks + b * p.blocks + bl
-    kid = ids_ref[number * p.views + v * p.views_here + view]
+    kid = ids_ref[v * p.views_here + view, number]
     if p.fast:
         x = (kid // p.n_gz) ^ b
         at = jnp.where(lax.rem(kid, p.n_gz) == g, 0, p.n_blk) + (x ^ (x >> 1))
@@ -287,7 +335,7 @@
 
 def blur(p, ids, pieces, kern, first):
     blurred = jax.ShapeDtypeStruct((p.blocks * p.views_here, p.ez, 16, p.nx), F32)
-    table = jax.ShapeDtypeStruct((kern.shape[0], 128), F32)
+    table = jax.ShapeDtypeStruct((p.taps, kern.shape[0], 128), F32)
     ins = [ids, *pieces, kern]
     return pl.pallas_call(
         functools.partial(blur_kernel, p),
@@ -295,99 +343,81 @@
         in_specs=[SM] + [VM] * (len(ins) - 1),
         out_specs=[VM] * (2 if first else 1),
         scratch_shapes=[
-            pltpu.VMEM((p.blocks, p.depth, p.zz * p.nx), BF16),
+            pltpu.VMEM((p.blocks, p.zz, p.depth, p.nx), BF16),
             pltpu.VMEM((kern.shape[0], 256), F32),
         ],
         name="blur", compiler_params=pltpu.CompilerParams(vmem_limit_bytes=10 << 20),
     )(*ins)
 
 
-def spread_kernel(p, pairs_ref, ids_ref, blur_ref, kb_ref, tiles_ref, out_ref, slot_ref, r_ref, r2_ref):
-    b, g, v = ranks()
+def spread_kernel(p, slot_ref, ids_ref, blur_ref, kb_ref, tiles_ref, out_ref, r_ref):
+    b, g, _ = ranks()
     taps, reach, nx, views = p.taps, p.reach, p.nx, p.views_here
-    r_ref[...] = jnp.zeros(r_ref.shape, F32)
-    for view in range(views):
-        r2_ref[view * 128 + taps * 16 : (view + 1) * 128, :] = jnp.zeros((128 - taps * 16, r2_ref.shape[1]), BF16)
     has_below, has_above = g > 0, g < p.n_gz - 1
     z_low = jnp.where(has_below, 0, reach)
     z_high = jnp.where(has_above, p.ez, p.ez - reach)
-    u_row = lax.broadcasted_iota(jnp.int32, (p.ey, nx), 0)
-    lane16 = lax.broadcasted_iota(jnp.int32, (16, nx), 1)
-
-    for i in range(p.blocks * views):
-        slot_ref[i] = -1
-
-    def from_source(k, carry):
-        first = (((b ^ k) * p.n_gz + g) * p.n_view + v) * p.tiles
-        rank = jnp.int32(0)
-        for j in range(p.tiles):
-            place = lax.rem(pairs_ref[2 * (first + j)], p.row_blocks)
-            mine = place // p.blocks == b
-            at = lax.rem(place, p.blocks) * views + pairs_ref[2 * (first + j) + 1] - v * views
-            at = jnp.where(mine, at, p.blocks * views)
-            slot_ref[at] = k * p.slots + rank
-            rank = rank + mine.astype(jnp.int32)
-        return carry
-
-    lax.fori_loop(0, p.n_blk, from_source, 0)
+    u_row = lax.broadcasted_iota(jnp.int32, (16, nx), 0)
+    lane8 = lax.broadcasted_iota(jnp.int32, (8, nx), 1)
 
     def block(bl, carry):
-        wb = []
-        for view in range(views):
-            base = kb_ref[kernel_rows(p, ids_ref, bl, view), :]
-            rows = [
-                pltpu.roll(jnp.broadcast_to(base[a : a + 1], (8, 128)), 0, 1, stride=1, stride_axis=0)
-                for a in range(taps)
-            ]
-            wb.append(jnp.concatenate(rows + [jnp.zeros((8, 128), F32)], axis=0))
-        wb = jnp.concatenate(wb, axis=1).astype(BF16)
+        wb = [[] for _ in range(taps)]
+        at = [kernel_rows(p, ids_ref, bl, view) for view in range(views)]
+        for e in range(taps):
+            base = kb_ref[e, at[-1], :]
+            for view in range(views - 2, -1, -1):
+                base = jnp.where(lane8 < 16 * view + 16, kb_ref[e, at[view], :], base)
+            for a in range(taps):
+                wide = jnp.broadcast_to(base[a : a + 1], (8, 128))
+                wb[a].append(pltpu.roll(wide, 0, 1, stride=1, stride_axis=0))
+        wb = jnp.concatenate([x for y in wb for x in y], axis=0).astype(BF16)[:, : 16 * views]
+        m = 8 * taps
         y_first = (b * p.blocks + bl) * p.by - reach
-        y_ok = (u_row + y_first >= 0) & (u_row + y_first < p.row_blocks * p.by)
+        y_ok = (u_row < p.ey) & (u_row + y_first >= 0) & (u_row + y_first < p.row_blocks * p.by)
         slots = [slot_ref[bl * views + view] for view in range(views)]
-        term = {}
+        acc = {}
         for pair in range(p.ez // 2):
             s0 = pair * 2
             for s in (s0, s0 + 1):
                 z_ok = (s >= z_low) & (s < z_high)
                 for view in range(views):
                     tile = tiles_ref[jnp.maximum(slots[view], 0), s * p.ey : (s + 1) * p.ey, :].astype(F32)
-                    ratio = tile / blur_ref[bl * views + view, s, : p.ey, :]
+                    tile = jnp.concatenate([tile, jnp.zeros((16 - p.ey, nx), F32)], axis=0)
+                    ratio = tile / blur_ref[bl * views + view, s]
                     keep = y_ok & (z_ok & (slots[view] >= 0))
-                    r_ref[view, s, : p.ey, :] = jnp.where(keep, ratio, 0.0)
-                    full = r_ref[view, s]
-                    for e in range(taps):
-                        at = view * 128 + e * 16
-                        r2_ref[at : at + 16, s * nx : (s + 1) * nx] = lane_shift(full, e, reach, lane16).astype(BF16)
-            lo, hi = max(0, 2 * reach - s0 - 1) // 2 * 2, min(taps - 1, 2 * reach + p.cz - 1 - s0) // 2 * 2 + 1
-            got = jnp.dot(
-                wb[8 * lo : 8 * hi + 8], r2_ref[:, s0 * nx : (s0 + 2) * nx], preferred_element_type=F32
-            )
+                    r_ref[bl, s, 16 * view : 16 * view + 16, :] = jnp.where(keep, ratio, 0.0).astype(BF16)
+            lo, hi = max(0, 2 * reach - s0 - 1) // 2 * 2, min(taps - 1, 2 * reach + p.cz - 1 - s0)
+            planes = jnp.concatenate([r_ref[bl, s0], r_ref[bl, s0 + 1]], axis=1)
+            got = jnp.dot(wb[m * lo : m * (hi + 1)], planes, preferred_element_type=F32)
             for half in range(2):
                 s = s0 + half
-                for a in range(lo, min(hi, taps - 1) + 1):
+                for a in range(lo, hi + 1):
                     z = s + a - 2 * reach
                     if 0 <= z < p.cz:
-                        at_a = 8 * (a - lo)
-                        part = got[at_a : at_a + 8, half * nx : (half + 1) * nx]
-                        term[z] = part if z not in term else term[z] + part
-        for z in range(p.cz):
-            out_ref[z, pl.ds(pl.multiple_of(bl * 8, 8), 8), :] = term[z]
+                        part = got[m * (a - lo) : m * (a - lo + 1), half * nx : (half + 1) * nx]
+                        acc[z] = part if z not in acc else acc[z] + part
+                z = s - 2 * reach
+                if 0 <= z < p.cz:
+                    done = acc.pop(z)
+                    term = done[8 * reach : 8 * reach + 8]
+                    for e in range(taps):
+                        if e != reach:
+                            term = term + lane_shift(done[8 * e : 8 * e + 8], e, reach, lane8)
+                    out_ref[z, bl * 8 : bl * 8 + 8, :] = term
         return carry
 
-    lax.fori_loop(0, p.blocks, block, 0)
-
-
-def spread(p, pairs, ids, blurred, table, arrived):
-    ins = [pairs, ids, blurred, table, arrived]
+    for bl in range(p.blocks):
+        block(bl, 0)
+
+
+def spread(p, slots, ids, blurred, table, arrived):
+    ins = [slots, ids, blurred, table, arrived]
     return pl.pallas_call(
         functools.partial(spread_kernel, p),
         out_shape=jax.ShapeDtypeStruct((p.cz, p.ly, p.nx), F32),
         in_specs=[SM, SM] + [VM] * (len(ins) - 2),
         out_specs=VM,
         scratch_shapes=[
-            pltpu.SMEM((p.blocks * p.views_here + 1,), jnp.int32),
-            pltpu.VMEM((p.views_here, p.ez, 16, p.nx), F32),
-            pltpu.VMEM((p.views_here * 128, p.ez * p.nx), BF16),
+            pltpu.VMEM((p.blocks, p.ez, p.views_here * 16, p.nx), BF16),
         ],
         name="spread", compiler_params=pltpu.CompilerParams(vmem_limit_bytes=6 << 20),
     )(*ins)
@@ -395,32 +425,26 @@
 
 def on_device(estimate, view_tiles, tile_pairs, kernel_table, kernel_ids):
     p = Plan(estimate, view_tiles, kernel_table)
-    b, g, _ = ranks()
-    pairs = tile_pairs.reshape(-1)
-    ids = kernel_ids.reshape(-1)
-    first_block = g * p.row_blocks + b * p.blocks
-    own_blocks = first_block + jnp.arange(p.blocks, dtype=jnp.int32)
-    count = jnp.sum((tile_pairs[None, :, 0] == own_blocks[:, None]).astype(F32), axis=1)
-
-    kern = kernel_table.reshape(p.views_here * p.sets_here, p.taps, p.taps * p.taps)
-    kern = jnp.pad(kern, ((0, 0), (0, 1), (0, 128 - p.taps * p.taps)))
-    if not p.fast:
+    pairs, ids = tile_pairs.T, kernel_ids.T
+    own, sa, sb, kern, count, *packed = first_sends(p, pairs, estimate, view_tiles, kernel_table)
+    pieces, gathered = halos(p, own, sa, sb, kern)
+    if p.fast:
+        kern = gathered
+    else:
+        kern = kernel_table.reshape(p.views_here, p.sets_here, p.taps, p.taps * p.taps)
+        kern = jnp.pad(kern, ((0, 0), (0, 0), (0, 1), (0, 128 - p.taps * p.taps)))
         kern = kern.reshape(p.views_here, p.sets_here * 8, 128)
-        kern = lax.all_gather(kern, ("blk", "gz"), axis=1, tiled=True)
-    kern = kern.reshape(-1, 128)
-
-    pieces, gathered = halos(p, *first_sends(p, estimate), kern)
-    kern = gathered if p.fast else kern
-    packed = pack(p, pairs, view_tiles)
+        kern = lax.all_gather(kern, ("blk", "gz"), axis=1, tiled=True).reshape(-1, 128)
     arrived = [packed[0]] + [None] * (p.n_blk - 1)
     for k in p.send_order:
         arrived[k] = lax.ppermute(packed[k], "blk", [(i, i ^ k) for i in range(p.n_blk)])
     blurred, table = blur(p, ids, pieces, kern, True)
     arrived = jnp.concatenate(arrived)
+    slots = slots_of(p, pairs, table)
     current = estimate
     for iteration in range(ITERS):
         last = iteration == ITERS - 1
-        mine = spread(p, pairs, ids, blurred, table, arrived)
+        mine = spread(p, slots, ids, blurred, table, arrived)
         other = lax.ppermute(mine, "view", [(0, 1), (1, 0)])
         out = update(p, count, current, mine, other, last)
         current = out[0]

time: 59.8 us -> 45.2 us (0.76)
  local copies, waits for them, and re-layouts: 4.67 us -> 0.16 us
  waiting for transfers between devices: 17.6 us -> 13.4 us
  Pallas kernels: 16.6 us -> 12.7 us
  starting transfers between devices: 20.3 us -> 18.6 us
    ppermute x2 -> x3, waiting for transfers between devices: 7.14 us -> 0.01 us  [the longest x1 0.01 us: halos(): b = lax.ppermute(jnp.concatenate([sb.reshape(nz, p.nx), kern]), 'blk', odd)]
    unnamed x13 -> x14, local copies, waits for them, and re-layouts: 2.81 us -> 0.12 us
    pallas_call x2, Pallas kernels: 6.53 us -> 4.05 us  [spread(): pl.pallas_call(functools.partial(spread_kernel, p), out_shape=jax.ShapeDt...]
    ppermute x2, starting transfers between devices: 7.01 us -> 4.62 us  [halos(): ra, rb = (lax.ppermute(sa, 'blk', pair), lax.ppermute(sb, 'blk', odd))]
    pallas_call x2, Pallas kernels: 7.39 us -> 5.08 us  [blur(): pl.pallas_call(functools.partial(blur_kernel, p), out_shape=[blurred, tab...]
    pallas_call x2, Pallas kernels: 0.83 us -> 2.84 us  [the longest x1 1.44 us: slots_of(): pl.pallas_call(functools.partial(slots_kernel, p), out_shape=jax.ShapeDty...]
    ppermute x3, waiting for transfers between devices: 0.01 us -> 1.59 us  [on_device(): lax.ppermute(packed[k], 'blk', [(i, i ^ k) for i in range(p.n_blk)])]
    reshape x6 -> x2, local copies, waits for them, and re-layouts: 1.14 us -> 0.01 us  [halos(): ra, rb = (a[:nz].reshape(sa.shape), b[:nz].reshape(sb.shape))]
  transfers between devices with their start and end apart: 11 -> 12, of which waited for: 6 -> 6; matrix products, arithmetic and copies ran while one was open for 3% -> 0% of each run, Pallas kernels for 8% -> 9%
where the time goes in v3:
time: 45.2 us; the launch traced here: 45.1 us
  starting transfers between devices  18.6 us (41%)
  waiting for transfers between devices  13.4 us (30%)
  Pallas kernels  12.7 us (28%)
    ppermute x1, starting transfers between devices, halos(): b = lax.ppermute(jnp.concatenate([sb.reshape(nz, p.nx), kern]), 'blk', odd)  5.13 us
    pallas_call x2, Pallas kernels, blur(): pl.pallas_call(functools.partial(blur_kernel, p), out_shape=[blurred, tab...  5.08 us
    ppermute x3, starting transfers between devices, on_device(): lax.ppermute(packed[k], 'blk', [(i, i ^ k) for i in range(p.n_blk)])  4.96 us
    ppermute x2, starting transfers between devices, halos(): ra, rb = (lax.ppermute(sa, 'blk', pair), lax.ppermute(sb, 'blk', odd))  4.62 us
    pallas_call x2, Pallas kernels, spread(): pl.pallas_call(functools.partial(spread_kernel, p), out_shape=jax.ShapeDt...  4.05 us
    ppermute x2, waiting for transfers between devices, halos(): ra, rb = (lax.ppermute(sa, 'blk', pair), lax.ppermute(sb, 'blk', odd))  3.16 us
    ppermute x1, waiting for transfers between devices, halos(): lax.ppermute(jnp.concatenate([out[0].reshape(ne, p.nx), kern]), 'gz', swap)  3.1 us
    ppermute x1, waiting for transfers between devices, halos(): below = above = lax.ppermute(out[0], 'gz', swap)  2.85 us
  transfers between devices with their start and end apart: 12, of which 6 were waited for; matrix products, arithmetic and copies ran while one was open for 0% of the time, Pallas kernels for 9%

profile of v3, /device:TPU:0, one launch (start us, length us, event | category | flops | bytes accessed | tf_op | source)
XLA Modules:
  0.0 45.1 jit_solution(1260640111978298679)
XLA Ops:
  0.0 0.0 copy-start.2
  0.0 0.0 copy-start.1
  0.0 1.4 %first.1 = (bf16[8,32,128]{2,1,0:T(8,128)(2,1)S(1)}, bf16[8,8,128]{2,1,0:T(8,128)(2,1)S(1)}, bf16[8,8,128]{2,1,0:T(8,128)(2,1)S(1)}, bf16[24,128]{1,0:T(8,128)(2...) custom-call(s32[2,96]{1,0:T(2,128)} %bitcast.19, ...), custom_call_target="tpu_custom_call" | custom-call | tf_op jit(solution)/shard_map/first/pallas_call | solution.py:168
  1.4 5.1 %collective-permute-start.1 = (bf16[88,128]{1,0:T(8,128)(2,1)S(1)}, bf16[88,128]{1,0:T(8,128)(2,1)S(1)}, u32[]{:S(2)}, u32[]{:S(2)}) collective-permute-start(bf16[88,128]{1,0:T(8,128)(2,1)S(1)} %get-tuple-element.43), channel_id=1, source_target_pairs={{0,12},{4,8},{8,4},{12,0},{1,13},{5,9},{9,5},{13,1},{2,14},{6,10},... | collective-permute-start | bytes 67592 | tf_op jit(solution)/shard_map/ppermute | solution.py:221
  6.6 0.0 collective-permute-start.2
  6.6 0.6 %collective-permute-start = (bf16[88,128]{1,0:T(8,128)(2,1)S(1)}, bf16[88,128]{1,0:T(8,128)(2,1)S(1)}, u32[]{:S(2)}, u32[]{:S(2)}) collective-permute-start(bf16[88,128]{1,0:T(8,128)(2,1)S(1)} %get-tuple-element.44), channel_id=1, source_target_pairs={{0,4},{4,0},{8,12},{12,8},{1,5},{5,1},{9,13},{13,9},{2,6},{6,2},{1... | collective-permute-start | bytes 67592 | tf_op jit(solution)/shard_map/ppermute | solution.py:220
  7.2 1.4 %collective-permute-start.4 = (bf16[3,196,128]{2,1,0:T(8,128)(2,1)S(1)}, bf16[3,196,128]{2,1,0:T(8,128)(2,1)S(1)}, u32[]{:S(2)}, u32[]{:S(2)}) collective-permute-start(bf16[3,196,128]{2,1,0:T(8,128)(2,1)S(1)} %get-tuple-element.28), channel_id=1, source_target_pairs={{0,4},{4,0},{8,12},{12,8},{1,5},{5,1},{9,13},{13,9},{2,6},{6,2},{1... | collective-permute-start | bytes 451592 | tf_op jit(solution)/shard_map/ppermute | solution.py:440
  8.6 2.9 %collective-permute-start.5 = (bf16[3,196,128]{2,1,0:T(8,128)(2,1)S(1)}, bf16[3,196,128]{2,1,0:T(8,128)(2,1)S(1)}, u32[]{:S(2)}, u32[]{:S(2)}) collective-permute-start(bf16[3,196,128]{2,1,0:T(8,128)(2,1)S(1)} %get-tuple-element.29), channel_id=1, source_target_pairs={{0,8},{4,12},{8,0},{12,4},{1,9},{5,13},{9,1},{13,5},{2,10},{6,14},... | collective-permute-start | bytes 451592 | tf_op jit(solution)/shard_map/ppermute | solution.py:440
  11.5 0.0 collective-permute-done.1
  11.5 0.6 %collective-permute-start.6 = (bf16[3,196,128]{2,1,0:T(8,128)(2,1)S(1)}, bf16[3,196,128]{2,1,0:T(8,128)(2,1)S(1)}, u32[]{:S(2)}, u32[]{:S(2)}) collective-permute-start(bf16[3,196,128]{2,1,0:T(8,128)(2,1)S(1)} %get-tuple-element.30), channel_id=1, source_target_pairs={{0,12},{4,8},{8,4},{12,0},{1,13},{5,9},{9,5},{13,1},{2,14},{6,10},... | collective-permute-start | bytes 451592 | tf_op jit(solution)/shard_map/ppermute | solution.py:440
  12.2 0.0 collective-permute-done
  12.3 0.0 collective-permute-done.2
  12.3 1.6 %collective-permute-start.3 = (bf16[384,128]{1,0:T(8,128)(2,1)S(1)}, bf16[384,128]{1,0:T(8,128)(2,1)S(1)}, u32[]{:S(2)}, u32[]{:S(2)}) collective-permute-start(bf16[384,128]{1,0:T(8,128)(2,1)S(1)} %get-tuple-element.40), channel_id=1, source_target_pairs={{0,2},{2,0},{1,3},{3,1},{4,6},{6,4},{5,7},{7,5},{8,10},{10,8},{9,1... | collective-permute-start | bytes 294920 | tf_op jit(solution)/shard_map/ppermute | solution.py:238
  13.9 3.1 %collective-permute-done.3 = bf16[384,128]{1,0:T(8,128)(2,1)S(1)} collective-permute-done((bf16[384,128]{1,0:T(8,128)(2,1)S(1)}, bf16[384,128]{1,0:T(8,128)(2,1)S(1)}, u32[]{:S(2)}, u32[]{:S(2)}) %collective-permute-start.3) | collective-permute-done | bytes 98336 | tf_op jit(solution)/shard_map/ppermute | solution.py:238
  17.0 0.0 copy-done.1
  17.0 2.6 %blur.2 = (f32[12,14,16,128]{3,2,1,0:T(8,128)S(1)}, f32[7,192,128]{2,1,0:T(8,128)S(1)}) custom-call(s32[6,32]{1,0:T(8,128)S(1)} %bitcast.13, bf16[8,32,128]{2,1,0:T(8,128)(2,1)S(1)} %get-tuple-element.21.own_ref, bf16[8,8,128]{2,1,0:T(8,128)(2,1)S(1)} %slice_bitcast_fusion.1.ra_ref, bf16[8,8,128]{2,1,0:T(8,128)(2,1)S(1)} %slice_bitcast_fusion.rb_ref, ...), custom_call_target="tpu_custom_call" | custom-call | tf_op jit(solution)/shard_map/blur/pallas_call | solution.py:340
  19.6 0.0 copy-done.2
  19.6 1.4 %slots.1.slot_ref = s32[13]{0:T(128)S(1)} custom-call(s32[2,96]{1,0:T(2,128)S(1)} %bitcast.20, f32[7,192,128]{2,1,0:T(8,128)S(1)} %get-tuple-element.25.after_ref.kb_ref), custom_call_target="tpu_custom_call" | custom-call | tf_op jit(solution)/shard_map/slots/pallas_call | solution.py:131
  21.0 0.0 collective-permute-done.4
  21.1 1.6 %collective-permute-done.5 = bf16[3,196,128]{2,1,0:T(8,128)(2,1)S(1)} collective-permute-done((bf16[3,196,128]{2,1,0:T(8,128)(2,1)S(1)}, bf16[3,196,128]{2,1,0:T(8,128)(2,1)S(1)}, u32[]{:S(2)}, u32[]{:S(2)}) %collective-permute-start.5) | collective-permute-done | bytes 150560 | tf_op jit(solution)/shard_map/ppermute | solution.py:440
  22.7 0.0 collective-permute-done.6
  22.7 0.0 copy-start
  22.7 2.0 %spread.2.mine_ref = f32[8,32,128]{2,1,0:T(8,128)S(1)} custom-call(s32[13]{0:T(128)S(1)} %slots.1.slot_ref, s32[6,32]{1,0:T(8,128)S(1)} %bitcast.14, f32[12,14,16,128]{3,2,1,0:T(8,128)S(1)} %get-tuple-element.26.blur_ref, f32[7,192,128]{2,1,0:T(8,128)S(1)} %get-tuple-element.25.after_ref.kb_ref, ...), custom_call_target="tpu_custom_call" | custom-call | tf_op jit(solution)/shard_map/spread/pallas_call | solution.py:414
  24.8 0.1 collective-permute-start.7
  24.8 1.3 %collective-permute-done.7.other_ref = f32[8,32,128]{2,1,0:T(8,128)S(1)} collective-permute-done((f32[8,32,128]{2,1,0:T(8,128)S(1)}, f32[8,32,128]{2,1,0:T(8,128)S(1)}, u32[]{:S(2)}, u32[]{:S(2)}) %collective-permute-start.7) | collective-permute-done | bytes 131104 | tf_op jit(solution)/shard_map/ppermute | solution.py:448
  26.2 0.0 copy-done
  26.2 2.2 %collective-permute-start.8 = (bf16[8,8,128]{2,1,0:T(8,128)(2,1)S(1)}, bf16[8,8,128]{2,1,0:T(8,128)(2,1)S(1)}, u32[]{:S(2)}, u32[]{:S(2)}) collective-permute-start(bf16[8,8,128]{2,1,0:T(8,128)(2,1)S(1)} %get-tuple-element.33), channel_id=1, source_target_pairs={{0,4},{4,0},{8,12},{12,8},{1,5},{5,1},{9,13},{13,9},{2,6},{6,2},{1... | collective-permute-start | bytes 49160 | tf_op jit(solution)/shard_map/ppermute | solution.py:226
  28.5 2.4 %collective-permute-start.9 = (bf16[8,8,128]{2,1,0:T(8,128)(2,1)S(1)}, bf16[8,8,128]{2,1,0:T(8,128)(2,1)S(1)}, u32[]{:S(2)}, u32[]{:S(2)}) collective-permute-start(bf16[8,8,128]{2,1,0:T(8,128)(2,1)S(1)} %get-tuple-element.34), channel_id=1, source_target_pairs={{0,12},{4,8},{8,4},{12,0},{1,13},{5,9},{9,5},{13,1},{2,14},{6,10},... | collective-permute-start | bytes 49160 | tf_op jit(solution)/shard_map/ppermute | solution.py:226
  30.8 0.0 collective-permute-done.8.ra_ref
  30.8 3.2 %collective-permute-done.9.rb_ref = bf16[8,8,128]{2,1,0:T(8,128)(2,1)S(1)} collective-permute-done((bf16[8,8,128]{2,1,0:T(8,128)(2,1)S(1)}, bf16[8,8,128]{2,1,0:T(8,128)(2,1)S(1)}, u32[]{:S(2)}, u32[]{:S(2)}) %collective-permute-start.9) | collective-permute-done | bytes 16416 | tf_op jit(solution)/shard_map/ppermute | solution.py:226
  34.0 1.6 %collective-permute-start.10 = (bf16[6,48,128]{2,1,0:T(8,128)(2,1)S(1)}, bf16[6,48,128]{2,1,0:T(8,128)(2,1)S(1)}, u32[]{:S(2)}, u32[]{:S(2)}) collective-permute-start(bf16[6,48,128]{2,1,0:T(8,128)(2,1)S(1)} %edges.3), channel_id=1, source_target_pairs={{0,2},{2,0},{1,3},{3,1},{4,6},{6,4},{5,7},{7,5},{8,10},{10,8},{9,1... | collective-permute-start | bytes 221192 | tf_op jit(solution)/shard_map/ppermute | solution.py:242
  35.6 2.9 %collective-permute-done.10.below_ref.above_ref = bf16[6,48,128]{2,1,0:T(8,128)(2,1)S(1)} collective-permute-done((bf16[6,48,128]{2,1,0:T(8,128)(2,1)S(1)}, bf16[6,48,128]{2,1,0:T(8,128)(2,1)S(1)}, u32[]{:S(2)}, u32[]{:S(2)}) %collective-permute-start.10) | collective-permute-done | bytes 73760 | tf_op jit(solution)/shard_map/ppermute | solution.py:242
  38.4 2.5 %blur.3.blur_ref = f32[12,14,16,128]{3,2,1,0:T(8,128)S(1)} custom-call(s32[6,32]{1,0:T(8,128)S(1)} %bitcast.15, bf16[8,32,128]{2,1,0:T(8,128)(2,1)S(1)} %get-tuple-element.32.own_ref, bf16[8,8,128]{2,1,0:T(8,128)(2,1)S(1)} %collective-permute-done.8.ra_ref, bf16[8,8,128]{2,1,0:T(8,128)(2,1)S(1)} %collective-permute-done.9.rb_ref, ...), custom_call_target="tpu_custom_call" | custom-call | tf_op jit(solution)/shard_map/blur/pallas_call | solution.py:340
  41.0 2.0 %spread.3.mine_ref = f32[8,32,128]{2,1,0:T(8,128)S(1)} custom-call(s32[13]{0:T(128)S(1)} %slots.1.slot_ref, s32[6,32]{1,0:T(8,128)S(1)} %bitcast.16, f32[12,14,16,128]{3,2,1,0:T(8,128)S(1)} %blur.3.blur_ref, f32[7,192,128]{2,1,0:T(8,128)S(1)} %get-tuple-element.25.after_ref.kb_ref, bf16[12,196,128]{2,1,0:T(8,128)(2,1)S(1)} %constant_dynamic-update-slice_fusion.10.tiles_ref), custom_call_target="tpu_custom_call" | custom-call | tf_op jit(solution)/shard_map/spread/pallas_call | solution.py:414
  43.0 0.1 collective-permute-start.11
  43.1 1.3 %collective-permute-done.11.other_ref = f32[8,32,128]{2,1,0:T(8,128)S(1)} collective-permute-done((f32[8,32,128]{2,1,0:T(8,128)S(1)}, f32[8,32,128]{2,1,0:T(8,128)S(1)}, u32[]{:S(2)}, u32[]{:S(2)}) %collective-permute-start.11) | collective-permute-done | bytes 131104 | tf_op jit(solution)/shard_map/ppermute | solution.py:448
  44.4 0.7 %update.3 = f32[8,32,128]{2,1,0:T(8,128)} custom-call(f32[32,128]{1,0:T(8,128)S(1)} %get-tuple-element.20.count_ref, f32[8,32,128]{2,1,0:T(8,128)S(1)} %get-tuple-element.31.est_ref, f32[8,32,128]{2,1,0:T(8,128)S(1)} %spread.3.mine_ref, f32[8,32,128]{2,1,0:T(8,128)S(1)} %collective-permute-done.11.other_ref), custom_call_target="tpu_custom_call" | custom-call | tf_op jit(solution)/shard_map/update/pallas_call | solution.py:182
  (17 shorter events, 0.2 us)
Async XLA Ops:
  0.0 19.6 %copy-start.2 = (s32[96,2]{0,1:T(2,128)S(1)}, s32[96,2]{0,1:T(2,128)}, u32[]{:S(2)}) copy-start(s32[96,2]{0,1:T(2,128)} %param.7) | copy-start | bytes 2308
  0.0 17.0 %copy-start.1 = (s32[32,6]{0,1:T(8,128)S(1)}, s32[32,6]{0,1:T(8,128)}, u32[]{:S(2)}) copy-start(s32[32,6]{0,1:T(8,128)} %param.9) | copy-start | bytes 2308
  1.4 10.1 %collective-permute-start.1 = (bf16[88,128]{1,0:T(8,128)(2,1)S(1)}, bf16[88,128]{1,0:T(8,128)(2,1)S(1)}, u32[]{:S(2)}, u32[]{:S(2)}) collective-permute-start(bf16[88,128]{1,0:T(8,128)(2,1)S(1)} %get-tuple-element.43), channel_id=1, source_target_pairs={{0,12},{4,8},{8,4},{12,0},{1,13},{5,9},{9,5},{13,1},{2,14},{6,10},... | collective-permute-start | bytes 67592 | tf_op jit(solution)/shard_map/ppermute | solution.py:221
  6.6 5.7 %collective-permute-start.2 = (bf16[24,128]{1,0:T(8,128)(2,1)S(1)}, bf16[24,128]{1,0:T(8,128)(2,1)S(1)}, u32[]{:S(2)}, u32[]{:S(2)}) collective-permute-start(bf16[24,128]{1,0:T(8,128)(2,1)S(1)} %get-tuple-element.23), channel_id=1, source_target_pairs={{0,8},{4,12},{8,0},{12,4},{1,9},{5,13},{9,1},{13,5},{2,10},{6,14},... | collective-permute-start | bytes 18440 | tf_op jit(solution)/shard_map/ppermute | solution.py:222
  6.6 5.6 %collective-permute-start = (bf16[88,128]{1,0:T(8,128)(2,1)S(1)}, bf16[88,128]{1,0:T(8,128)(2,1)S(1)}, u32[]{:S(2)}, u32[]{:S(2)}) collective-permute-start(bf16[88,128]{1,0:T(8,128)(2,1)S(1)} %get-tuple-element.44), channel_id=1, source_target_pairs={{0,4},{4,0},{8,12},{12,8},{1,5},{5,1},{9,13},{13,9},{2,6},{6,2},{1... | collective-permute-start | bytes 67592 | tf_op jit(solution)/shard_map/ppermute | solution.py:220
  7.2 13.8 %collective-permute-start.4 = (bf16[3,196,128]{2,1,0:T(8,128)(2,1)S(1)}, bf16[3,196,128]{2,1,0:T(8,128)(2,1)S(1)}, u32[]{:S(2)}, u32[]{:S(2)}) collective-permute-start(bf16[3,196,128]{2,1,0:T(8,128)(2,1)S(1)} %get-tuple-element.28), channel_id=1, source_target_pairs={{0,4},{4,0},{8,12},{12,8},{1,5},{5,1},{9,13},{13,9},{2,6},{6,2},{1... | collective-permute-start | bytes 451592 | tf_op jit(solution)/shard_map/ppermute | solution.py:440
  8.6 14.1 %collective-permute-start.5 = (bf16[3,196,128]{2,1,0:T(8,128)(2,1)S(1)}, bf16[3,196,128]{2,1,0:T(8,128)(2,1)S(1)}, u32[]{:S(2)}, u32[]{:S(2)}) collective-permute-start(bf16[3,196,128]{2,1,0:T(8,128)(2,1)S(1)} %get-tuple-element.29), channel_id=1, source_target_pairs={{0,8},{4,12},{8,0},{12,4},{1,9},{5,13},{9,1},{13,5},{2,10},{6,14},... | collective-permute-start | bytes 451592 | tf_op jit(solution)/shard_map/ppermute | solution.py:440
  11.5 11.2 %collective-permute-start.6 = (bf16[3,196,128]{2,1,0:T(8,128)(2,1)S(1)}, bf16[3,196,128]{2,1,0:T(8,128)(2,1)S(1)}, u32[]{:S(2)}, u32[]{:S(2)}) collective-permute-start(bf16[3,196,128]{2,1,0:T(8,128)(2,1)S(1)} %get-tuple-element.30), channel_id=1, source_target_pairs={{0,12},{4,8},{8,4},{12,0},{1,13},{5,9},{9,5},{13,1},{2,14},{6,10},... | collective-permute-start | bytes 451592 | tf_op jit(solution)/shard_map/ppermute | solution.py:440
  12.3 4.7 %collective-permute-start.3 = (bf16[384,128]{1,0:T(8,128)(2,1)S(1)}, bf16[384,128]{1,0:T(8,128)(2,1)S(1)}, u32[]{:S(2)}, u32[]{:S(2)}) collective-permute-start(bf16[384,128]{1,0:T(8,128)(2,1)S(1)} %get-tuple-element.40), channel_id=1, source_target_pairs={{0,2},{2,0},{1,3},{3,1},{4,6},{6,4},{5,7},{7,5},{8,10},{10,8},{9,1... | collective-permute-start | bytes 294920 | tf_op jit(solution)/shard_map/ppermute | solution.py:238
  22.7 3.5 %copy-start = (f32[8,32,128]{2,1,0:T(8,128)S(1)}, f32[8,32,128]{2,1,0:T(8,128)}, u32[]{:S(2)}) copy-start(f32[8,32,128]{2,1,0:T(8,128)} %est_ref.1) | copy-start | bytes 393220
  24.8 1.4 %collective-permute-start.7 = (f32[8,32,128]{2,1,0:T(8,128)S(1)}, f32[8,32,128]{2,1,0:T(8,128)S(1)}, u32[]{:S(2)}, u32[]{:S(2)}) collective-permute-start(f32[8,32,128]{2,1,0:T(8,128)S(1)} %spread.2.mine_ref), channel_id=1, source_target_pairs={{0,1},{1,0},{2,3},{3,2},{4,5},{5,4},{6,7},{7,6},{8,9},{9,8},{10,11... | collective-permute-start | bytes 393224 | tf_op jit(solution)/shard_map/ppermute | solution.py:448
  26.2 4.6 %collective-permute-start.8 = (bf16[8,8,128]{2,1,0:T(8,128)(2,1)S(1)}, bf16[8,8,128]{2,1,0:T(8,128)(2,1)S(1)}, u32[]{:S(2)}, u32[]{:S(2)}) collective-permute-start(bf16[8,8,128]{2,1,0:T(8,128)(2,1)S(1)} %get-tuple-element.33), channel_id=1, source_target_pairs={{0,4},{4,0},{8,12},{12,8},{1,5},{5,1},{9,13},{13,9},{2,6},{6,2},{1... | collective-permute-start | bytes 49160 | tf_op jit(solution)/shard_map/ppermute | solution.py:226
  28.5 5.5 %collective-permute-start.9 = (bf16[8,8,128]{2,1,0:T(8,128)(2,1)S(1)}, bf16[8,8,128]{2,1,0:T(8,128)(2,1)S(1)}, u32[]{:S(2)}, u32[]{:S(2)}) collective-permute-start(bf16[8,8,128]{2,1,0:T(8,128)(2,1)S(1)} %get-tuple-element.34), channel_id=1, source_target_pairs={{0,12},{4,8},{8,4},{12,0},{1,13},{5,9},{9,5},{13,1},{2,14},{6,10},... | collective-permute-start | bytes 49160 | tf_op jit(solution)/shard_map/ppermute | solution.py:226
  34.0 4.4 %collective-permute-start.10 = (bf16[6,48,128]{2,1,0:T(8,128)(2,1)S(1)}, bf16[6,48,128]{2,1,0:T(8,128)(2,1)S(1)}, u32[]{:S(2)}, u32[]{:S(2)}) collective-permute-start(bf16[6,48,128]{2,1,0:T(8,128)(2,1)S(1)} %edges.3), channel_id=1, source_target_pairs={{0,2},{2,0},{1,3},{3,1},{4,6},{6,4},{5,7},{7,5},{8,10},{10,8},{9,1... | collective-permute-start | bytes 221192 | tf_op jit(solution)/shard_map/ppermute | solution.py:242
  43.0 1.4 %collective-permute-start.11 = (f32[8,32,128]{2,1,0:T(8,128)S(1)}, f32[8,32,128]{2,1,0:T(8,128)S(1)}, u32[]{:S(2)}, u32[]{:S(2)}) collective-permute-start(f32[8,32,128]{2,1,0:T(8,128)S(1)} %spread.3.mine_ref), channel_id=1, source_target_pairs={{0,1},{1,0},{2,3},{3,2},{4,5},{5,4},{6,7},{7,6},{8,9},{9,8},{10,11... | collective-permute-start | bytes 393224 | tf_op jit(solution)/shard_map/ppermute | solution.py:448

commit v4 on v3

--- a/solution.py
+++ b/solution.py
@@ -37,7 +37,6 @@
         self.halo = 2 * self.reach
         assert self.by == 8 and self.cz == 8 and self.nx == 128 and self.taps == 7
         assert self.n_blk & (self.n_blk - 1) == 0 and self.n_blk > 1 and self.ez <= 16
-        self.zz = self.cz + 2 * self.halo
         self.rows = self.ly + 16
         self.yw = 24
         self.depth = (self.taps * self.yw + 15) // 16 * 16
@@ -247,9 +246,38 @@
     return (own, ra, rb, below, above), kern
 
 
-def blur_kernel(p, ids_ref, own_ref, ra_ref, rb_ref, below_ref, above_ref, kern_ref, *rest):
-    first = len(rest) == 4
-    out_ref, kb_ref, xs_ref, kf_ref = rest if first else (rest[0], None, *rest[1:])
+def put_shifts(p, xs_ref, at, plane, lane):
+    taps, yw = p.taps, p.yw
+    moved = [lane_shift(plane, e, p.reach, lane) for e in range(taps)]
+    for bl in range(p.blocks):
+        rows = slice(8 * bl, 8 * bl + yw)
+        for e in range(0, taps, 2):
+            high = moved[e + 1][rows] if e + 1 < taps else jnp.zeros((p.depth - e * yw - yw, p.nx), F32)
+            both = jnp.concatenate([moved[e][rows], high], axis=0).astype(BF16)
+            xs_ref[bl, at, e * yw : e * yw + both.shape[0], :] = both
+
+
+def put_blur(p, wf, xs_ref, bl, planes, done):
+    m, nx = 16 * p.views_here, p.nx
+    acc = {}
+    for n, z0 in enumerate(planes):
+        lo, hi = max(0, z0 - p.ez + 1), min(p.taps - 1, z0 + 1)
+        both = jnp.concatenate([xs_ref[bl, 2 * n], xs_ref[bl, 2 * n + 1]], axis=1)
+        got = jnp.dot(wf[m * lo : m * (hi + 1)], both, preferred_element_type=F32)
+        for half in range(2):
+            z = z0 + half
+            for a in range(lo, hi + 1):
+                s = z - a
+                if 0 <= s < p.ez:
+                    part = got[m * (a - lo) : m * (a - lo + 1), half * nx : (half + 1) * nx]
+                    acc[s] = part if s not in acc else acc[s] + part
+            for s in [s for s in acc if s + p.taps - 1 <= z or z == planes[-1] + 1]:
+                done(s, acc.pop(s))
+
+
+def blur_kernel(p, ids_ref, own_ref, ra_ref, rb_ref, kern_ref, *rest):
+    first = len(rest) == 5
+    out_ref, wf_ref, kb_ref, xs_ref, kf_ref = rest if first else (*rest[:2], None, *rest[2:])
     taps, nx, yw = p.taps, p.nx, p.yw
     row = lax.broadcasted_iota(jnp.int32, (128, 256), 0)
     col = lax.broadcasted_iota(jnp.int32, (128, 256), 1)
@@ -263,31 +291,17 @@
             select = (select & (row < taps * taps)).astype(BF16)
             kb_ref[e] = jnp.dot(kern_ref[...], select, preferred_element_type=F32)
 
-    b, g, _ = ranks()
+    b, _, _ = ranks()
     even = b % 2 == 0
     has_left, has_right = b > 0, b < p.n_blk - 1
-    has_below, has_above = g > 0, g < p.n_gz - 1
     lane = lax.broadcasted_iota(jnp.int32, (p.rows, nx), 1)
-    for z in range(p.zz):
-        i = z - p.halo
-        if i < 0:
-            plane = jnp.where(has_below, below_ref[z].astype(F32), 0.0)
-        elif i >= p.cz:
-            plane = jnp.where(has_above, above_ref[i - p.cz].astype(F32), 0.0)
-        else:
-            ra, rb = ra_ref[i].astype(F32), rb_ref[i].astype(F32)
-            left = jnp.where(has_left, jnp.where(even, rb, ra), 0.0)
-            right = jnp.where(has_right, jnp.where(even, ra, rb), 0.0)
-            plane = jnp.concatenate([left, own_ref[i].astype(F32), right], axis=0)
-        moved = [lane_shift(plane, e, p.reach, lane) for e in range(taps)] + [jnp.zeros_like(plane)]
-        for bl in range(p.blocks):
-            for e in range(0, taps, 2):
-                at = slice(8 * bl, 8 * bl + yw)
-                high = moved[e + 1][at] if e + 1 < taps else jnp.zeros((p.depth - e * yw - yw, nx), F32)
-                both = jnp.concatenate([moved[e][at], high], axis=0).astype(BF16)
-                xs_ref[bl, z, e * yw : e * yw + both.shape[0], :] = both
-
-    def block(bl, carry):
+    for i in range(p.cz):
+        ra, rb = ra_ref[i].astype(F32), rb_ref[i].astype(F32)
+        left = jnp.where(has_left, jnp.where(even, rb, ra), 0.0)
+        right = jnp.where(has_right, jnp.where(even, ra, rb), 0.0)
+        put_shifts(p, xs_ref, i, jnp.concatenate([left, own_ref[i].astype(F32), right], axis=0), lane)
+
+    for bl in range(p.blocks):
         wf = [[] for _ in range(taps)]
         for view in range(p.views_here):
             base = pltpu.roll(kf_ref[kernel_rows(p, ids_ref, bl, view), :], 2, 1)
@@ -295,29 +309,32 @@
                 wide = jnp.broadcast_to(base[a : a + 1], (16, 256))
                 wf[a].append(pltpu.roll(wide, 0, 1, stride=1, stride_axis=0))
         wf = jnp.concatenate([x for y in wf for x in y], axis=0).astype(BF16)[:, : p.depth]
-        m = 16 * p.views_here
-        acc = {}
-        for pair in range(p.zz // 2):
-            z0 = pair * 2
-            lo, hi = max(0, z0 - p.ez + 1), min(taps - 1, z0 + 1)
-            planes = jnp.concatenate([xs_ref[bl, z0], xs_ref[bl, z0 + 1]], axis=1)
-            got = jnp.dot(wf[m * lo : m * (hi + 1)], planes, preferred_element_type=F32)
-            for half in range(2):
-                z = z0 + half
-                for a in range(lo, hi + 1):
-                    s = z - a
-                    if 0 <= s < p.ez:
-                        part = got[m * (a - lo) : m * (a - lo + 1), half * nx : (half + 1) * nx]
-                        acc[s] = part if s not in acc else acc[s] + part
-                s = z - taps + 1
-                if 0 <= s < p.ez:
-                    done = acc.pop(s)
+        wf_ref[bl] = wf
+
+        def done(s, total):
+            for view in range(p.views_here):
+                out_ref[bl * p.views_here + view, s] = total[16 * view : 16 * view + 16]
+
+        put_blur(p, wf, xs_ref, bl, range(p.halo, p.halo + p.cz, 2), done)
+
+
+def beside_kernel(p, below_ref, above_ref, before_ref, wf_ref, out_ref, xs_ref):
+    _, g, _ = ranks()
+    lane = lax.broadcasted_iota(jnp.int32, (p.rows, p.nx), 1)
+    for there, ref, z0 in ((g > 0, below_ref, 0), (g < p.n_gz - 1, above_ref, p.halo + p.cz)):
+
+        @pl.when(there)
+        def _():
+            for z in range(p.halo):
+                put_shifts(p, xs_ref, z, ref[z].astype(F32), lane)
+            for bl in range(p.blocks):
+
+                def done(s, total):
                     for view in range(p.views_here):
-                        out_ref[bl * p.views_here + view, s] = done[16 * view : 16 * view + 16]
-        return carry
-
-    for bl in range(p.blocks):
-        block(bl, 0)
+                        at = bl * p.views_here + view
+                        out_ref[at, s] = before_ref[at, s] + total[16 * view : 16 * view + 16]
+
+                put_blur(p, wf_ref[bl], xs_ref, bl, range(z0, z0 + p.halo, 2), done)
 
 
 def kernel_rows(p, ids_ref, bl, view):
@@ -334,20 +351,27 @@
 
 
 def blur(p, ids, pieces, kern, first):
-    blurred = jax.ShapeDtypeStruct((p.blocks * p.views_here, p.ez, 16, p.nx), F32)
+    own, ra, rb, below, above = pieces
+    partial = jax.ShapeDtypeStruct((p.blocks * p.views_here, p.ez, 16, p.nx), F32)
+    left = jax.ShapeDtypeStruct((p.blocks, 16 * p.views_here * p.taps, p.depth), BF16)
     table = jax.ShapeDtypeStruct((p.taps, kern.shape[0], 128), F32)
-    ins = [ids, *pieces, kern]
-    return pl.pallas_call(
+    shapes = [partial, left] + ([table] if first else [])
+    out = pl.pallas_call(
         functools.partial(blur_kernel, p),
-        out_shape=[blurred, table] if first else [blurred],
-        in_specs=[SM] + [VM] * (len(ins) - 1),
-        out_specs=[VM] * (2 if first else 1),
+        out_shape=shapes, in_specs=[SM] + [VM] * 4, out_specs=[VM] * len(shapes),
         scratch_shapes=[
-            pltpu.VMEM((p.blocks, p.zz, p.depth, p.nx), BF16),
+            pltpu.VMEM((p.blocks, p.cz, p.depth, p.nx), BF16),
             pltpu.VMEM((kern.shape[0], 256), F32),
         ],
         name="blur", compiler_params=pltpu.CompilerParams(vmem_limit_bytes=10 << 20),
-    )(*ins)
+    )(ids, own, ra, rb, kern)
+    whole = pl.pallas_call(
+        functools.partial(beside_kernel, p),
+        out_shape=partial, in_specs=[VM] * 4, out_specs=VM, input_output_aliases={2: 0},
+        scratch_shapes=[pltpu.VMEM((p.blocks, p.halo, p.depth, p.nx), BF16)],
+        name="beside", compiler_params=pltpu.CompilerParams(vmem_limit_bytes=10 << 20),
+    )(below, above, out[0], out[1])
+    return whole, out[2] if first else None
 
 
 def spread_kernel(p, slot_ref, ids_ref, blur_ref, kb_ref, tiles_ref, out_ref, r_ref):

time: 45.2 us -> 43.4 us (0.960)
  waiting for transfers between devices: 13.4 us -> 11.5 us
    ppermute x1, waiting for transfers between devices: 2.85 us -> 0.99 us  [halos(): below = above = lax.ppermute(out[0], 'gz', swap)]
    pallas_call x2 -> x4, Pallas kernels: 5.08 us -> 5.08 us  [the longest x2 3.74 us: blur(): pl.pallas_call(functools.partial(blur_kernel, p), out_shape=shapes, in_sp...]
  transfers between devices with their start and end apart: 12 -> 12, of which waited for: 6 -> 6; matrix products, arithmetic and copies ran while one was open for 0% -> 0% of each run, Pallas kernels for 9% -> 14%
where the time goes in v4:
time: 43.4 us; the launch traced here: 43.2 us
  starting transfers between devices  18.6 us (43%)
  Pallas kernels  12.7 us (29%)
  waiting for transfers between devices  11.5 us (26%)
    ppermute x1, starting transfers between devices, halos(): b = lax.ppermute(jnp.concatenate([sb.reshape(nz, p.nx), kern]), 'blk', odd)  5.13 us
    ppermute x3, starting transfers between devices, on_device(): lax.ppermute(packed[k], 'blk', [(i, i ^ k) for i in range(p.n_blk)])  4.96 us
    ppermute x2, starting transfers between devices, halos(): ra, rb = (lax.ppermute(sa, 'blk', pair), lax.ppermute(sb, 'blk', odd))  4.61 us
    pallas_call x2, Pallas kernels, spread(): pl.pallas_call(functools.partial(spread_kernel, p), out_shape=jax.ShapeDt...  4.05 us
    pallas_call x2, Pallas kernels, blur(): pl.pallas_call(functools.partial(blur_kernel, p), out_shape=shapes, in_sp...  3.74 us
    ppermute x2, waiting for transfers between devices, halos(): ra, rb = (lax.ppermute(sa, 'blk', pair), lax.ppermute(sb, 'blk', odd))  3.16 us
    ppermute x1, waiting for transfers between devices, halos(): lax.ppermute(jnp.concatenate([out[0].reshape(ne, p.nx), kern]), 'gz', swap)  3.1 us
    ppermute x2, waiting for transfers between devices, on_device(): other = lax.ppermute(mine, 'view', [(0, 1), (1, 0)])  2.67 us
  transfers between devices with their start and end apart: 12, of which 6 were waited for; matrix products, arithmetic and copies ran while one was open for 0% of the time, Pallas kernels for 14%

profile of v4, /device:TPU:0, one launch (start us, length us, event | category | flops | bytes accessed | tf_op | source)
XLA Modules:
  0.0 43.2 jit_solution(834831770193041944)
XLA Ops:
  0.0 0.0 copy-start.2
  0.0 0.0 copy-start.1
  0.0 1.4 %first.1 = (bf16[8,32,128]{2,1,0:T(8,128)(2,1)S(1)}, bf16[8,8,128]{2,1,0:T(8,128)(2,1)S(1)}, bf16[8,8,128]{2,1,0:T(8,128)(2,1)S(1)}, bf16[24,128]{1,0:T(8,128)(2...) custom-call(s32[2,96]{1,0:T(2,128)} %bitcast.19, ...), custom_call_target="tpu_custom_call" | custom-call | tf_op jit(solution)/shard_map/first/pallas_call | solution.py:167
  1.4 5.1 %collective-permute-start.1 = (bf16[88,128]{1,0:T(8,128)(2,1)S(1)}, bf16[88,128]{1,0:T(8,128)(2,1)S(1)}, u32[]{:S(2)}, u32[]{:S(2)}) collective-permute-start(bf16[88,128]{1,0:T(8,128)(2,1)S(1)} %get-tuple-element.49), channel_id=1, source_target_pairs={{0,12},{4,8},{8,4},{12,0},{1,13},{5,9},{9,5},{13,1},{2,14},{6,10},... | collective-permute-start | bytes 67592 | tf_op jit(solution)/shard_map/ppermute | solution.py:220
  6.6 0.0 collective-permute-start.2
  6.6 0.6 %collective-permute-start = (bf16[88,128]{1,0:T(8,128)(2,1)S(1)}, bf16[88,128]{1,0:T(8,128)(2,1)S(1)}, u32[]{:S(2)}, u32[]{:S(2)}) collective-permute-start(bf16[88,128]{1,0:T(8,128)(2,1)S(1)} %get-tuple-element.50), channel_id=1, source_target_pairs={{0,4},{4,0},{8,12},{12,8},{1,5},{5,1},{9,13},{13,9},{2,6},{6,2},{1... | collective-permute-start | bytes 67592 | tf_op jit(solution)/shard_map/ppermute | solution.py:219
  7.2 1.4 %collective-permute-start.4 = (bf16[3,196,128]{2,1,0:T(8,128)(2,1)S(1)}, bf16[3,196,128]{2,1,0:T(8,128)(2,1)S(1)}, u32[]{:S(2)}, u32[]{:S(2)}) collective-permute-start(bf16[3,196,128]{2,1,0:T(8,128)(2,1)S(1)} %get-tuple-element.32), channel_id=1, source_target_pairs={{0,4},{4,0},{8,12},{12,8},{1,5},{5,1},{9,13},{13,9},{2,6},{6,2},{1... | collective-permute-start | bytes 451592 | tf_op jit(solution)/shard_map/ppermute | solution.py:464
  8.6 2.9 %collective-permute-start.5 = (bf16[3,196,128]{2,1,0:T(8,128)(2,1)S(1)}, bf16[3,196,128]{2,1,0:T(8,128)(2,1)S(1)}, u32[]{:S(2)}, u32[]{:S(2)}) collective-permute-start(bf16[3,196,128]{2,1,0:T(8,128)(2,1)S(1)} %get-tuple-element.33), channel_id=1, source_target_pairs={{0,8},{4,12},{8,0},{12,4},{1,9},{5,13},{9,1},{13,5},{2,10},{6,14},... | collective-permute-start | bytes 451592 | tf_op jit(solution)/shard_map/ppermute | solution.py:464
  11.5 0.0 collective-permute-done.1
  11.5 0.6 %collective-permute-start.6 = (bf16[3,196,128]{2,1,0:T(8,128)(2,1)S(1)}, bf16[3,196,128]{2,1,0:T(8,128)(2,1)S(1)}, u32[]{:S(2)}, u32[]{:S(2)}) collective-permute-start(bf16[3,196,128]{2,1,0:T(8,128)(2,1)S(1)} %get-tuple-element.34), channel_id=1, source_target_pairs={{0,12},{4,8},{8,4},{12,0},{1,13},{5,9},{9,5},{13,1},{2,14},{6,10},... | collective-permute-start | bytes 451592 | tf_op jit(solution)/shard_map/ppermute | solution.py:464
  12.2 0.0 collective-permute-done
  12.3 0.0 collective-permute-done.2
  12.3 1.6 %collective-permute-start.3 = (bf16[384,128]{1,0:T(8,128)(2,1)S(1)}, bf16[384,128]{1,0:T(8,128)(2,1)S(1)}, u32[]{:S(2)}, u32[]{:S(2)}) collective-permute-start(bf16[384,128]{1,0:T(8,128)(2,1)S(1)} %get-tuple-element.45), channel_id=1, source_target_pairs={{0,2},{2,0},{1,3},{3,1},{4,6},{6,4},{5,7},{7,5},{8,10},{10,8},{9,1... | collective-permute-start | bytes 294920 | tf_op jit(solution)/shard_map/ppermute | solution.py:237
  13.9 3.1 %collective-permute-done.3 = bf16[384,128]{1,0:T(8,128)(2,1)S(1)} collective-permute-done((bf16[384,128]{1,0:T(8,128)(2,1)S(1)}, bf16[384,128]{1,0:T(8,128)(2,1)S(1)}, u32[]{:S(2)}, u32[]{:S(2)}) %collective-permute-start.3) | collective-permute-done | bytes 98336 | tf_op jit(solution)/shard_map/ppermute | solution.py:237
  17.0 0.0 copy-done.1
  17.0 1.9 %blur.2 = (f32[12,14,16,128]{3,2,1,0:T(8,128)S(1)}, bf16[4,336,176]{2,1,0:T(8,128)(2,1)S(1)}, f32[7,192,128]{2,1,0:T(8,128)S(1)}) custom-call(s32[6,32]{1,0:T(8,128)S(1)} %bitcast.13, bf16[8,32,128]{2,1,0:T(8,128)(2,1)S(1)} %get-tuple-element.24.own_ref, bf16[8,8,128]{2,1,0:T(8,128)(2,1)S(1)} %slice_bitcast_fusion.1.ra_ref, ...), custom_call_target="tpu_custom_call" | custom-call | tf_op jit(solution)/shard_map/blur/pallas_call | solution.py:359
  18.9 0.0 copy-done.2
  18.9 1.4 %slots.1.slot_ref = s32[13]{0:T(128)S(1)} custom-call(s32[2,96]{1,0:T(2,128)S(1)} %bitcast.20, f32[7,192,128]{2,1,0:T(8,128)S(1)} %get-tuple-element.28.after_ref.kb_ref), custom_call_target="tpu_custom_call" | custom-call | tf_op jit(solution)/shard_map/slots/pallas_call | solution.py:130
  20.3 0.7 %beside.2.blur_ref = f32[12,14,16,128]{3,2,1,0:T(8,128)S(1)} custom-call(bf16[6,48,128]{2,1,0:T(8,128)(2,1)S(1)} %bitcast.10, bf16[6,48,128]{2,1,0:T(8,128)(2,1)S(1)} %bitcast.11, f32[12,14,16,128]{3,2,1,0:T(8,128)S(1)} %get-tuple-element.29.before_ref, bf16[4,336,176]{2,1,0:T(8,128)(2,1)S(1)} %get-tuple-element.30.wf_ref), custom_call_target="tpu_custom_call", output_to_operand_aliasing={{}: (2, {})} | custom-call | tf_op jit(solution)/shard_map/beside/pallas_call | solution.py:368
  21.0 0.0 collective-permute-done.4
  21.1 1.6 %collective-permute-done.5 = bf16[3,196,128]{2,1,0:T(8,128)(2,1)S(1)} collective-permute-done((bf16[3,196,128]{2,1,0:T(8,128)(2,1)S(1)}, bf16[3,196,128]{2,1,0:T(8,128)(2,1)S(1)}, u32[]{:S(2)}, u32[]{:S(2)}) %collective-permute-start.5) | collective-permute-done | bytes 150560 | tf_op jit(solution)/shard_map/ppermute | solution.py:464
  22.7 0.0 collective-permute-done.6
  22.7 0.0 copy-start
  22.7 2.0 %spread.2.mine_ref = f32[8,32,128]{2,1,0:T(8,128)S(1)} custom-call(s32[13]{0:T(128)S(1)} %slots.1.slot_ref, s32[6,32]{1,0:T(8,128)S(1)} %bitcast.14, f32[12,14,16,128]{3,2,1,0:T(8,128)S(1)} %beside.2.blur_ref, f32[7,192,128]{2,1,0:T(8,128)S(1)} %get-tuple-element.28.after_ref.kb_ref, bf16[12,196,128]{2,1,0:T(8,128)(2,1)S(1)} %constant_dynamic-update-slice_fusion.10.tiles_ref), custom_call_target="tpu_custom_call" | custom-call | tf_op jit(solution)/shard_map/spread/pallas_call | solution.py:438
  24.8 0.1 collective-permute-start.7
  24.8 1.3 %collective-permute-done.7.other_ref = f32[8,32,128]{2,1,0:T(8,128)S(1)} collective-permute-done((f32[8,32,128]{2,1,0:T(8,128)S(1)}, f32[8,32,128]{2,1,0:T(8,128)S(1)}, u32[]{:S(2)}, u32[]{:S(2)}) %collective-permute-start.7) | collective-permute-done | bytes 131104 | tf_op jit(solution)/shard_map/ppermute | solution.py:472
  26.2 0.0 copy-done
  26.2 2.2 %collective-permute-start.8 = (bf16[8,8,128]{2,1,0:T(8,128)(2,1)S(1)}, bf16[8,8,128]{2,1,0:T(8,128)(2,1)S(1)}, u32[]{:S(2)}, u32[]{:S(2)}) collective-permute-start(bf16[8,8,128]{2,1,0:T(8,128)(2,1)S(1)} %get-tuple-element.37), channel_id=1, source_target_pairs={{0,4},{4,0},{8,12},{12,8},{1,5},{5,1},{9,13},{13,9},{2,6},{6,2},{1... | collective-permute-start | bytes 49160 | tf_op jit(solution)/shard_map/ppermute | solution.py:225
  28.4 2.4 %collective-permute-start.9 = (bf16[8,8,128]{2,1,0:T(8,128)(2,1)S(1)}, bf16[8,8,128]{2,1,0:T(8,128)(2,1)S(1)}, u32[]{:S(2)}, u32[]{:S(2)}) collective-permute-start(bf16[8,8,128]{2,1,0:T(8,128)(2,1)S(1)} %get-tuple-element.38), channel_id=1, source_target_pairs={{0,12},{4,8},{8,4},{12,0},{1,13},{5,9},{9,5},{13,1},{2,14},{6,10},... | collective-permute-start | bytes 49160 | tf_op jit(solution)/shard_map/ppermute | solution.py:225
  30.8 0.0 collective-permute-done.8.ra_ref
  30.8 3.2 %collective-permute-done.9.rb_ref = bf16[8,8,128]{2,1,0:T(8,128)(2,1)S(1)} collective-permute-done((bf16[8,8,128]{2,1,0:T(8,128)(2,1)S(1)}, bf16[8,8,128]{2,1,0:T(8,128)(2,1)S(1)}, u32[]{:S(2)}, u32[]{:S(2)}) %collective-permute-start.9) | collective-permute-done | bytes 16416 | tf_op jit(solution)/shard_map/ppermute | solution.py:225
  34.0 1.6 %collective-permute-start.10 = (bf16[6,48,128]{2,1,0:T(8,128)(2,1)S(1)}, bf16[6,48,128]{2,1,0:T(8,128)(2,1)S(1)}, u32[]{:S(2)}, u32[]{:S(2)}) collective-permute-start(bf16[6,48,128]{2,1,0:T(8,128)(2,1)S(1)} %edges.3), channel_id=1, source_target_pairs={{0,2},{2,0},{1,3},{3,1},{4,6},{6,4},{5,7},{7,5},{8,10},{10,8},{9,1... | collective-permute-start | bytes 221192 | tf_op jit(solution)/shard_map/ppermute | solution.py:241
  35.6 1.8 %blur.3 = (f32[12,14,16,128]{3,2,1,0:T(8,128)S(1)}, bf16[4,336,176]{2,1,0:T(8,128)(2,1)S(1)}) custom-call(s32[6,32]{1,0:T(8,128)S(1)} %bitcast.15, bf16[8,32,128]{2,1,0:T(8,128)(2,1)S(1)} %get-tuple-element.36.own_ref, bf16[8,8,128]{2,1,0:T(8,128)(2,1)S(1)} %collective-permute-done.8.ra_ref, bf16[8,8,128]{2,1,0:T(8,128)(2,1)S(1)} %collective-permute-done.9.rb_ref, ...), custom_call_target="tpu_custom_call" | custom-call | tf_op jit(solution)/shard_map/blur/pallas_call | solution.py:359
  37.4 1.0 %collective-permute-done.10.below_ref.above_ref = bf16[6,48,128]{2,1,0:T(8,128)(2,1)S(1)} collective-permute-done((bf16[6,48,128]{2,1,0:T(8,128)(2,1)S(1)}, bf16[6,48,128]{2,1,0:T(8,128)(2,1)S(1)}, u32[]{:S(2)}, u32[]{:S(2)}) %collective-permute-start.10) | collective-permute-done | bytes 73760 | tf_op jit(solution)/shard_map/ppermute | solution.py:241
  38.4 0.7 %beside.3.blur_ref = f32[12,14,16,128]{3,2,1,0:T(8,128)S(1)} custom-call(bf16[6,48,128]{2,1,0:T(8,128)(2,1)S(1)} %collective-permute-done.10.below_ref.above_ref, bf16[6,48,128]{2,1,0:T(8,128)(2,1)S(1)} %collective-permute-done.10.below_ref.above_ref, f32[12,14,16,128]{3,2,1,0:T(8,128)S(1)} %get-tuple-element.39.before_ref, ...), custom_call_target="tpu_custom_call", output_to_operand_aliasing={{}: (2, {})} | custom-call | tf_op jit(solution)/shard_map/beside/pallas_call | solution.py:368
  39.1 2.0 %spread.3.mine_ref = f32[8,32,128]{2,1,0:T(8,128)S(1)} custom-call(s32[13]{0:T(128)S(1)} %slots.1.slot_ref, s32[6,32]{1,0:T(8,128)S(1)} %bitcast.16, f32[12,14,16,128]{3,2,1,0:T(8,128)S(1)} %beside.3.blur_ref, f32[7,192,128]{2,1,0:T(8,128)S(1)} %get-tuple-element.28.after_ref.kb_ref, bf16[12,196,128]{2,1,0:T(8,128)(2,1)S(1)} %constant_dynamic-update-slice_fusion.10.tiles_ref), custom_call_target="tpu_custom_call" | custom-call | tf_op jit(solution)/shard_map/spread/pallas_call | solution.py:438
  41.1 0.1 collective-permute-start.11
  41.2 1.3 %collective-permute-done.11.other_ref = f32[8,32,128]{2,1,0:T(8,128)S(1)} collective-permute-done((f32[8,32,128]{2,1,0:T(8,128)S(1)}, f32[8,32,128]{2,1,0:T(8,128)S(1)}, u32[]{:S(2)}, u32[]{:S(2)}) %collective-permute-start.11) | collective-permute-done | bytes 131104 | tf_op jit(solution)/shard_map/ppermute | solution.py:472
  42.5 0.7 %update.3 = f32[8,32,128]{2,1,0:T(8,128)} custom-call(f32[32,128]{1,0:T(8,128)S(1)} %get-tuple-element.23.count_ref, f32[8,32,128]{2,1,0:T(8,128)S(1)} %get-tuple-element.35.est_ref, f32[8,32,128]{2,1,0:T(8,128)S(1)} %spread.3.mine_ref, f32[8,32,128]{2,1,0:T(8,128)S(1)} %collective-permute-done.11.other_ref), custom_call_target="tpu_custom_call" | custom-call | tf_op jit(solution)/shard_map/update/pallas_call | solution.py:181
  (17 shorter events, 0.2 us)
Async XLA Ops:
  0.0 18.9 %copy-start.2 = (s32[96,2]{0,1:T(2,128)S(1)}, s32[96,2]{0,1:T(2,128)}, u32[]{:S(2)}) copy-start(s32[96,2]{0,1:T(2,128)} %param.7) | copy-start | bytes 2308
  0.0 17.0 %copy-start.1 = (s32[32,6]{0,1:T(8,128)S(1)}, s32[32,6]{0,1:T(8,128)}, u32[]{:S(2)}) copy-start(s32[32,6]{0,1:T(8,128)} %param.9) | copy-start | bytes 2308
  1.4 10.1 %collective-permute-start.1 = (bf16[88,128]{1,0:T(8,128)(2,1)S(1)}, bf16[88,128]{1,0:T(8,128)(2,1)S(1)}, u32[]{:S(2)}, u32[]{:S(2)}) collective-permute-start(bf16[88,128]{1,0:T(8,128)(2,1)S(1)} %get-tuple-element.49), channel_id=1, source_target_pairs={{0,12},{4,8},{8,4},{12,0},{1,13},{5,9},{9,5},{13,1},{2,14},{6,10},... | collective-permute-start | bytes 67592 | tf_op jit(solution)/shard_map/ppermute | solution.py:220
  6.6 5.7 %collective-permute-start.2 = (bf16[24,128]{1,0:T(8,128)(2,1)S(1)}, bf16[24,128]{1,0:T(8,128)(2,1)S(1)}, u32[]{:S(2)}, u32[]{:S(2)}) collective-permute-start(bf16[24,128]{1,0:T(8,128)(2,1)S(1)} %get-tuple-element.26), channel_id=1, source_target_pairs={{0,8},{4,12},{8,0},{12,4},{1,9},{5,13},{9,1},{13,5},{2,10},{6,14},... | collective-permute-start | bytes 18440 | tf_op jit(solution)/shard_map/ppermute | solution.py:221
  6.6 5.6 %collective-permute-start = (bf16[88,128]{1,0:T(8,128)(2,1)S(1)}, bf16[88,128]{1,0:T(8,128)(2,1)S(1)}, u32[]{:S(2)}, u32[]{:S(2)}) collective-permute-start(bf16[88,128]{1,0:T(8,128)(2,1)S(1)} %get-tuple-element.50), channel_id=1, source_target_pairs={{0,4},{4,0},{8,12},{12,8},{1,5},{5,1},{9,13},{13,9},{2,6},{6,2},{1... | collective-permute-start | bytes 67592 | tf_op jit(solution)/shard_map/ppermute | solution.py:219
  7.2 13.8 %collective-permute-start.4 = (bf16[3,196,128]{2,1,0:T(8,128)(2,1)S(1)}, bf16[3,196,128]{2,1,0:T(8,128)(2,1)S(1)}, u32[]{:S(2)}, u32[]{:S(2)}) collective-permute-start(bf16[3,196,128]{2,1,0:T(8,128)(2,1)S(1)} %get-tuple-element.32), channel_id=1, source_target_pairs={{0,4},{4,0},{8,12},{12,8},{1,5},{5,1},{9,13},{13,9},{2,6},{6,2},{1... | collective-permute-start | bytes 451592 | tf_op jit(solution)/shard_map/ppermute | solution.py:464
  8.6 14.1 %collective-permute-start.5 = (bf16[3,196,128]{2,1,0:T(8,128)(2,1)S(1)}, bf16[3,196,128]{2,1,0:T(8,128)(2,1)S(1)}, u32[]{:S(2)}, u32[]{:S(2)}) collective-permute-start(bf16[3,196,128]{2,1,0:T(8,128)(2,1)S(1)} %get-tuple-element.33), channel_id=1, source_target_pairs={{0,8},{4,12},{8,0},{12,4},{1,9},{5,13},{9,1},{13,5},{2,10},{6,14},... | collective-permute-start | bytes 451592 | tf_op jit(solution)/shard_map/ppermute | solution.py:464
  11.5 11.2 %collective-permute-start.6 = (bf16[3,196,128]{2,1,0:T(8,128)(2,1)S(1)}, bf16[3,196,128]{2,1,0:T(8,128)(2,1)S(1)}, u32[]{:S(2)}, u32[]{:S(2)}) collective-permute-start(bf16[3,196,128]{2,1,0:T(8,128)(2,1)S(1)} %get-tuple-element.34), channel_id=1, source_target_pairs={{0,12},{4,8},{8,4},{12,0},{1,13},{5,9},{9,5},{13,1},{2,14},{6,10},... | collective-permute-start | bytes 451592 | tf_op jit(solution)/shard_map/ppermute | solution.py:464
  12.3 4.7 %collective-permute-start.3 = (bf16[384,128]{1,0:T(8,128)(2,1)S(1)}, bf16[384,128]{1,0:T(8,128)(2,1)S(1)}, u32[]{:S(2)}, u32[]{:S(2)}) collective-permute-start(bf16[384,128]{1,0:T(8,128)(2,1)S(1)} %get-tuple-element.45), channel_id=1, source_target_pairs={{0,2},{2,0},{1,3},{3,1},{4,6},{6,4},{5,7},{7,5},{8,10},{10,8},{9,1... | collective-permute-start | bytes 294920 | tf_op jit(solution)/shard_map/ppermute | solution.py:237
  22.7 3.5 %copy-start = (f32[8,32,128]{2,1,0:T(8,128)S(1)}, f32[8,32,128]{2,1,0:T(8,128)}, u32[]{:S(2)}) copy-start(f32[8,32,128]{2,1,0:T(8,128)} %est_ref.1) | copy-start | bytes 393220
  24.8 1.4 %collective-permute-start.7 = (f32[8,32,128]{2,1,0:T(8,128)S(1)}, f32[8,32,128]{2,1,0:T(8,128)S(1)}, u32[]{:S(2)}, u32[]{:S(2)}) collective-permute-start(f32[8,32,128]{2,1,0:T(8,128)S(1)} %spread.2.mine_ref), channel_id=1, source_target_pairs={{0,1},{1,0},{2,3},{3,2},{4,5},{5,4},{6,7},{7,6},{8,9},{9,8},{10,11... | collective-permute-start | bytes 393224 | tf_op jit(solution)/shard_map/ppermute | solution.py:472
  26.2 4.6 %collective-permute-start.8 = (bf16[8,8,128]{2,1,0:T(8,128)(2,1)S(1)}, bf16[8,8,128]{2,1,0:T(8,128)(2,1)S(1)}, u32[]{:S(2)}, u32[]{:S(2)}) collective-permute-start(bf16[8,8,128]{2,1,0:T(8,128)(2,1)S(1)} %get-tuple-element.37), channel_id=1, source_target_pairs={{0,4},{4,0},{8,12},{12,8},{1,5},{5,1},{9,13},{13,9},{2,6},{6,2},{1... | collective-permute-start | bytes 49160 | tf_op jit(solution)/shard_map/ppermute | solution.py:225
  28.4 5.5 %collective-permute-start.9 = (bf16[8,8,128]{2,1,0:T(8,128)(2,1)S(1)}, bf16[8,8,128]{2,1,0:T(8,128)(2,1)S(1)}, u32[]{:S(2)}, u32[]{:S(2)}) collective-permute-start(bf16[8,8,128]{2,1,0:T(8,128)(2,1)S(1)} %get-tuple-element.38), channel_id=1, source_target_pairs={{0,12},{4,8},{8,4},{12,0},{1,13},{5,9},{9,5},{13,1},{2,14},{6,10},... | collective-permute-start | bytes 49160 | tf_op jit(solution)/shard_map/ppermute | solution.py:225
  34.0 4.4 %collective-permute-start.10 = (bf16[6,48,128]{2,1,0:T(8,128)(2,1)S(1)}, bf16[6,48,128]{2,1,0:T(8,128)(2,1)S(1)}, u32[]{:S(2)}, u32[]{:S(2)}) collective-permute-start(bf16[6,48,128]{2,1,0:T(8,128)(2,1)S(1)} %edges.3), channel_id=1, source_target_pairs={{0,2},{2,0},{1,3},{3,1},{4,6},{6,4},{5,7},{7,5},{8,10},{10,8},{9,1... | collective-permute-start | bytes 221192 | tf_op jit(solution)/shard_map/ppermute | solution.py:241
  41.1 1.4 %collective-permute-start.11 = (f32[8,32,128]{2,1,0:T(8,128)S(1)}, f32[8,32,128]{2,1,0:T(8,128)S(1)}, u32[]{:S(2)}, u32[]{:S(2)}) collective-permute-start(f32[8,32,128]{2,1,0:T(8,128)S(1)} %spread.3.mine_ref), channel_id=1, source_target_pairs={{0,1},{1,0},{2,3},{3,2},{4,5},{5,4},{6,7},{7,6},{8,9},{9,8},{10,11... | collective-permute-start | bytes 393224 | tf_op jit(solution)/shard_map/ppermute | solution.py:472

commit v5 on v4

--- a/solution.py
+++ b/solution.py
@@ -222,7 +222,8 @@
         ra, rb = a[:nz].reshape(sa.shape), b[:nz].reshape(sb.shape)
         kern = jnp.concatenate([kern, a[nz:], b[nz:], c])
     else:
-        ra, rb = lax.ppermute(sa, "blk", pair), lax.ppermute(sb, "blk", odd)
+        inner = [(i, j) for i, j in odd if abs(i - j) == 1]
+        ra, rb = lax.ppermute(sa, "blk", pair), lax.ppermute(sb, "blk", inner)
     two = p.n_gz == 2
     edge = jax.ShapeDtypeStruct((p.halo, p.rows, p.nx), BF16)
     out = pl.pallas_call(
@@ -383,25 +384,35 @@
     u_row = lax.broadcasted_iota(jnp.int32, (16, nx), 0)
     lane8 = lax.broadcasted_iota(jnp.int32, (8, nx), 1)
 
-    def block(bl, carry):
-        wb = [[] for _ in range(taps)]
+    pitch = 16 * views
+    depth = pitch * taps
+
+    def block(bl):
+        wb = []
         at = [kernel_rows(p, ids_ref, bl, view) for view in range(views)]
         for e in range(taps):
-            base = kb_ref[e, at[-1], :]
+            base = jnp.where(lane8 < pitch, kb_ref[e, at[-1], :], 0.0)
             for view in range(views - 2, -1, -1):
                 base = jnp.where(lane8 < 16 * view + 16, kb_ref[e, at[view], :], base)
+            wide = [jnp.zeros((8, 128), F32)] * (-(-depth // 128))
             for a in range(taps):
-                wide = jnp.broadcast_to(base[a : a + 1], (8, 128))
-                wb[a].append(pltpu.roll(wide, 0, 1, stride=1, stride_axis=0))
-        wb = jnp.concatenate([x for y in wb for x in y], axis=0).astype(BF16)[:, : 16 * views]
-        m = 8 * taps
+                begin = pitch * (taps - 1 - a)
+                n, off = begin // 128, begin % 128
+                part = jnp.broadcast_to(base[a : a + 1], (8, 128))
+                part = pltpu.roll(part, off, 1, stride=1, stride_axis=0)
+                if off + pitch <= 128:
+                    wide[n] = wide[n] + part
+                else:
+                    wide[n] = wide[n] + jnp.where(lane8 >= off, part, 0.0)
+                    wide[n + 1] = wide[n + 1] + jnp.where(lane8 < off, part, 0.0)
+            wb.append(jnp.concatenate(wide, axis=1))
+        wb = jnp.concatenate(wb, axis=0).astype(BF16)[:, :depth]
         y_first = (b * p.blocks + bl) * p.by - reach
         y_ok = (u_row < p.ey) & (u_row + y_first >= 0) & (u_row + y_first < p.row_blocks * p.by)
         slots = [slot_ref[bl * views + view] for view in range(views)]
-        acc = {}
-        for pair in range(p.ez // 2):
-            s0 = pair * 2
-            for s in (s0, s0 + 1):
+        ready = 0
+        for z0 in range(0, p.cz, 2):
+            for s in range(ready, z0 + taps + 1):
                 z_ok = (s >= z_low) & (s < z_high)
                 for view in range(views):
                     tile = tiles_ref[jnp.maximum(slots[view], 0), s * p.ey : (s + 1) * p.ey, :].astype(F32)
@@ -409,28 +420,19 @@
                     ratio = tile / blur_ref[bl * views + view, s]
                     keep = y_ok & (z_ok & (slots[view] >= 0))
                     r_ref[bl, s, 16 * view : 16 * view + 16, :] = jnp.where(keep, ratio, 0.0).astype(BF16)
-            lo, hi = max(0, 2 * reach - s0 - 1) // 2 * 2, min(taps - 1, 2 * reach + p.cz - 1 - s0)
-            planes = jnp.concatenate([r_ref[bl, s0], r_ref[bl, s0 + 1]], axis=1)
-            got = jnp.dot(wb[m * lo : m * (hi + 1)], planes, preferred_element_type=F32)
+            ready = z0 + taps + 1
+            planes = [r_ref[bl, z : z + taps].reshape(depth, nx) for z in (z0, z0 + 1)]
+            got = jnp.dot(wb, jnp.concatenate(planes, axis=1), preferred_element_type=F32)
             for half in range(2):
-                s = s0 + half
-                for a in range(lo, hi + 1):
-                    z = s + a - 2 * reach
-                    if 0 <= z < p.cz:
-                        part = got[m * (a - lo) : m * (a - lo + 1), half * nx : (half + 1) * nx]
-                        acc[z] = part if z not in acc else acc[z] + part
-                z = s - 2 * reach
-                if 0 <= z < p.cz:
-                    done = acc.pop(z)
-                    term = done[8 * reach : 8 * reach + 8]
-                    for e in range(taps):
-                        if e != reach:
-                            term = term + lane_shift(done[8 * e : 8 * e + 8], e, reach, lane8)
-                    out_ref[z, bl * 8 : bl * 8 + 8, :] = term
-        return carry
+                done = got[:, half * nx : (half + 1) * nx]
+                term = done[8 * reach : 8 * reach + 8]
+                for e in range(taps):
+                    if e != reach:
+                        term = term + lane_shift(done[8 * e : 8 * e + 8], e, reach, lane8)
+                out_ref[z0 + half, bl * 8 : bl * 8 + 8, :] = term
 
     for bl in range(p.blocks):
-        block(bl, 0)
+        block(bl)
 
 
 def spread(p, slots, ids, blurred, table, arrived):

time: 43.4 us -> 39.8 us (0.917)
  the two profiles are of different devices: /device:TPU:0 before, /device:TPU:11 now
where the time goes in v5:
time: 39.8 us; the launch traced here: 39.7 us
  starting transfers between devices  15.3 us (38%)
  waiting for transfers between devices  12.2 us (31%)
  Pallas kernels  11.7 us (29%)
    ppermute x2, starting transfers between devices, on_device(): other = lax.ppermute(mine, 'view', [(0, 1), (1, 0)])  5.29 us
    ppermute x3, waiting for transfers between devices, on_device(): lax.ppermute(packed[k], 'blk', [(i, i ^ k) for i in range(p.n_blk)])  4.3 us
    pallas_call x2, Pallas kernels, blur(): pl.pallas_call(functools.partial(blur_kernel, p), out_shape=shapes, in_sp...  3.74 us
    ppermute x1, waiting for transfers between devices, halos(): lax.ppermute(jnp.concatenate([out[0].reshape(ne, p.nx), kern]), 'gz', swap)  3.49 us
    ppermute x2, starting transfers between devices, halos(): ra, rb = (lax.ppermute(sa, 'blk', pair), lax.ppermute(sb, 'blk', inner))  3.17 us
    pallas_call x2, Pallas kernels, spread(): pl.pallas_call(functools.partial(spread_kernel, p), out_shape=jax.ShapeDt...  3.14 us
    ppermute x3, starting transfers between devices, on_device(): lax.ppermute(packed[k], 'blk', [(i, i ^ k) for i in range(p.n_blk)])  2.65 us
    ppermute x2, waiting for transfers between devices, on_device(): other = lax.ppermute(mine, 'view', [(0, 1), (1, 0)])  1.97 us
  transfers between devices with their start and end apart: 12, of which 6 were waited for; matrix products, arithmetic and copies ran while one was open for 0% of the time, Pallas kernels for 15%

profile of v5, /device:TPU:11, one launch (start us, length us, event | category | flops | bytes accessed | tf_op | source)
XLA Modules:
  0.0 39.7 jit_solution(12329998287955112619)
XLA Ops:
  0.0 0.0 copy-start.2
  0.0 0.0 copy-start.1
  0.0 1.4 %first.1 = (bf16[8,32,128]{2,1,0:T(8,128)(2,1)S(1)}, bf16[8,8,128]{2,1,0:T(8,128)(2,1)S(1)}, bf16[8,8,128]{2,1,0:T(8,128)(2,1)S(1)}, bf16[24,128]{1,0:T(8,128)(2...) custom-call(s32[2,96]{1,0:T(2,128)} %bitcast.19, ...), custom_call_target="tpu_custom_call" | custom-call | tf_op jit(solution)/shard_map/first/pallas_call | solution.py:167
  1.4 1.3 %collective-permute-start.1 = (bf16[88,128]{1,0:T(8,128)(2,1)S(1)}, bf16[88,128]{1,0:T(8,128)(2,1)S(1)}, u32[]{:S(2)}, u32[]{:S(2)}) collective-permute-start(bf16[88,128]{1,0:T(8,128)(2,1)S(1)} %get-tuple-element.49), channel_id=1, source_target_pairs={{0,12},{4,8},{8,4},{12,0},{1,13},{5,9},{9,5},{13,1},{2,14},{6,10},... | collective-permute-start | bytes 67592 | tf_op jit(solution)/shard_map/ppermute | solution.py:220
  2.8 1.1 %collective-permute-start.2 = (bf16[24,128]{1,0:T(8,128)(2,1)S(1)}, bf16[24,128]{1,0:T(8,128)(2,1)S(1)}, u32[]{:S(2)}, u32[]{:S(2)}) collective-permute-start(bf16[24,128]{1,0:T(8,128)(2,1)S(1)} %get-tuple-element.26), channel_id=1, source_target_pairs={{0,8},{4,12},{8,0},{12,4},{1,9},{5,13},{9,1},{13,5},{2,10},{6,14},... | collective-permute-start | bytes 18440 | tf_op jit(solution)/shard_map/ppermute | solution.py:221
  3.9 1.1 %collective-permute-start = (bf16[88,128]{1,0:T(8,128)(2,1)S(1)}, bf16[88,128]{1,0:T(8,128)(2,1)S(1)}, u32[]{:S(2)}, u32[]{:S(2)}) collective-permute-start(bf16[88,128]{1,0:T(8,128)(2,1)S(1)} %get-tuple-element.50), channel_id=1, source_target_pairs={{0,4},{4,0},{8,12},{12,8},{1,5},{5,1},{9,13},{13,9},{2,6},{6,2},{1... | collective-permute-start | bytes 67592 | tf_op jit(solution)/shard_map/ppermute | solution.py:219
  5.0 0.4 collective-permute-start.4
  5.3 2.0 %collective-permute-start.5 = (bf16[3,196,128]{2,1,0:T(8,128)(2,1)S(1)}, bf16[3,196,128]{2,1,0:T(8,128)(2,1)S(1)}, u32[]{:S(2)}, u32[]{:S(2)}) collective-permute-start(bf16[3,196,128]{2,1,0:T(8,128)(2,1)S(1)} %get-tuple-element.33), channel_id=1, source_target_pairs={{0,8},{4,12},{8,0},{12,4},{1,9},{5,13},{9,1},{13,5},{2,10},{6,14},... | collective-permute-start | bytes 451592 | tf_op jit(solution)/shard_map/ppermute | solution.py:466
  7.4 0.0 collective-permute-done.1
  7.4 0.3 collective-permute-start.6
  7.6 0.0 collective-permute-done
  7.7 0.0 collective-permute-done.2
  7.8 0.3 collective-permute-start.3
  8.1 3.5 %collective-permute-done.3 = bf16[384,128]{1,0:T(8,128)(2,1)S(1)} collective-permute-done((bf16[384,128]{1,0:T(8,128)(2,1)S(1)}, bf16[384,128]{1,0:T(8,128)(2,1)S(1)}, u32[]{:S(2)}, u32[]{:S(2)}) %collective-permute-start.3) | collective-permute-done | bytes 98336 | tf_op jit(solution)/shard_map/ppermute | solution.py:238
  11.6 0.0 copy-done.1
  11.6 1.9 %blur.2 = (f32[12,14,16,128]{3,2,1,0:T(8,128)S(1)}, bf16[4,336,176]{2,1,0:T(8,128)(2,1)S(1)}, f32[7,192,128]{2,1,0:T(8,128)S(1)}) custom-call(s32[6,32]{1,0:T(8,128)S(1)} %bitcast.13, bf16[8,32,128]{2,1,0:T(8,128)(2,1)S(1)} %get-tuple-element.24.own_ref, bf16[8,8,128]{2,1,0:T(8,128)(2,1)S(1)} %slice_bitcast_fusion.1.ra_ref, ...), custom_call_target="tpu_custom_call" | custom-call | tf_op jit(solution)/shard_map/blur/pallas_call | solution.py:360
  13.5 0.0 copy-done.2
  13.5 1.4 %slots.1.slot_ref = s32[13]{0:T(128)S(1)} custom-call(s32[2,96]{1,0:T(2,128)S(1)} %bitcast.20, f32[7,192,128]{2,1,0:T(8,128)S(1)} %get-tuple-element.28.after_ref.kb_ref), custom_call_target="tpu_custom_call" | custom-call | tf_op jit(solution)/shard_map/slots/pallas_call | solution.py:130
  15.0 0.6 %beside.2.blur_ref = f32[12,14,16,128]{3,2,1,0:T(8,128)S(1)} custom-call(bf16[6,48,128]{2,1,0:T(8,128)(2,1)S(1)} %bitcast.10, bf16[6,48,128]{2,1,0:T(8,128)(2,1)S(1)} %bitcast.11, f32[12,14,16,128]{3,2,1,0:T(8,128)S(1)} %get-tuple-element.29.before_ref, bf16[4,336,176]{2,1,0:T(8,128)(2,1)S(1)} %get-tuple-element.30.wf_ref), custom_call_target="tpu_custom_call", output_to_operand_aliasing={{}: (2, {})} | custom-call | tf_op jit(solution)/shard_map/beside/pallas_call | solution.py:369
  15.6 0.0 collective-permute-done.4
  15.6 0.0 collective-permute-done.5
  15.7 4.3 %collective-permute-done.6 = bf16[3,196,128]{2,1,0:T(8,128)(2,1)S(1)} collective-permute-done((bf16[3,196,128]{2,1,0:T(8,128)(2,1)S(1)}, bf16[3,196,128]{2,1,0:T(8,128)(2,1)S(1)}, u32[]{:S(2)}, u32[]{:S(2)}) %collective-permute-start.6) | collective-permute-done | bytes 150560 | tf_op jit(solution)/shard_map/ppermute | solution.py:466
  20.0 0.0 copy-start
  20.0 1.6 %spread.2.mine_ref = f32[8,32,128]{2,1,0:T(8,128)S(1)} custom-call(s32[13]{0:T(128)S(1)} %slots.1.slot_ref, s32[6,32]{1,0:T(8,128)S(1)} %bitcast.14, f32[12,14,16,128]{3,2,1,0:T(8,128)S(1)} %beside.2.blur_ref, f32[7,192,128]{2,1,0:T(8,128)S(1)} %get-tuple-element.28.after_ref.kb_ref, bf16[12,196,128]{2,1,0:T(8,128)(2,1)S(1)} %constant_dynamic-update-slice_fusion.10.tiles_ref), custom_call_target="tpu_custom_call" | custom-call | tf_op jit(solution)/shard_map/spread/pallas_call | solution.py:440
  21.6 2.6 %collective-permute-start.7 = (f32[8,32,128]{2,1,0:T(8,128)S(1)}, f32[8,32,128]{2,1,0:T(8,128)S(1)}, u32[]{:S(2)}, u32[]{:S(2)}) collective-permute-start(f32[8,32,128]{2,1,0:T(8,128)S(1)} %spread.2.mine_ref), channel_id=1, source_target_pairs={{0,1},{1,0},{2,3},{3,2},{4,5},{5,4},{6,7},{7,6},{8,9},{9,8},{10,11... | collective-permute-start | bytes 393224 | tf_op jit(solution)/shard_map/ppermute | solution.py:474
  24.2 1.0 %collective-permute-done.7.other_ref = f32[8,32,128]{2,1,0:T(8,128)S(1)} collective-permute-done((f32[8,32,128]{2,1,0:T(8,128)S(1)}, f32[8,32,128]{2,1,0:T(8,128)S(1)}, u32[]{:S(2)}, u32[]{:S(2)}) %collective-permute-start.7) | collective-permute-done | bytes 131104 | tf_op jit(solution)/shard_map/ppermute | solution.py:474
  25.2 0.0 copy-done
  25.2 0.1 collective-permute-start.8
  25.3 3.1 %collective-permute-start.9 = (bf16[8,8,128]{2,1,0:T(8,128)(2,1)S(1)}, bf16[8,8,128]{2,1,0:T(8,128)(2,1)S(1)}, u32[]{:S(2)}, u32[]{:S(2)}) collective-permute-start(bf16[8,8,128]{2,1,0:T(8,128)(2,1)S(1)} %get-tuple-element.38), channel_id=1, source_target_pairs={{4,8},{8,4},{5,9},{9,5},{6,10},{10,6},{7,11},{11,7},{20,24},{24,20... | collective-permute-start | bytes 49160 | tf_op jit(solution)/shard_map/ppermute | solution.py:226
  28.4 0.0 collective-permute-done.8.ra_ref
  28.4 1.4 %collective-permute-done.9.rb_ref = bf16[8,8,128]{2,1,0:T(8,128)(2,1)S(1)} collective-permute-done((bf16[8,8,128]{2,1,0:T(8,128)(2,1)S(1)}, bf16[8,8,128]{2,1,0:T(8,128)(2,1)S(1)}, u32[]{:S(2)}, u32[]{:S(2)}) %collective-permute-start.9) | collective-permute-done | bytes 16416 | tf_op jit(solution)/shard_map/ppermute | solution.py:226
  29.8 0.3 collective-permute-start.10
  30.1 1.8 %blur.3 = (f32[12,14,16,128]{3,2,1,0:T(8,128)S(1)}, bf16[4,336,176]{2,1,0:T(8,128)(2,1)S(1)}) custom-call(s32[6,32]{1,0:T(8,128)S(1)} %bitcast.15, bf16[8,32,128]{2,1,0:T(8,128)(2,1)S(1)} %get-tuple-element.36.own_ref, bf16[8,8,128]{2,1,0:T(8,128)(2,1)S(1)} %collective-permute-done.8.ra_ref, bf16[8,8,128]{2,1,0:T(8,128)(2,1)S(1)} %collective-permute-done.9.rb_ref, ...), custom_call_target="tpu_custom_call" | custom-call | tf_op jit(solution)/shard_map/blur/pallas_call | solution.py:360
  31.9 1.1 %collective-permute-done.10.below_ref.above_ref = bf16[6,48,128]{2,1,0:T(8,128)(2,1)S(1)} collective-permute-done((bf16[6,48,128]{2,1,0:T(8,128)(2,1)S(1)}, bf16[6,48,128]{2,1,0:T(8,128)(2,1)S(1)}, u32[]{:S(2)}, u32[]{:S(2)}) %collective-permute-start.10) | collective-permute-done | bytes 73760 | tf_op jit(solution)/shard_map/ppermute | solution.py:242
  33.0 0.6 %beside.3.blur_ref = f32[12,14,16,128]{3,2,1,0:T(8,128)S(1)} custom-call(bf16[6,48,128]{2,1,0:T(8,128)(2,1)S(1)} %collective-permute-done.10.below_ref.above_ref, bf16[6,48,128]{2,1,0:T(8,128)(2,1)S(1)} %collective-permute-done.10.below_ref.above_ref, f32[12,14,16,128]{3,2,1,0:T(8,128)S(1)} %get-tuple-element.39.before_ref, ...), custom_call_target="tpu_custom_call", output_to_operand_aliasing={{}: (2, {})} | custom-call | tf_op jit(solution)/shard_map/beside/pallas_call | solution.py:369
  33.7 1.6 %spread.3.mine_ref = f32[8,32,128]{2,1,0:T(8,128)S(1)} custom-call(s32[13]{0:T(128)S(1)} %slots.1.slot_ref, s32[6,32]{1,0:T(8,128)S(1)} %bitcast.16, f32[12,14,16,128]{3,2,1,0:T(8,128)S(1)} %beside.3.blur_ref, f32[7,192,128]{2,1,0:T(8,128)S(1)} %get-tuple-element.28.after_ref.kb_ref, bf16[12,196,128]{2,1,0:T(8,128)(2,1)S(1)} %constant_dynamic-update-slice_fusion.10.tiles_ref), custom_call_target="tpu_custom_call" | custom-call | tf_op jit(solution)/shard_map/spread/pallas_call | solution.py:440
  35.3 2.7 %collective-permute-start.11 = (f32[8,32,128]{2,1,0:T(8,128)S(1)}, f32[8,32,128]{2,1,0:T(8,128)S(1)}, u32[]{:S(2)}, u32[]{:S(2)}) collective-permute-start(f32[8,32,128]{2,1,0:T(8,128)S(1)} %spread.3.mine_ref), channel_id=1, source_target_pairs={{0,1},{1,0},{2,3},{3,2},{4,5},{5,4},{6,7},{7,6},{8,9},{9,8},{10,11... | collective-permute-start | bytes 393224 | tf_op jit(solution)/shard_map/ppermute | solution.py:474
  38.0 1.0 %collective-permute-done.11.other_ref = f32[8,32,128]{2,1,0:T(8,128)S(1)} collective-permute-done((f32[8,32,128]{2,1,0:T(8,128)S(1)}, f32[8,32,128]{2,1,0:T(8,128)S(1)}, u32[]{:S(2)}, u32[]{:S(2)}) %collective-permute-start.11) | collective-permute-done | bytes 131104 | tf_op jit(solution)/shard_map/ppermute | solution.py:474
  39.0 0.7 %update.3 = f32[8,32,128]{2,1,0:T(8,128)} custom-call(f32[32,128]{1,0:T(8,128)S(1)} %get-tuple-element.23.count_ref, f32[8,32,128]{2,1,0:T(8,128)S(1)} %get-tuple-element.35.est_ref, f32[8,32,128]{2,1,0:T(8,128)S(1)} %spread.3.mine_ref, f32[8,32,128]{2,1,0:T(8,128)S(1)} %collective-permute-done.11.other_ref), custom_call_target="tpu_custom_call" | custom-call | tf_op jit(solution)/shard_map/update/pallas_call | solution.py:181
  (17 shorter events, 0.2 us)
Async XLA Ops:
  0.0 13.5 %copy-start.2 = (s32[96,2]{0,1:T(2,128)S(1)}, s32[96,2]{0,1:T(2,128)}, u32[]{:S(2)}) copy-start(s32[96,2]{0,1:T(2,128)} %param.7) | copy-start | bytes 2308
  0.0 11.6 %copy-start.1 = (s32[32,6]{0,1:T(8,128)S(1)}, s32[32,6]{0,1:T(8,128)}, u32[]{:S(2)}) copy-start(s32[32,6]{0,1:T(8,128)} %param.9) | copy-start | bytes 2308
  1.4 5.9 %collective-permute-start.1 = (bf16[88,128]{1,0:T(8,128)(2,1)S(1)}, bf16[88,128]{1,0:T(8,128)(2,1)S(1)}, u32[]{:S(2)}, u32[]{:S(2)}) collective-permute-start(bf16[88,128]{1,0:T(8,128)(2,1)S(1)} %get-tuple-element.49), channel_id=1, source_target_pairs={{0,12},{4,8},{8,4},{12,0},{1,13},{5,9},{9,5},{13,1},{2,14},{6,10},... | collective-permute-start | bytes 67592 | tf_op jit(solution)/shard_map/ppermute | solution.py:220
  2.8 5.0 %collective-permute-start.2 = (bf16[24,128]{1,0:T(8,128)(2,1)S(1)}, bf16[24,128]{1,0:T(8,128)(2,1)S(1)}, u32[]{:S(2)}, u32[]{:S(2)}) collective-permute-start(bf16[24,128]{1,0:T(8,128)(2,1)S(1)} %get-tuple-element.26), channel_id=1, source_target_pairs={{0,8},{4,12},{8,0},{12,4},{1,9},{5,13},{9,1},{13,5},{2,10},{6,14},... | collective-permute-start | bytes 18440 | tf_op jit(solution)/shard_map/ppermute | solution.py:221
  3.9 3.8 %collective-permute-start = (bf16[88,128]{1,0:T(8,128)(2,1)S(1)}, bf16[88,128]{1,0:T(8,128)(2,1)S(1)}, u32[]{:S(2)}, u32[]{:S(2)}) collective-permute-start(bf16[88,128]{1,0:T(8,128)(2,1)S(1)} %get-tuple-element.50), channel_id=1, source_target_pairs={{0,4},{4,0},{8,12},{12,8},{1,5},{5,1},{9,13},{13,9},{2,6},{6,2},{1... | collective-permute-start | bytes 67592 | tf_op jit(solution)/shard_map/ppermute | solution.py:219
  5.0 10.6 %collective-permute-start.4 = (bf16[3,196,128]{2,1,0:T(8,128)(2,1)S(1)}, bf16[3,196,128]{2,1,0:T(8,128)(2,1)S(1)}, u32[]{:S(2)}, u32[]{:S(2)}) collective-permute-start(bf16[3,196,128]{2,1,0:T(8,128)(2,1)S(1)} %get-tuple-element.32), channel_id=1, source_target_pairs={{0,4},{4,0},{8,12},{12,8},{1,5},{5,1},{9,13},{13,9},{2,6},{6,2},{1... | collective-permute-start | bytes 451592 | tf_op jit(solution)/shard_map/ppermute | solution.py:466
  5.3 10.3 %collective-permute-start.5 = (bf16[3,196,128]{2,1,0:T(8,128)(2,1)S(1)}, bf16[3,196,128]{2,1,0:T(8,128)(2,1)S(1)}, u32[]{:S(2)}, u32[]{:S(2)}) collective-permute-start(bf16[3,196,128]{2,1,0:T(8,128)(2,1)S(1)} %get-tuple-element.33), channel_id=1, source_target_pairs={{0,8},{4,12},{8,0},{12,4},{1,9},{5,13},{9,1},{13,5},{2,10},{6,14},... | collective-permute-start | bytes 451592 | tf_op jit(solution)/shard_map/ppermute | solution.py:466
  7.4 12.6 %collective-permute-start.6 = (bf16[3,196,128]{2,1,0:T(8,128)(2,1)S(1)}, bf16[3,196,128]{2,1,0:T(8,128)(2,1)S(1)}, u32[]{:S(2)}, u32[]{:S(2)}) collective-permute-start(bf16[3,196,128]{2,1,0:T(8,128)(2,1)S(1)} %get-tuple-element.34), channel_id=1, source_target_pairs={{0,12},{4,8},{8,4},{12,0},{1,13},{5,9},{9,5},{13,1},{2,14},{6,10},... | collective-permute-start | bytes 451592 | tf_op jit(solution)/shard_map/ppermute | solution.py:466
  7.8 3.8 %collective-permute-start.3 = (bf16[384,128]{1,0:T(8,128)(2,1)S(1)}, bf16[384,128]{1,0:T(8,128)(2,1)S(1)}, u32[]{:S(2)}, u32[]{:S(2)}) collective-permute-start(bf16[384,128]{1,0:T(8,128)(2,1)S(1)} %get-tuple-element.45), channel_id=1, source_target_pairs={{0,2},{2,0},{1,3},{3,1},{4,6},{6,4},{5,7},{7,5},{8,10},{10,8},{9,1... | collective-permute-start | bytes 294920 | tf_op jit(solution)/shard_map/ppermute | solution.py:238
  20.0 5.2 %copy-start = (f32[8,32,128]{2,1,0:T(8,128)S(1)}, f32[8,32,128]{2,1,0:T(8,128)}, u32[]{:S(2)}) copy-start(f32[8,32,128]{2,1,0:T(8,128)} %est_ref.1) | copy-start | bytes 393220
  21.6 3.6 %collective-permute-start.7 = (f32[8,32,128]{2,1,0:T(8,128)S(1)}, f32[8,32,128]{2,1,0:T(8,128)S(1)}, u32[]{:S(2)}, u32[]{:S(2)}) collective-permute-start(f32[8,32,128]{2,1,0:T(8,128)S(1)} %spread.2.mine_ref), channel_id=1, source_target_pairs={{0,1},{1,0},{2,3},{3,2},{4,5},{5,4},{6,7},{7,6},{8,9},{9,8},{10,11... | collective-permute-start | bytes 393224 | tf_op jit(solution)/shard_map/ppermute | solution.py:474
  25.2 3.2 %collective-permute-start.8 = (bf16[8,8,128]{2,1,0:T(8,128)(2,1)S(1)}, bf16[8,8,128]{2,1,0:T(8,128)(2,1)S(1)}, u32[]{:S(2)}, u32[]{:S(2)}) collective-permute-start(bf16[8,8,128]{2,1,0:T(8,128)(2,1)S(1)} %get-tuple-element.37), channel_id=1, source_target_pairs={{0,4},{4,0},{8,12},{12,8},{1,5},{5,1},{9,13},{13,9},{2,6},{6,2},{1... | collective-permute-start | bytes 49160 | tf_op jit(solution)/shard_map/ppermute | solution.py:226
  25.3 4.5 %collective-permute-start.9 = (bf16[8,8,128]{2,1,0:T(8,128)(2,1)S(1)}, bf16[8,8,128]{2,1,0:T(8,128)(2,1)S(1)}, u32[]{:S(2)}, u32[]{:S(2)}) collective-permute-start(bf16[8,8,128]{2,1,0:T(8,128)(2,1)S(1)} %get-tuple-element.38), channel_id=1, source_target_pairs={{4,8},{8,4},{5,9},{9,5},{6,10},{10,6},{7,11},{11,7},{20,24},{24,20... | collective-permute-start | bytes 49160 | tf_op jit(solution)/shard_map/ppermute | solution.py:226
  29.8 3.3 %collective-permute-start.10 = (bf16[6,48,128]{2,1,0:T(8,128)(2,1)S(1)}, bf16[6,48,128]{2,1,0:T(8,128)(2,1)S(1)}, u32[]{:S(2)}, u32[]{:S(2)}) collective-permute-start(bf16[6,48,128]{2,1,0:T(8,128)(2,1)S(1)} %edges.3), channel_id=1, source_target_pairs={{0,2},{2,0},{1,3},{3,1},{4,6},{6,4},{5,7},{7,5},{8,10},{10,8},{9,1... | collective-permute-start | bytes 221192 | tf_op jit(solution)/shard_map/ppermute | solution.py:242
  35.3 3.7 %collective-permute-start.11 = (f32[8,32,128]{2,1,0:T(8,128)S(1)}, f32[8,32,128]{2,1,0:T(8,128)S(1)}, u32[]{:S(2)}, u32[]{:S(2)}) collective-permute-start(f32[8,32,128]{2,1,0:T(8,128)S(1)} %spread.3.mine_ref), channel_id=1, source_target_pairs={{0,1},{1,0},{2,3},{3,2},{4,5},{5,4},{6,7},{7,6},{8,9},{9,8},{10,11... | collective-permute-start | bytes 393224 | tf_op jit(solution)/shard_map/ppermute | solution.py:474
